TPU v7x, 32 devices: a whole 2x2x4 slice. The times are simulated.
32 devices in a mesh: dp: 8 (over y, x, core), fsdp: 4 (over z).
Axes of the slice: x: 2, y: 2, z: 4, core: 2. Of those that a mesh axis runs over, the one named last changes fastest.
Arguments:
- tokens: bfloat16 [32768, 768], P(('dp', 'fsdp')), may hold values from -8 to 8
- chip_ids: int32 [32768], P(('dp', 'fsdp')), may hold values from 0 to 511, as said below
- ln1_gain: bfloat16 [768], P('fsdp'), may hold values from 0.5 to 1.5
- ln1_bias: bfloat16 [768], P('fsdp'), may hold values from -1.5 to 1.5
- w_qkv: bfloat16 [768, 2304], P('fsdp'), may hold values from -0.3125 to 0.3125
- w_out: bfloat16 [768, 768], P('fsdp'), may hold values from -0.625 to 0.625
- b_out: bfloat16 [768], P('fsdp'), may hold values from -1.5 to 1.5
- ln2_gain: bfloat16 [768], P('fsdp'), may hold values from 0.5 to 1.5
- ln2_bias: bfloat16 [768], P('fsdp'), may hold values from -1.5 to 1.5
- w_fc1: bfloat16 [768, 3072], P('fsdp'), may hold values from -0.21875 to 0.21875
- b_fc1: bfloat16 [3072], P('fsdp'), may hold values from -2.5 to 2.5
- w_fc2: bfloat16 [3072, 768], P('fsdp'), may hold values from -0.15625 to 0.15625
- b_fc2: bfloat16 [768], P('fsdp'), may hold values from -1.5 to 1.5
- cotangent: bfloat16 [32768, 768], P(('dp', 'fsdp')), may hold values from -6 to 6
Outputs:
- layer_out: bfloat16 [32768, 768], P(('dp', 'fsdp'))
- grad_tokens: float32 [32768, 768], P(('dp', 'fsdp'))
- grad_ln1_gain: float32 [768], P('fsdp')
- grad_ln1_bias: float32 [768], P('fsdp')
- grad_w_qkv: float32 [768, 2304], P('fsdp')
- grad_w_out: float32 [768, 768], P('fsdp')
- grad_b_out: float32 [768], P('fsdp')
- grad_ln2_gain: float32 [768], P('fsdp')
- grad_ln2_bias: float32 [768], P('fsdp')
- grad_w_fc1: float32 [768, 3072], P('fsdp')
- grad_b_fc1: float32 [3072], P('fsdp')
- grad_w_fc2: float32 [3072, 768], P('fsdp')
- grad_b_fc2: float32 [768], P('fsdp')
Inputs may be any that keep to these rules, and one draw needn't show every extreme that they name: `chip_ids`: chip numbers never fall along the tokens. Each chip holds exactly 64 or 256 tokens and lies inside one device's block of 1024 rows; every such block holds at least one chip of 256 tokens and may hold only such chips. The chips of the d-th block of rows carry numbers from d * 16 to (d + 1) * 16 - 1, the first and the last of them always used.
All inputs are finite; a program needn't handle non-finite values.
Results may differ from a plain program's by a relative error of at most 0.015.
Values may be sent and summed in bfloat16 or wider, within the bound.
No kernel may reach another device: no remote copies, remote signals or barrier semaphores. Data moves between devices by JAX's collectives and lax.ppermute only.
A program may use at most 320 MiB of HBM per device.

v0:
```python
import functools
import math

import jax
import jax.numpy as jnp
from jax import lax
from jax.experimental import pallas as pl
from jax.experimental.pallas import tpu as pltpu
from jax.sharding import PartitionSpec as P

HEADS = 12
HEAD = 64
UNIT = 64
BLOCK = 256
PER = BLOCK // UNIT
EPS = 1e-05
NEG = -1e30
RSQRT2 = 1.0 / math.sqrt(2.0)
RSQRT_TAU = 1.0 / math.sqrt(2.0 * math.pi)
SCALE = 1.0 / math.sqrt(HEAD)
EXT = 256
VMEM_LIMIT = 64 * 1024 * 1024 - 65536
ALL = ("dp", "fsdp")
F32 = jnp.float32
BF16 = jnp.bfloat16

I_LONG, I_C, I_X, I_Y, I_Z, I_B1, I_B2 = 16, 17, 18, 19, 20, 21, 22


def nn(a, b):
    return lax.dot_general(a, b, (((1,), (0,)), ((), ())), preferred_element_type=F32)


def nt(a, b):
    return lax.dot_general(a, b, (((1,), (1,)), ((), ())), preferred_element_type=F32)


def tn(a, b):
    return lax.dot_general(a, b, (((0,), (0,)), ((), ())), preferred_element_type=F32)


SHORT = pl.CostEstimate(flops=1, bytes_accessed=1, transcendentals=0)


def params(**kw):
    return pltpu.CompilerParams(vmem_limit_bytes=VMEM_LIMIT, **kw)


ANY = pl.BlockSpec(memory_space=pl.ANY)
WHOLE = pl.BlockSpec(memory_space=pltpu.VMEM)


def tie(a, *after):
    return lax.optimization_barrier((a,) + after)[0]


class Routes:
    def __init__(self, n_dp, n_z):
        self.n_dp, self.n_z = n_dp, n_z

    def table(self, move):
        pairs = []
        for d in range(self.n_dp):
            for z in range(self.n_z):
                e, w = move(d, z)
                pairs.append((d * self.n_z + z, e * self.n_z + w % self.n_z))
        return pairs

    def core(self, a):
        return lax.ppermute(a, ALL, self.table(lambda d, z: (d ^ 1, z)))

    def first(self, a):
        return lax.ppermute(a, ALL, self.table(lambda d, z: (d ^ (2 if d % 2 == 0 else 4), z)))

    def second(self, a):
        return lax.ppermute(a, ALL, self.table(lambda d, z: (d ^ (4 if d % 2 == 0 else 2), z)))

    def z_near(self, a):
        return lax.ppermute(a, ALL, self.table(lambda d, z: (d, z + (1 if d % 2 == 0 else self.n_z - 1))))

    def z_far(self, a):
        return lax.ppermute(a, ALL, self.table(lambda d, z: (d, z + 2)))

    def z_flip(self, a, bit):
        return lax.ppermute(a, ALL, self.table(lambda d, z: (d, z ^ bit)))

    def diagonal(self, a):
        return lax.ppermute(a, ALL, self.table(lambda d, z: (d ^ 6, z)))


def spread(routes, block):
    own = around(routes, block)
    return own + [routes.core(b) for b in own]


def around(routes, block):
    return [block, routes.first(block), routes.second(block), routes.diagonal(block)]


def holder(meta, t):
    flip = t // 4
    cc = meta[I_C] if flip == 0 else 1 - meta[I_C]
    x, y = meta[I_X], meta[I_Y]
    t = t % 4
    if t == 1:
        x, y = x ^ (1 - cc), y ^ cc
    elif t == 2:
        x, y = x ^ cc, y ^ (1 - cc)
    elif t == 3:
        x, y = x ^ 1, y ^ 1
    return cc, x, y


def gather_mixed(routes, near, far, early, late):
    block = jnp.concatenate([routes.z_near(near), routes.z_far(far)], axis=1)
    block = tie(block, early)
    one = routes.first(block)
    two = routes.second(block)
    own = [block, one, two, routes.second(tie(one, *late))]
    return own + [routes.core(b) for b in own]


def mixed_copies(meta, shard, blocks, w, sems):
    rows, wide = shard.shape
    quarter, part = rows // 4, wide // 2
    z = meta[I_Z]
    out = [(shard, w.at[pl.ds(pl.multiple_of(z * rows, 16), rows)])]
    for t, block in enumerate(blocks):
        cc, x, y = holder(meta, t)
        q = 2 * y + x
        plane = lax.rem(z + jnp.where(cc == 0, 3, 1), 4)
        far = lax.rem(z + 2, 4)
        out.append((block.at[:, pl.ds(0, wide)],
                    w.at[pl.ds(pl.multiple_of(plane * rows + q * quarter, 16), quarter)]))
        out.append((block.at[:, pl.ds(wide, part)],
                    w.at[pl.ds(pl.multiple_of(far * rows + q * quarter, 16), quarter),
                         pl.ds(pl.multiple_of(cc * part, 128), part)]))
    return [pltpu.make_async_copy(s, d, sems.at[i]) for i, (s, d) in enumerate(out)]


PARTS = ((1, 0), (2, 1))


def piece_rows(ng, rows, d):
    return 4 * ng * (rows // 4) + ng * (d // 128) * 32


def pack_body(pos, *refs):
    w_qkv, w_out = refs[0:2]
    vecs, b1, f1, f2 = refs[2:8], refs[8], refs[9], refs[10]
    mixed, near, far = refs[11:14]
    outs, sems = refs[14:16], refs[16]
    c, x, y = pos[0] & 1, (pos[0] >> 1) & 1, (pos[0] >> 2) & 1
    p = 2 * y + x
    d = w_out.shape[1]
    rows = w_out.shape[0]
    quarter = rows // 4
    ff = f1.shape[1]
    copies = []
    for out, (ng, go) in zip(outs, PARTS):
        for zz in range(4):
            for g in range(ng):
                col = pl.multiple_of(zz * (ff // 4) + c * (ff // 8) + (go + g) * 128, 128)
                copies.append((f1.at[pl.ds(pl.multiple_of(p * quarter, 16), quarter), pl.ds(col, 128)],
                               out.at[pl.ds((zz * ng + g) * quarter, quarter)]))
        base = 4 * ng * quarter
        for g in range(ng):
            row = pl.multiple_of(c * (ff // 8) + (go + g) * 128 + p * 32, 32)
            for k in range(d // 128):
                copies.append((f2.at[pl.ds(row, 32), pl.ds(k * 128, 128)],
                               out.at[pl.ds(base + (g * (d // 128) + k) * 32, 32)]))
    copies = [pltpu.make_async_copy(s, t, sems.at[i]) for i, (s, t) in enumerate(copies)]
    for cp in copies:
        cp.start()
    mixed[:, 0 : 3 * d] = w_qkv[...]
    mixed[:, 3 * d : 4 * d] = w_out[...]
    lines = [v[...].astype(F32).reshape(1, rows) for v in vecs] + [jnp.zeros((128 - len(vecs), rows), F32)]
    mixed[:, 4 * d : 4 * d + 128] = jnp.concatenate(lines, axis=0).T.astype(BF16)
    n = b1.shape[0] // 128
    lines = [b1[pl.ds(128 * i, 128)].astype(F32).reshape(1, 128) for i in range(n)] + [jnp.zeros((rows - n, 128), F32)]
    mixed[:, 4 * d + 128 :] = jnp.concatenate(lines, axis=0).astype(BF16)
    own = pl.ds(pl.multiple_of(p * quarter, 16), quarter)
    near[...] = mixed[own, :]
    part = mixed.shape[1] // 2
    far[...] = mixed[own, pl.ds(pl.multiple_of(c * part, 128), part)]
    for cp in copies:
        cp.wait()


def pack(pos, w_qkv, w_out, vecs, b1, f1, f2):
    rows, d = w_out.shape
    wide = 4 * d + EXT
    sd = jax.ShapeDtypeStruct
    count = sum(4 * ng + ng * (d // 128) for ng, _ in PARTS)
    return pl.pallas_call(
        pack_body,
        in_specs=[pl.BlockSpec(memory_space=pltpu.SMEM)] + [WHOLE] * 9 + [ANY] * 2,
        out_specs=[WHOLE] * 5,
        scratch_shapes=[pltpu.SemaphoreType.DMA((count,))],
        out_shape=[sd((rows, wide), BF16), sd((rows // 4, wide), BF16), sd((rows // 4, wide // 2), BF16)]
        + [sd((piece_rows(ng, rows, d), 128), BF16) for ng, _ in PARTS],
        compiler_params=params(),
        name="pack",
    )(pos, w_qkv, w_out, *vecs, b1, f1, f2)


def norm_stats(rows):
    centred = rows - jnp.mean(rows, axis=-1, keepdims=True)
    inverse = lax.rsqrt(jnp.mean(centred * centred, axis=-1, keepdims=True) + EPS)
    return centred * inverse, inverse


def norm_back(grad, normed, inverse, gain):
    e = grad * gain
    return inverse * (
        e - jnp.mean(e, axis=-1, keepdims=True) - normed * jnp.mean(e * normed, axis=-1, keepdims=True)
    )


def lane_masks():
    lane = lax.broadcasted_iota(jnp.int32, (1, 2 * HEAD), 1)
    low = jnp.where(lane < HEAD, 1.0, 0.0).astype(BF16)
    return low, (1.0 - low.astype(F32)).astype(BF16)


def k1_body(meta, *refs):
    tok, cot = refs[0:4], refs[4:8]
    shard, blocks = refs[8], refs[9:17]
    qkv_o, prob_o, inv_o, o_o, x1_o, a2_o, a1_o, gp_o, w_o, vec_o, b1_o, dbf_o = refs[17:29]
    w, vec, sems, out_sem = refs[29:]
    b = pl.program_id(0)
    d = w.shape[0]

    @pl.when(b == 0)
    def _():
        copies = mixed_copies(meta, shard, blocks, w, sems)
        for cp in copies:
            cp.start()
        for cp in copies:
            cp.wait()
        pltpu.make_async_copy(w, w_o, out_sem).start()
        ext = w[:, 4 * d : 4 * d + 128].astype(F32).T
        vec[...] = ext[0:16]
        vec_o[...] = ext[0:16]
        dbf_o[...] = jnp.zeros_like(dbf_o)
        rows = d // 4
        for zz in range(4):
            for r in range(b1_o.shape[1] // 128):
                b1_o[zz : zz + 1, 128 * r : 128 * (r + 1)] = w[
                    zz * rows : zz * rows + 8, 4 * d + 128 : 4 * d + 256
                ].astype(F32)[r : r + 1]

    g1, s1, b_out = vec[0:1], vec[1:2], vec[2:3]
    g2, s2 = vec[3:4], vec[4:5]
    x = jnp.concatenate([r[...] for r in tok], axis=0).astype(F32)
    g = jnp.concatenate([r[...] for r in cot], axis=0)
    gp_o[...] = g
    dbf_o[0:1] += jnp.sum(g.astype(F32), axis=0, keepdims=True)
    n1, _ = norm_stats(x)
    a1 = (n1 * g1 + s1).astype(BF16)
    a1_o[...] = a1
    for k in range(3):
        qkv_o[:, k * d : (k + 1) * d] = nn(a1, w[:, k * d : (k + 1) * d]).astype(BF16)
    row = lax.broadcasted_iota(jnp.int32, (BLOCK, BLOCK), 0) // UNIT
    col = lax.broadcasted_iota(jnp.int32, (BLOCK, BLOCK), 1) // UNIT
    keep = (row == col) | (b < meta[I_LONG])
    low, high = lane_masks()
    left = lax.broadcasted_iota(jnp.int32, (BLOCK, 2 * HEAD), 1) < HEAD
    for j in range(HEADS // 2):
        s = slice(128 * j, 128 * (j + 1))
        q = qkv_o[:, s]
        k = qkv_o[:, d + 128 * j : d + 128 * (j + 1)]
        v = qkv_o[:, 2 * d + 128 * j : 2 * d + 128 * (j + 1)]
        mixed, inv = None, []
        for h, m in ((0, low), (1, high)):
            sc = jnp.where(keep, nt(q * (m * SCALE), k), NEG)
            e = jnp.exp(sc - jnp.max(sc, axis=-1, keepdims=True))
            inv.append(1.0 / jnp.sum(e, axis=-1, keepdims=True))
            e = e.astype(BF16)
            prob_o[0, 2 * j + h] = e
            part = nn(e, v * m)
            mixed = part if mixed is None else mixed + part
        inv = jnp.where(left, inv[0], inv[1])
        inv_o[:, s] = inv
        o_o[:, s] = (mixed * inv).astype(BF16)
    x1 = x + (nn(o_o[...], w[:, 3 * d : 4 * d]) + b_out)
    x1_o[...] = x1
    n2, _ = norm_stats(x1)
    a2_o[...] = (n2 * g2 + s2).astype(BF16)

    @pl.when(b == pl.num_programs(0) - 1)
    def _():
        pltpu.make_async_copy(w, w_o, out_sem).wait()


def unit_spec(i, d):
    return pl.BlockSpec((UNIT, d), lambda b, meta: (meta[PER * b + i], 0))


def k1(meta, tokens, cot, shard, blocks, ff):
    t, d = tokens.shape
    nb = t // BLOCK
    wide = shard.shape[1]
    blk = lambda n: pl.BlockSpec((BLOCK, n), lambda b, meta: (b, 0))
    fixed = lambda s: pl.BlockSpec(s, lambda b, meta: (0,) * len(s))
    sd = jax.ShapeDtypeStruct
    return pl.pallas_call(
        k1_body,
        grid_spec=pltpu.PrefetchScalarGridSpec(
            num_scalar_prefetch=1,
            grid=(nb,),
            in_specs=[unit_spec(i, d) for i in range(PER)] * 2 + [ANY] * 9,
            out_specs=[
                blk(3 * d),
                pl.BlockSpec((1, HEADS, BLOCK, BLOCK), lambda b, meta: (b, 0, 0, 0)),
                blk(d), blk(d), blk(d), blk(d), blk(d), blk(d), ANY,
                fixed((16, d)), fixed((4, ff // 4)), fixed((8, d)),
            ],
            scratch_shapes=[
                pltpu.VMEM((d, wide), BF16),
                pltpu.VMEM((16, d), F32),
                pltpu.SemaphoreType.DMA((17,)),
                pltpu.SemaphoreType.DMA,
            ],
        ),
        out_shape=[
            sd((t, 3 * d), BF16), sd((nb, HEADS, BLOCK, BLOCK), BF16), sd((t, d), F32), sd((t, d), BF16), sd((t, d), F32),
            sd((t, d), BF16), sd((t, d), BF16), sd((t, d), BF16), sd((d, wide), BF16),
            sd((16, d), F32), sd((4, ff // 4), F32), sd((8, d), F32),
        ],
        compiler_params=params(),
        cost_estimate=pl.CostEstimate(flops=2 * t * d * 5 * d, bytes_accessed=40 << 20, transcendentals=t * BLOCK * HEADS),
        name="norm_qkv_attend",
    )(meta, *([tokens] * PER), *([cot] * PER), shard, *blocks)


def gelu_and_slope(z):
    t = 1.0 / (1.0 + (0.3275911 * RSQRT2) * jnp.abs(z))
    e = jnp.exp(-0.5 * z * z)
    poly = t * (0.5 * 0.254829592 + t * (-0.5 * 0.284496736 + t * (0.5 * 1.421413741 + t * (
        -0.5 * 1.453152027 + t * (0.5 * 1.061405429)))))
    tail = poly * e
    cdf = jnp.where(z >= 0.0, 1.0 - tail, tail)
    return z * cdf, cdf + z * e * RSQRT_TAU


def mlp_body(ng, go, first, meta, *refs):
    a2o, a2p, g_o, g_p, b1, f1, f2 = refs[0:7]
    blocks = refs[7:11]
    at = 11
    prev = None
    if not first:
        prev, at = refs[11:15], 15
    yo, do, yp, dp, send, keep, db = refs[at : at + 7]
    a2, g, u_s, dz_s, w1, w2, dw1, dw2, sems = refs[at + 7 :]
    b = pl.program_id(0)
    last = pl.num_programs(0) - 1
    t, d = a2o.shape
    nb = t // BLOCK
    n = 128 * ng
    c, x, y, z = meta[I_C], meta[I_X], meta[I_Y], meta[I_Z]
    rows = f1.shape[0]
    quarter = rows // 4
    nk = d // 128

    def loads():
        ff = f1.shape[1]
        early = [(a2o, a2.at[pl.ds(0, t)]), (g_o, g.at[pl.ds(0, t)])]
        for zz in range(4):
            col = pl.multiple_of(zz * (ff // 4) + c * (ff // 8) + go * 128, 128)
            early.append((f1.at[:, pl.ds(col, n)], w1.at[pl.ds(pl.multiple_of(z * rows, 16), rows), pl.ds(zz * n, n)]))
        row = pl.multiple_of(c * (ff // 8) + go * 128, 128)
        early.append((f2.at[pl.ds(row, n)], w2.at[pl.ds(pl.multiple_of(z * n, 128), n)]))
        late = [(a2p, a2.at[pl.ds(t, t)]), (g_p, g.at[pl.ds(t, t)])]
        cps = [pltpu.make_async_copy(s, q, sems.at[i]) for i, (s, q) in enumerate(early + late)]
        return cps[: len(early)], cps[len(early) :]

    @pl.when(b == 0)
    def _():
        early, late = loads()
        for cp in early + late:
            cp.start()
        db[...] = jnp.zeros_like(db)
        for k, blk in enumerate(blocks):
            xx, yy = x, y
            if k == 1:
                xx, yy = x ^ (1 - c), y ^ c
            elif k == 2:
                xx, yy = x ^ c, y ^ (1 - c)
            elif k == 3:
                xx, yy = x ^ 1, y ^ 1
            p = 2 * yy + xx

            def place(f, carry):
                plane = z ^ (f + 1)
                r1 = pl.ds(pl.multiple_of(plane * rows + p * quarter, 16), quarter)
                for j in range(4 * ng):
                    w1[r1, j * 128 : (j + 1) * 128] = blk[f, j * quarter : (j + 1) * quarter, :]
                for gg in range(ng):
                    r2 = pl.ds(pl.multiple_of(plane * n + gg * 128 + p * 32, 32), 32)
                    for kk in range(nk):
                        lo = 4 * ng * quarter + (gg * nk + kk) * 32
                        w2[r2, kk * 128 : (kk + 1) * 128] = blk[f, lo : lo + 32, :]
                return carry

            lax.fori_loop(0, 3, place, 0)
        for cp in early:
            cp.wait()

    @pl.when(b == nb)
    def _():
        for cp in loads()[1]:
            cp.wait()

    rr = pl.ds(pl.multiple_of(b * BLOCK, BLOCK), BLOCK)
    a = a2[rr, :]
    gr = g[rr, :]
    per = 2 // ng
    for k in range(2 * ng):
        cols = slice(k * 256, (k + 1) * 256)
        lane = pl.ds(pl.multiple_of(c * (b1.shape[1] // 2) + go * 128, 128), n)
        bias = jnp.concatenate([b1[zz : zz + 1, lane] for zz in range(k * per, (k + 1) * per)], axis=1)
        u, s = gelu_and_slope(nn(a, w1[:, cols]) + bias)
        u_s[rr, cols] = u.astype(BF16)
        dz = (nt(gr, w2[cols, :]) * s).astype(BF16)
        dz_s[rr, cols] = dz
        db[0:1, cols] += jnp.sum(dz.astype(F32), axis=0, keepdims=True)
    yv = nn(u_s[rr, :], w2[...])
    dv = nt(dz_s[rr, :], w1[...])

    def put(y_ref, d_ref, y_old, d_old):
        y_ref[...] = (yv if y_old is None else yv + y_old[...].astype(F32)).astype(BF16)
        d_ref[...] = (dv if d_old is None else dv + d_old[...].astype(F32)).astype(BF16)

    @pl.when(b < nb)
    def _():
        put(yo, do, *((None, None) if first else prev[0:2]))

    @pl.when(b >= nb)
    def _():
        put(yp, dp, *((None, None) if first else prev[2:4]))

    @pl.when(b == last)
    def _():
        def weights(k, carry):
            cols = pl.ds(pl.multiple_of(k * 256, 256), 256)
            dw1[:, cols] = tn(a2[...], dz_s[:, cols]).astype(BF16)
            dw2[cols, :] = tn(u_s[:, cols], g[...]).astype(BF16)
            return carry

        lax.fori_loop(0, 2 * ng, weights, 0)
        for out, sel in ((send, 1 - meta[I_B1]), (keep, meta[I_B1])):
            for i in range(2):

                def cut(plane, carry):
                    r1 = pl.ds(pl.multiple_of(plane * rows + sel * 2 * quarter + i * quarter, 16), quarter)
                    for j in range(4 * ng):
                        out[i, plane, j * quarter : (j + 1) * quarter, :] = dw1[r1, j * 128 : (j + 1) * 128]
                    for gg in range(ng):
                        r2 = pl.ds(pl.multiple_of(plane * n + gg * 128 + sel * 64 + i * 32, 32), 32)
                        for kk in range(nk):
                            lo = 4 * ng * quarter + (gg * nk + kk) * 32
                            out[i, plane, lo : lo + 32, :] = dw2[r2, kk * 128 : (kk + 1) * 128]
                    return carry

                lax.fori_loop(0, 4, cut, 0)


def mlp(part, meta, a2o, a2p, g_o, g_p, b1, f1, f2, blocks, prev=()):
    ng, go = PARTS[part]
    first = not prev
    t, d = a2o.shape
    nb = t // BLOCK
    n = 128 * ng
    size = blocks[0].shape[1]
    sd = jax.ShapeDtypeStruct
    fixed = lambda s: pl.BlockSpec(s, lambda i, meta: (0,) * len(s), pipeline_mode=pl.Buffered(1))
    outf = lambda s: pl.BlockSpec(s, lambda i, meta: (0,) * len(s))
    own = pl.BlockSpec((BLOCK, d), lambda i, meta: (jnp.minimum(i, nb - 1), 0))
    other = pl.BlockSpec((BLOCK, d), lambda i, meta: (jnp.maximum(i - nb, 0), 0))
    tok = sd((t, d), BF16)
    half = (2, 4, size, 128)
    return pl.pallas_call(
        functools.partial(mlp_body, ng, go, first),
        grid_spec=pltpu.PrefetchScalarGridSpec(
            num_scalar_prefetch=1,
            grid=(2 * nb,),
            in_specs=[ANY] * 4 + [fixed(b1.shape)] + [ANY] * 2 + [fixed(k.shape) for k in blocks]
            + ([] if first else [own, own, other, other]),
            out_specs=[own, own, other, other, outf(half), outf(half), outf((8, 4 * n))],
            scratch_shapes=[
                pltpu.VMEM((2 * t, d), BF16), pltpu.VMEM((2 * t, d), BF16),
                pltpu.VMEM((2 * t, 4 * n), BF16), pltpu.VMEM((2 * t, 4 * n), BF16),
                pltpu.VMEM((d, 4 * n), BF16), pltpu.VMEM((4 * n, d), BF16),
                pltpu.VMEM((d, 4 * n), BF16), pltpu.VMEM((4 * n, d), BF16),
                pltpu.SemaphoreType.DMA((9,)),
            ],
        ),
        out_shape=[tok, tok, tok, tok, sd(half, BF16), sd(half, BF16), sd((8, 4 * n), F32)],
        compiler_params=params(),
        cost_estimate=pl.CostEstimate(flops=2 * 2 * t * d * 4 * n * 6, bytes_accessed=30 << 20, transcendentals=2 * t * 4 * n),
        name="hidden_first" if first else "hidden_second",
    )(meta, a2o, a2p, g_o, g_p, b1, f1, f2, *blocks, *prev)


EARLY = 8


def heads_back(pairs, lo, do, prob, inv, o, qkv, out):
    d = qkv.shape[1] // 3
    n = 128 * pairs
    lo_m, hi_m = lane_masks()
    for j in range(pairs):
        cols = slice(128 * (lo + j), 128 * (lo + j + 1))
        q, k, v = (qkv[:, i * d + cols.start : i * d + cols.stop] for i in range(3))
        dop = (do[:, 128 * j : 128 * (j + 1)].astype(F32) * inv[:, cols]).astype(BF16)
        dot = dop.astype(F32) * o[:, cols].astype(F32)
        dq = dk = dv = None
        for h, m in ((0, lo_m), (1, hi_m)):
            e = prob[0, 2 * j + h]
            mean = jnp.sum(dot * m.astype(F32), axis=-1, keepdims=True)
            dom = dop * m
            ds = (e.astype(F32) * (nt(dom, v) - mean)).astype(BF16)
            ms = m * SCALE
            parts = (nn(ds, k * ms), tn(ds, q * ms), tn(e, dom))
            dq, dk, dv = parts if dq is None else (dq + parts[0], dk + parts[1], dv + parts[2])
        for i, a in enumerate((dq, dk, dv)):
            out[:, i * n + 128 * j : i * n + 128 * (j + 1)] = a.astype(BF16)


def back_early_body(gp, da_o, da_p, x1_r, prob, inv, o, qkv, w_out, vec, dbf, dx1_o, dl, dq, acc):
    n = 64 * EARLY

    @pl.when(pl.program_id(0) == 0)
    def _():
        acc[...] = jnp.zeros_like(acc)
        acc[5:6] = dbf[0:1]

    da2 = da_o[...].astype(F32) + da_p[...].astype(F32)
    n2, r2 = norm_stats(x1_r[...])
    dx1 = gp[...].astype(F32) + norm_back(da2, n2, r2, vec[3:4])
    low = dx1.astype(BF16)
    acc[3:4] += jnp.sum(da2 * n2, axis=0, keepdims=True)
    acc[4:5] += jnp.sum(da2, axis=0, keepdims=True)
    acc[2:3] += jnp.sum(low.astype(F32), axis=0, keepdims=True)
    dx1_o[...] = dx1
    dl[...] = low
    do = nt(low, w_out[0:n, :]).astype(BF16)
    heads_back(EARLY // 2, 0, do, prob, inv, o, qkv, dq)


def back_early(gp, da_o, da_p, x1, prob, inv, o, qkv, w, vec, dbf):
    t, d = gp.shape
    blk = lambda n: pl.BlockSpec((BLOCK, n), lambda b: (b, 0))
    sd = jax.ShapeDtypeStruct
    fixed = lambda s: pl.BlockSpec(s, lambda b: (0,) * len(s), pipeline_mode=pl.Buffered(1))
    cols = 3 * 64 * EARLY
    return pl.pallas_call(
        back_early_body,
        grid=(t // BLOCK,),
        in_specs=[blk(d), blk(d), blk(d), blk(d),
                  pl.BlockSpec((1, EARLY, BLOCK, BLOCK), lambda b: (b, 0, 0, 0)), blk(d), blk(d), blk(3 * d),
                  pl.BlockSpec((d, d), lambda b: (0, 3), pipeline_mode=pl.Buffered(1)),
                  fixed(vec.shape), fixed(dbf.shape)],
        out_specs=[blk(d), blk(d), blk(cols), pl.BlockSpec((128, d), lambda b: (0, 0))],
        out_shape=[sd((t, d), F32), sd((t, d), BF16), sd((t, cols), BF16), sd((128, d), F32)],
        compiler_params=params(),
        cost_estimate=pl.CostEstimate(flops=2 * t * d * 4 * d, bytes_accessed=24 << 20, transcendentals=0),
        name="attend_back_early",
    )(gp, da_o, da_p, x1, prob, inv, o, qkv, w, vec, dbf)


def back_late_body(meta, *refs):
    tok = refs[0:4]
    dx1, dl, dqe, prob, inv, o, qkv, w, vec, acc_in = refs[4:14]
    gt_o, dq, acc = refs[14:17]
    gt, sems = refs[17:]
    b = pl.program_id(0)
    nb = pl.num_programs(0)
    d = dl.shape[1]
    slot = lax.rem(b, 2)
    n = 64 * EARLY

    def puts(step, sl):
        return [
            pltpu.make_async_copy(
                gt.at[sl, pl.ds(i * UNIT, UNIT)],
                gt_o.at[pl.ds(pl.multiple_of(meta[PER * step + i] * UNIT, UNIT), UNIT)],
                sems.at[sl, i],
            )
            for i in range(PER)
        ]

    @pl.when(b == 0)
    def _():
        acc[...] = acc_in[...]

    @pl.when(b >= 2)
    def _():
        for cp in puts(b - 2, slot):
            cp.wait()

    do = nt(dl[...], w[n:, 3 * d : 4 * d]).astype(BF16)
    heads_back((HEADS - EARLY) // 2, EARLY // 2, do, prob, inv, o, qkv, dq)
    rest = d - n
    da1 = None
    for i in range(3):
        part = nt(dqe[:, i * n : (i + 1) * n], w[:, i * d : i * d + n])
        part = part + nt(dq[:, i * rest : (i + 1) * rest], w[:, i * d + n : (i + 1) * d])
        da1 = part if da1 is None else da1 + part
    x = jnp.concatenate([r[...] for r in tok], axis=0).astype(F32)
    n1, r1 = norm_stats(x)
    acc[0:1] += jnp.sum(da1 * n1, axis=0, keepdims=True)
    acc[1:2] += jnp.sum(da1, axis=0, keepdims=True)
    gt[slot] = dx1[...] + norm_back(da1, n1, r1, vec[0:1])
    for cp in puts(b, slot):
        cp.start()

    @pl.when(b == nb - 1)
    def _():
        for cp in puts(b - 1, 1 - slot) + puts(b, slot):
            cp.wait()


def back_late(meta, tokens, dx1, dl, dqe, prob, inv, o, qkv, w, vec, acc_in):
    t, d = tokens.shape
    late = HEADS - EARLY
    blk = lambda n: pl.BlockSpec((BLOCK, n), lambda b, meta: (b, 0))
    sd = jax.ShapeDtypeStruct
    fixed = lambda s: pl.BlockSpec(s, lambda b, meta: (0,) * len(s), pipeline_mode=pl.Buffered(1))
    return pl.pallas_call(
        back_late_body,
        grid_spec=pltpu.PrefetchScalarGridSpec(
            num_scalar_prefetch=1,
            grid=(t // BLOCK,),
            in_specs=[unit_spec(i, d) for i in range(PER)] + [
                blk(d), blk(d), blk(dqe.shape[1]),
                pl.BlockSpec((1, late, BLOCK, BLOCK), lambda b, meta: (b, EARLY // late, 0, 0)), blk(d), blk(d), blk(3 * d),
            ] + [fixed(a.shape) for a in (w, vec, acc_in)],
            out_specs=[ANY, blk(3 * 64 * late), pl.BlockSpec((128, d), lambda b, meta: (0, 0))],
            scratch_shapes=[pltpu.VMEM((2, BLOCK, d), F32), pltpu.SemaphoreType.DMA((2, PER))],
        ),
        out_shape=[sd((t, d), F32), sd((t, 3 * 64 * late), BF16), sd((128, d), F32)],
        compiler_params=params(),
        cost_estimate=pl.CostEstimate(flops=2 * t * d * 5 * d, bytes_accessed=20 << 20, transcendentals=0),
        name="attend_back_late",
    )(meta, *([tokens] * PER), dx1, dl, dqe, prob, inv, o, qkv, w, vec, acc_in)


def split(meta, stage, send_o, keep_o, at, width):
    c = meta[I_C]
    rows = stage.shape[0] // 4
    n = rows // 2
    for zz in range(4):
        for i in range(2):
            for out, h in ((send_o, 1 - c), (keep_o, c)):
                lot = stage[pl.ds(pl.multiple_of(zz * rows + n * h + (n // 2) * i, 16), n // 2), 0:width]
                out[i, 0, zz, :, pl.ds(at, width)] = lot[0 : n // 4]
                out[i, 1, zz, :, pl.ds(at, width)] = lot[n // 4 :]


def grads_early_body(meta, a1, dq, o, dl, send_o, keep_o, stage):
    d = a1.shape[1]
    s = pl.program_id(0)
    last = pl.num_programs(0) - 1

    @pl.when(s < last)
    def _():
        stage[...] = tn(a1[...], dq[...]).astype(BF16)

    @pl.when(s == last)
    def _():
        stage[...] = tn(o[...], dl[...]).astype(BF16)

    split(meta, stage, send_o, keep_o, pl.multiple_of(s * d, 128), d)


def grads_late_body(meta, a1, dq, acc, dba, dbb, send_o, keep_o, stage):
    d = a1.shape[1]
    c = meta[I_C]
    rows = d // 4
    stage[...] = tn(a1[...], dq[...]).astype(BF16)
    split(meta, stage, send_o, keep_o, 0, d)
    stage[:, 0:128] = acc[...].T.astype(BF16)
    stage[:, 128:256] = jnp.zeros((d, 128), BF16)
    for zz in range(4):
        parts = []
        for hh in range(2):
            for src, (ng, go) in ((dba, PARTS[0]), (dbb, PARTS[1])):
                for k in range(ng):
                    at = (zz * ng + k) * 128
                    parts.append(jnp.where(hh == c, src[0:1, at : at + 128], 0.0))
        parts.append(jnp.zeros((16 - len(parts), 128), F32))
        stage[zz * rows : zz * rows + 16, 128:256] = jnp.concatenate(parts, axis=0).astype(BF16)
    split(meta, stage, send_o, keep_o, d, EXT)


def grads(body, steps, wide, meta, a1, dq, *rest, cost=None):
    t, d = a1.shape
    cost = cost or pl.CostEstimate(flops=2 * t * d * steps * d, bytes_accessed=12 << 20, transcendentals=0)
    half = (2, 2, 4, d // 32, wide)
    sd = jax.ShapeDtypeStruct
    fixed = lambda a: pl.BlockSpec(a.shape, lambda s, meta: (0,) * a.ndim, pipeline_mode=pl.Buffered(1))
    outf = pl.BlockSpec(half, lambda s, meta: (0,) * 5)
    last = dq.shape[1] // d - 1
    return pl.pallas_call(
        body,
        grid_spec=pltpu.PrefetchScalarGridSpec(
            num_scalar_prefetch=1,
            grid=(steps,),
            in_specs=[fixed(a1), pl.BlockSpec((t, d), lambda s, meta: (0, jnp.minimum(s, last)))]
            + [fixed(a) for a in rest],
            out_specs=[outf, outf],
            scratch_shapes=[pltpu.VMEM((d, d), BF16)],
        ),
        out_shape=[sd(half, BF16), sd(half, BF16)],
        compiler_params=params(),
        cost_estimate=cost,
        name="weight_grads",
    )(meta, a1, dq, *rest)


def out_body(meta, ya, yb, x1, vec, out, buf, sems):
    b = pl.program_id(0)
    slot = lax.rem(b, 2)

    def puts(step, sl):
        return [
            pltpu.make_async_copy(
                buf.at[sl, pl.ds(i * UNIT, UNIT)],
                out.at[pl.ds(pl.multiple_of(meta[PER * step + i] * UNIT, UNIT), UNIT)],
                sems.at[sl, i],
            )
            for i in range(PER)
        ]

    @pl.when(b >= 2)
    def _():
        for cp in puts(b - 2, slot):
            cp.wait()

    y = ya[...].astype(F32) + yb[...].astype(F32)
    buf[slot] = (x1[...] + (y + vec[5:6])).astype(BF16)
    for cp in puts(b, slot):
        cp.start()

    @pl.when(b == pl.num_programs(0) - 1)
    def _():
        for cp in puts(b - 1, 1 - slot) + puts(b, slot):
            cp.wait()


def layer_output(meta, ya, yb, x1, vec):
    t, d = x1.shape
    blk = lambda n: pl.BlockSpec((BLOCK, n), lambda b, meta: (b, 0))
    fixed = lambda s: pl.BlockSpec(s, lambda b, meta: (0,) * len(s), pipeline_mode=pl.Buffered(1))
    return pl.pallas_call(
        out_body,
        grid_spec=pltpu.PrefetchScalarGridSpec(
            num_scalar_prefetch=1,
            grid=(t // BLOCK,),
            in_specs=[blk(d), blk(d), blk(d), fixed(vec.shape)],
            out_specs=ANY,
            scratch_shapes=[pltpu.VMEM((2, BLOCK, d), BF16), pltpu.SemaphoreType.DMA((2, PER))],
        ),
        out_shape=jax.ShapeDtypeStruct((t, d), BF16),
        compiler_params=params(),
        cost_estimate=pl.CostEstimate(flops=4 * t * d, bytes_accessed=8 << 20, transcendentals=0),
        name="layer_out",
    )(meta, ya, yb, x1, vec)


def halve_body(jobs, meta, *refs):
    at, to = 0, sum(2 * n for _, n, _ in jobs)
    for place, n, loops in jobs:
        ks, vs, (send, keep) = refs[at : at + n], refs[at + n : at + 2 * n], refs[to : to + 2]
        at, to = at + 2 * n, to + 2
        bit = meta[place]
        for out, sel in ((send, 1 - bit), (keep, bit)):
            for pre in range(ks[0].shape[0]):

                def step(r, carry):
                    col = 0
                    for k, v in zip(ks, vs):
                        w = k.shape[-1]
                        part = k[pre, sel, r].astype(F32) + v[pre, sel, r].astype(F32)
                        out[pre, r, :, col : col + w] = part.astype(BF16)
                        col += w
                    return carry

                lax.fori_loop(0, loops, step, 0)


def halve(meta, *jobs):
    sd = jax.ShapeDtypeStruct
    jobs = [(p, k if isinstance(k, list) else [k], v if isinstance(v, list) else [v]) for p, k, v in jobs]
    outs = []
    for _, ks, _ in jobs:
        shape = ks[0].shape
        outs += [sd((shape[0],) + shape[2:-1] + (sum(k.shape[-1] for k in ks),), BF16)] * 2
    arrays = [a for _, ks, vs in jobs for a in (*ks, *vs)]
    size = sum(a.size for a in arrays) // 2
    return pl.pallas_call(
        functools.partial(halve_body, tuple((p, len(ks), ks[0].shape[2]) for p, ks, _ in jobs)),
        in_specs=[pl.BlockSpec(memory_space=pltpu.SMEM)] + [WHOLE] * len(arrays),
        out_specs=[WHOLE] * len(outs),
        out_shape=outs,
        compiler_params=params(),
        cost_estimate=pl.CostEstimate(flops=size, bytes_accessed=6 * size, transcendentals=0),
        name="add_halve",
    )(meta, *arrays)


def total(routes, k, v):
    piece = k.astype(F32) + v.astype(F32)
    if routes.n_dp > 8:
        groups = [[j + 8 * o for o in range(routes.n_dp // 8)] for j in range(8)]
        piece = lax.psum(piece, "dp", axis_index_groups=groups)
    return piece.astype(BF16)


def ranks(meta, t):
    cc, x, y = holder(meta, t)
    return cc, 2 * jnp.where(cc == 0, x, y) + jnp.where(cc == 0, y, x)


def final_hidden_body(meta, *refs):
    pieces = refs[:8]
    d1, d2 = refs[8:10]
    rows, ff = d1.shape
    d = d2.shape[1]
    quarter = rows // 4
    nk = d // 128
    for t in range(8):
        cc, q = ranks(meta, t)
        at = 0
        for ng, go in PARTS:
            r1 = pl.ds(pl.multiple_of(q * quarter, 16), quarter)
            for zz in range(4):
                for g in range(ng):
                    col = pl.multiple_of(zz * (ff // 4) + cc * (ff // 8) + (go + g) * 128, 128)
                    d1[r1, pl.ds(col, 128)] = pieces[t][at : at + quarter, :].astype(F32)
                    at += quarter
            for g in range(ng):
                r2 = pl.ds(pl.multiple_of(cc * (ff // 8) + (go + g) * 128 + q * 32, 32), 32)
                for k in range(nk):
                    d2[r2, k * 128 : (k + 1) * 128] = pieces[t][at : at + 32, :].astype(F32)
                    at += 32


def final_mixed_body(meta, *refs):
    pieces = refs[:8]
    dqkv, dout, dg1, ds1, dbo, dg2, ds2, dbf, db1 = refs[8:17]
    ext = refs[17]
    n = pieces[0].shape[0]
    d = dout.shape[1]
    for t in range(8):
        cc, x, y = holder(meta, t)
        first, second = jnp.where(cc == 0, x, y), jnp.where(cc == 0, y, x)
        rows = pl.ds(pl.multiple_of(n * (4 * cc + 2 * first + second), n), n)
        v = pieces[t][...].astype(F32)
        m = 64 * EARLY
        for k in range(3):
            dqkv[rows, k * d : k * d + m] = v[:, k * m : (k + 1) * m]
            at = 3 * m + d + k * (d - m)
            dqkv[rows, k * d + m : (k + 1) * d] = v[:, at : at + d - m]
        dout[rows, :] = v[:, 3 * m : 3 * m + d]
        ext[rows, :] = v[:, 4 * d :]
    vec = ext[:, 0:128].T
    for i, ref in enumerate((dg1, ds1, dbo, dg2, ds2, dbf)):
        ref[...] = vec[i]
    for r in range(db1.shape[0] // 128):
        db1[pl.ds(128 * r, 128)] = ext[r, 128:256]


def final(body, meta, pieces, outs, scratch=()):
    sd = [jax.ShapeDtypeStruct(s, F32) for s in outs]
    res = pl.pallas_call(
        body,
        in_specs=[pl.BlockSpec(memory_space=pltpu.SMEM)] + [WHOLE] * 8,
        out_specs=[WHOLE] * len(outs),
        scratch_shapes=list(scratch),
        out_shape=sd,
        compiler_params=params(),
        name="place_sums",
    )(meta, *pieces)
    return res


def scalars(chip_ids):
    n = chip_ids.shape[0] // UNIT
    ids = chip_ids.reshape(n, UNIT)[:, 0]
    here = jnp.arange(n, dtype=jnp.int32)
    same = (ids[:, None] == ids[None, :]).astype(jnp.int32)
    long = jnp.sum(same, axis=1) > 1
    longs = long.astype(jnp.int32)
    before = jnp.sum(jnp.where(here[None, :] < here[:, None], longs[None, :], 0), axis=1)
    total = jnp.sum(longs)
    pos = jnp.where(long, before, total + here - before)
    src = jnp.sum(jnp.where(pos[None, :] == here[:, None], here[None, :], 0), axis=1)
    dp, z = lax.axis_index("dp"), lax.axis_index("fsdp")
    c, x, y = dp & 1, (dp >> 1) & 1, (dp >> 2) & 1
    b1, b2 = jnp.where(c == 0, x, y), jnp.where(c == 0, y, x)
    rest = jnp.stack([total >> 2, c, x, y, z, b1, b2, jnp.zeros_like(z), z & 1, z >> 1]).astype(jnp.int32)
    return jnp.concatenate([src.astype(jnp.int32), rest])


def on_device(n_dp, n_z, tokens, chip_ids, ln1_gain, ln1_bias, w_qkv, w_out, b_out, ln2_gain, ln2_bias,
              w_fc1, b_fc1, w_fc2, b_fc2, cotangent):
    routes = Routes(n_dp, n_z)
    t, d = tokens.shape
    ff = w_fc1.shape[1]
    rows = w_qkv.shape[0]
    pos = lax.axis_index("dp").astype(jnp.int32).reshape(1)
    meta = scalars(chip_ids)

    vecs = (ln1_gain, ln1_bias, b_out, ln2_gain, ln2_bias, b_fc2)
    mixed, near, far, ha, hb = pack(pos, w_qkv, w_out, vecs, b_fc1, w_fc1, w_fc2)

    def planes(own, other):
        return routes.z_flip(jnp.stack([own, other]), 2)

    join = lambda other, two: jnp.concatenate([other[None], two], axis=0)
    mate_a, mate_b = routes.z_flip(ha, 1), routes.z_flip(hb, 1)
    two_a = planes(ha, mate_a)
    p_mixed = gather_mixed(routes, near, far, mate_a, (two_a, mate_b))
    block_a = join(mate_a, two_a)
    p_a = around(routes, block_a)
    two_b = planes(hb, tie(mate_b, block_a))
    qkv, prob, inv, o, x1, a2, a1, gp, w, vec, b1, dbf = k1(meta, tokens, cotangent, tie(mixed, block_a), p_mixed, ff)
    block_b = join(mate_b, tie(two_b, a2))
    p_b = around(routes, block_b)

    swap = lax.optimization_barrier((a2, gp, block_b, *p_a))
    a2p, gpp = routes.core(swap[0]), routes.core(swap[1])
    *part, sa, ka, dba = mlp(0, meta, a2, a2p, gp, gpp, b1, w_fc1, w_fc2, p_a)
    got_a = routes.first(sa)
    yo, do, yp, dp, sb, kb, dbb = mlp(1, meta, a2, a2p, gp, gpp, b1, w_fc1, w_fc2, p_b, part)

    def view(a, pre, rest):
        return a.reshape((pre, 2) + rest)

    tall = lambda a: (4 * a.shape[2] // 96, 96, 128)
    flat = lambda a: (a.shape[2] // 96, 96, 128)
    size_a, size_b = tall(sa), tall(sb)
    s_a, k_a = halve(meta, (I_B2, view(ka, 1, size_a), view(got_a, 1, size_a)))
    dp, yp, sb = lax.optimization_barrier((dp, yp, sb, got_a))[:3]
    dq = routes.core(dp)
    yq = routes.core(yp)
    got_a, got_b = routes.second(s_a), routes.first(sb)
    dx1, dl, dqe, acc = back_early(tie(gp, s_a), do, dq, x1, prob, inv, o, qkv, w, vec, dbf)
    early = 3 * 64 * EARLY + d
    late = 4 * d - early + EXT
    sm, km = grads(grads_early_body, early // d, early, meta, tie(a1, yq), dqe, o, dl, cost=SHORT)
    got_m = routes.core(tie(sm, got_a, got_b))

    lo_a, lo_b = (2, 2) + flat(sa), (2, 2) + flat(sb)
    hi_a, hi_b = (1,) + lo_a[1:], (1,) + lo_b[1:]
    s_a, k_a, s_b, k_b = halve(meta, (I_Z + 4, k_a.reshape(lo_a), tie(got_a, sm).reshape(lo_a)),
                               (I_B2, view(kb, 1, size_b), view(tie(got_b, sm), 1, size_b)))
    got_a, got_b = routes.z_flip(s_a, 1), routes.second(s_b)
    chunk = lambda a, pre, loops: a.reshape(pre, 2, loops, d // 32, a.shape[-1])
    s_m, k_m = halve(meta, (I_B1, chunk(km, 1, 8), chunk(tie(got_m, s_b), 1, 8)))
    got_m = routes.first(s_m)
    gt, dql, acc = back_late(meta, tokens, tie(dx1, s_m), dl, dqe, prob, inv, o, qkv, w, vec, acc)

    s_a, k_a, s_b, k_b, s_m, k_m = halve(
        meta, (I_Z + 5, k_a.reshape(hi_a), tie(got_a, acc).reshape(hi_a)),
        (I_Z + 4, k_b.reshape(lo_b), tie(got_b, acc).reshape(lo_b)),
        (I_B2, chunk(k_m, 1, 4), chunk(tie(got_m, acc), 1, 4)))
    got_m = routes.second(s_m)
    got_a, got_b = routes.z_flip(s_a, 2), routes.z_flip(s_b, 1)
    sl, kl = grads(grads_late_body, 1, late, meta, tie(a1, s_m), dql, acc, dba, dbb)
    joint = lambda a, b: jnp.concatenate([a.reshape(-1, 128), b.reshape(-1, 128)], axis=0)
    got_l = routes.core(tie(sl, got_m, got_a, got_b))
    s_m, k_m, s_b, k_b = halve(
        meta, (I_Z + 4, chunk(k_m, 2, 1), chunk(tie(got_m, sl), 2, 1)),
        (I_Z + 5, k_b.reshape(hi_b), tie(got_b, sl).reshape(hi_b)))
    got_m, got_b = routes.z_flip(s_m, 1), routes.z_flip(s_b, 2)
    s_l, k_l = halve(meta, (I_B1, chunk(kl, 1, 8), chunk(tie(got_l, s_b), 1, 8)))
    got_l = routes.first(s_l)
    layer_out = layer_output(meta, yo, yq, x1, tie(vec, s_l))
    s_l, k_l, s_m, k_m = halve(meta, (I_B2, chunk(k_l, 1, 4), chunk(tie(got_l, layer_out), 1, 4)),
                               (I_Z + 5, chunk(k_m, 1, 1), chunk(tie(got_m, layer_out), 1, 1)))
    got_l, got_m = routes.second(s_l), routes.z_flip(s_m, 2)
    piece = total(routes, joint(k_a, k_b), joint(got_a, tie(got_b, s_l)))
    near_by = around(routes, piece)
    s_l, k_l = halve(meta, (I_Z + 4, chunk(k_l, 2, 1), chunk(tie(got_l, piece), 2, 1)))
    s_l, k_l = halve(meta, (I_Z + 5, chunk(k_l, 1, 1), chunk(tie(routes.z_flip(s_l, 1), got_m), 1, 1)))
    got_l = tie(routes.z_flip(s_l, 2), *near_by)
    side = lambda a, b: jnp.concatenate([a.reshape(d // 32, -1), b.reshape(d // 32, -1)], axis=1)
    piece = total(routes, side(k_m, k_l), side(got_m, got_l))
    near_m = around(routes, piece)
    pieces = near_by + [routes.core(b) for b in lax.optimization_barrier((*near_by, piece))[:4]]
    g_fc1, g_fc2 = final(final_hidden_body, meta, pieces, [w_fc1.shape, w_fc2.shape])
    near_m = list(lax.optimization_barrier((*near_m, g_fc1))[:4])
    pieces_m = near_m + [routes.core(b) for b in near_m]

    vecs = [(rows,)] * 6
    g_qkv, g_out, dg1, ds1, dbo, dg2, ds2, dbf2, db1 = final(
        final_mixed_body, meta, pieces_m, [w_qkv.shape, w_out.shape, *vecs, b_fc1.shape],
        [pltpu.VMEM((rows, EXT), F32)])
    return (layer_out, gt, dg1, ds1, g_qkv, g_out, dbo, dg2, ds2, g_fc1, db1, g_fc2, dbf2)


def solution(mesh):
    token, part, plain = P(ALL, None), P("fsdp", None), P("fsdp")
    return jax.shard_map(
        functools.partial(on_device, mesh.shape["dp"], mesh.shape["fsdp"]),
        mesh=mesh,
        in_specs=(token, P(ALL), plain, plain, part, part, plain, plain, plain, part, plain, part, plain, token),
        out_specs=(token, token, plain, plain, part, part, plain, plain, plain, part, plain, part, plain),
        check_vma=False,
    )
```

profile of v0, /device:TPU:0, one launch (start us, length us, event | category | flops | bytes accessed | tf_op | source)
XLA Modules:
  0.0 290.8 jit_solution(3016856859279180347)
XLA Ops:
  0.7 3.8 %pack.1 = (bf16[192,3328]{1,0:T(8,128)(2,1)}, bf16[48,3328]{1,0:T(8,128)(2,1)}, bf16[48,1664]{1,0:T(8,128)(2,1)}, bf16[384,128]{1,0:T(8,128)(2,1)}, bf16[768,128]{1,0:T(8,128)(2,1)}) custom-call(s32[1]{0:T(128)} %bitcast.9.pos, bf16[192,2304]{1,0:T(8,128)(2,1)} %refs_0_.3, bf16[192,768]{1,0:T(8,128)(2,1)} %refs_1_.3, bf16[192]{0:T(256)(128)(2,1)} %refs_2_.3, ...), custom_call_target="tpu_custom_call" | custom-call | tf_op jit(solution)/shard_map/pack/pallas_call | solution.py:195
  4.5 3.1 %collective-permute-start.2 = (bf16[48,3328]{1,0:T(8,128)(2,1)}, bf16[48,3328]{1,0:T(8,128)(2,1)S(1)}, u32[]{:S(2)}, u32[]{:S(2)}) collective-permute-start(bf16[48,3328]{1,0:T(8,128)(2,1)} %get-tuple-element.137), channel_id=1, source_target_pairs={{0,1},{1,2},{2,3},{3,0},{4,7},{5,4},{6,5},{7,6},{8,9},{9,10},{10,1... | collective-permute-start | bytes 958472 | tf_op jit(solution)/shard_map/ppermute | solution.py:79
  7.6 2.6 collective-permute-start.3
  10.3 11.8 %collective-permute-done.3 = bf16[48,1664]{1,0:T(8,128)(2,1)S(1)} collective-permute-done((bf16[48,1664]{1,0:T(8,128)(2,1)}, bf16[48,1664]{1,0:T(8,128)(2,1)S(1)}, u32[]{:S(2)}, u32[]{:S(2)}) %collective-permute-start.3) | collective-permute-done | bytes 159776 | tf_op jit(solution)/shard_map/ppermute | solution.py:82
  26.8 3.3 %collective-permute-start.1 = (bf16[2,384,128]{2,1,0:T(8,128)(2,1)S(1)}, bf16[2,384,128]{2,1,0:T(8,128)(2,1)S(1)}, u32[]{:S(2)}, u32[]{:S(2)}) collective-permute-start(bf16[2,384,128]{2,1,0:T(8,128)(2,1)S(1)} %pad_maximum_fusion.4), channel_id=1, source_target_pairs={{0,2},{1,3},{2,0},{3,1},{4,6},{5,7},{6,4},{7,5},{8,10},{9,11},{10,... | collective-permute-start | bytes 589832 | tf_op jit(solution)/shard_map/ppermute | solution.py:85
  32.7 2.1 collective-permute-done.6
  34.8 2.7 collective-permute-done.1
  40.3 5.9 %collective-permute-done.7.refs_12_ = bf16[48,4992]{1,0:T(8,128)(2,1)S(1)} collective-permute-done((bf16[48,4992]{1,0:T(8,128)(2,1)S(1)}, bf16[48,4992]{1,0:T(8,128)(2,1)S(1)}, u32[]{:S(2)}, u32[]{:S(2)}) %collective-permute-start.7) | collective-permute-done | bytes 479264 | tf_op jit(solution)/shard_map/ppermute | solution.py:76
  52.8 23.5 %norm_qkv_attend.1 = (bf16[1024,2304]{1,0:T(8,128)(2,1)}, bf16[4,12,256,256]{3,2,1,0:T(8,128)(2,1)}, f32[1024,768]{1,0:T(8,128)}, bf16[1024,768]{1,0:T(8,128)(2,...) custom-call(s32[26]{0:T(128)} %concatenate.24.meta, ...), custom_call_target="tpu_custom_call" | custom-call | flops 6039797760 | bytes 41943040 | tf_op jit(solution)/shard_map/norm_qkv_attend/pallas_call | solution.py:307
  84.3 21.1 %hidden_first.1 = (bf16[1024,768]{1,0:T(8,128)(2,1)}, bf16[1024,768]{1,0:T(8,128)(2,1)}, bf16[1024,768]{1,0:T(8,128)(2,1)}, bf16[1024,768]{1,0:T(8,128)(2,1)}, b...) custom-call(s32[26]{0:T(128)} %concatenate.24.meta, ...), custom_call_target="tpu_custom_call" | custom-call | flops 9663676416 | bytes 31457280 | tf_op jit(solution)/shard_map/hidden_first/pallas_call | solution.py:483
  108.0 36.8 %hidden_second.1 = (bf16[1024,768]{1,0:T(8,128)(2,1)}, bf16[1024,768]{1,0:T(8,128)(2,1)}, bf16[1024,768]{1,0:T(8,128)(2,1)}, bf16[1024,768]{1,0:T(8,128)(2,1)}, ...) custom-call(s32[26]{0:T(128)} %concatenate.24.meta, ...), custom_call_target="tpu_custom_call" | custom-call | flops 19327352832 | bytes 31457280 | tf_op jit(solution)/shard_map/hidden_second/pallas_call | solution.py:483
  146.9 2.6 add_halve.9
  150.9 15.9 %attend_back_early.1 = (f32[1024,768]{1,0:T(8,128)}, bf16[1024,768]{1,0:T(8,128)(2,1)}, bf16[1024,1536]{1,0:T(8,128)(2,1)}, f32[128,768]{1,0:T(8,128)}) custom-call(bf16[1024,768]{1,0:T(8,128)(2,1)} %get-tuple-element.166.refs_2_.gp, bf16[1024,768]{1,0:T(8,128)(2,1)} %get-tuple-element.167.da_o, bf16[1024,768]{1,0:T(8,128)(2,1)} %collective-permute-done.24.da_p, ...), custom_call_target="tpu_custom_call" | custom-call | flops 4831838208 | bytes 25165824 | tf_op jit(solution)/shard_map/attend_back_early/pallas_call | solution.py:558
  166.8 9.9 %weight_grads.2 = (bf16[2,2,4,24,2304]{4,3,2,1,0:T(8,128)(2,1)}, bf16[2,2,4,24,2304]{4,3,2,1,0:T(8,128)(2,1)}) custom-call(s32[26]{0:T(128)} %concatenate.24.meta, bf16[1024,768]{1,0:T(8,128)(2,1)} %get-tuple-element.199.a1, bf16[1024,1536]{1,0:T(8,128)(2,1)} %get-tuple-element.175.dq.refs_6_, bf16[1024,768]{1,0:T(8,128)(2,1)} %get-tuple-element.171.o.refs_9_, ...), custom_call_target="tpu_custom_call" | custom-call | flops 1 | bytes 1 | tf_op jit(solution)/shard_map/weight_grads/pallas_call | solution.py:706
  176.9 4.3 %add_halve.10 = (bf16[2,4,96,128]{3,2,1,0:T(8,128)(2,1)}, bf16[2,4,96,128]{3,2,1,0:T(8,128)(2,1)}, bf16[1,32,96,128]{3,2,1,0:T(8,128)(2,1)}, bf16[1,32,96,128]{3,2,1,0:T(8,128)(2,1)}) custom-call(s32[26]{0:T(128)} %concatenate.24.meta, bf16[2,2,4,96,128]{4,3,2,1,0:T(8,128)(2,1)} %bitcast.62, bf16[2,2,4,96,128]{4,3,2,1,0:T(8,128)(2,1)} %bitcast.18.refs_1_, ...), custom_call_target="tpu_custom_call" | custom-call | flops 983040 | bytes 5898240 | tf_op jit(solution)/shard_map/add_halve/pallas_call | solution.py:803
  181.2 3.7 %add_halve.11 = (bf16[1,8,24,2304]{3,2,1,0:T(8,128)(2,1)}, bf16[1,8,24,2304]{3,2,1,0:T(8,128)(2,1)}) custom-call(s32[26]{0:T(128)} %concatenate.24.meta, bf16[1,2,8,24,2304]{4,3,2,1,0:T(8,128)(2,1)} %bitcast.53, bf16[1,2,8,24,2304]{4,3,2,1,0:T(8,128)(2,1)} %bitcast.23.refs_1_), custom_call_target="tpu_custom_call" | custom-call | flops 884736 | bytes 5308416 | tf_op jit(solution)/shard_map/add_halve/pallas_call | solution.py:803
  187.1 3.8 %collective-permute-start.26 = (bf16[2,4,96,128]{3,2,1,0:T(8,128)(2,1)}, bf16[2,4,96,128]{3,2,1,0:T(8,128)(2,1)}, u32[]{:S(2)}, u32[]{:S(2)}) collective-permute-start(bf16[2,4,96,128]{3,2,1,0:T(8,128)(2,1)} %get-tuple-element.183), channel_id=1, source_target_pairs={{0,1},{1,0},{2,3},{3,2},{4,5},{5,4},{6,7},{7,6},{8,9},{9,8},{10,11... | collective-permute-start | bytes 589832 | tf_op jit(solution)/shard_map/ppermute | solution.py:85
  190.9 19.3 %attend_back_late.1 = (f32[1024,768]{1,0:T(8,128)}, bf16[1024,768]{1,0:T(8,128)(2,1)}, f32[128,768]{1,0:T(8,128)}) custom-call(s32[26]{0:T(128)} %concatenate.24.meta, bf16[1024,768]{1,0:T(8,128)(2,1)} %refs_3_.5, bf16[1024,768]{1,0:T(8,128)(2,1)} %refs_3_.5, bf16[1024,768]{1,0:T(8,128)(2,1)} %refs_3_.5, bf16[1024,768]{1,0:T(8,128)(2,1)} %refs_3_.5, ...), custom_call_target="tpu_custom_call" | custom-call | flops 6039797760 | bytes 20971520 | tf_op jit(solution)/shard_map/attend_back_late/pallas_call | solution.py:631
  210.2 4.0 %add_halve.12 = (bf16[1,4,96,128]{3,2,1,0:T(8,128)(2,1)}, bf16[1,4,96,128]{3,2,1,0:T(8,128)(2,1)}, bf16[2,8,96,128]{3,2,1,0:T(8,128)(2,1)}, bf16[2,8,96,128]{3,2...) custom-call(s32[26]{0:T(128)} %concatenate.24.meta, ...), custom_call_target="tpu_custom_call" | custom-call | flops 933888 | bytes 5603328 | tf_op jit(solution)/shard_map/add_halve/pallas_call | solution.py:803
  216.8 5.4 %weight_grads.3 = (bf16[2,2,4,24,1024]{4,3,2,1,0:T(8,128)(2,1)}, bf16[2,2,4,24,1024]{4,3,2,1,0:T(8,128)(2,1)}) custom-call(s32[26]{0:T(128)} %concatenate.24.meta, bf16[1024,768]{1,0:T(8,128)(2,1)} %get-tuple-element.199.a1, bf16[1024,768]{1,0:T(8,128)(2,1)} %get-tuple-element.200.dq, f32[128,768]{1,0:T(8,128)} %get-tuple-element.192.acc, ...), custom_call_target="tpu_custom_call" | custom-call | flops 1207959552 | bytes 12582912 | tf_op jit(solution)/shard_map/weight_grads/pallas_call | solution.py:706
  222.2 3.4 %collective-permute-done.31 = bf16[1,4,96,128]{3,2,1,0:T(8,128)(2,1)} collective-permute-done((bf16[1,4,96,128]{3,2,1,0:T(8,128)(2,1)}, bf16[1,4,96,128]{3,2,1,0:T(8,128)(2,1)}, u32[]{:S(2)}, u32[]{:S(2)}) %collective-permute-start.31) | collective-permute-done | bytes 98336 | tf_op jit(solution)/shard_map/ppermute | solution.py:85
  227.5 2.6 add_halve.13
  230.2 2.5 add_halve.14
  235.3 5.4 %layer_out.1 = bf16[1024,768]{1,0:T(8,128)(2,1)} custom-call(s32[26]{0:T(128)} %concatenate.24.meta, bf16[1024,768]{1,0:T(8,128)(2,1)} %get-tuple-element.153.ya, bf16[1024,768]{1,0:T(8,128)(2,1)} %collective-permute-done.22.yb, f32[1024,768]{1,0:T(8,128)} %get-tuple-element.159.x1_r.x1, f32[16,768]{1,0:T(8,128)} %get-tuple-element.215.vec.refs_12_), custom_call_target="tpu_custom_call" | custom-call | flops 3145728 | bytes 8388608 | tf_op jit(solution)/shard_map/layer_out/pallas_call | solution.py:757
  240.7 4.6 %collective-permute-done.35 = bf16[2,1,24,2304]{3,2,0,1:T(8,128)(2,1)} collective-permute-done((bf16[2,1,24,2304]{3,2,0,1:T(8,128)(2,1)}, bf16[2,1,24,2304]{3,2,0,1:T(8,128)(2,1)}, u32[]{:S(2)}, u32[]{:S(2)}) %collective-permute-start.35) | collective-permute-done | bytes 221216 | tf_op jit(solution)/shard_map/ppermute | solution.py:85
  245.3 2.2 add_halve.15
  257.0 3.7 %collective-permute-done.39 = bf16[1,1,24,2304]{3,2,1,0:T(8,128)(2,1)} collective-permute-done((bf16[1,1,24,2304]{3,2,1,0:T(8,128)(2,1)}, bf16[1,1,24,2304]{3,2,1,0:T(8,128)(2,1)}, u32[]{:S(2)}, u32[]{:S(2)}) %collective-permute-start.39) | collective-permute-done | bytes 110624 | tf_op jit(solution)/shard_map/ppermute | solution.py:85
  263.3 2.3 collective-permute-start.40
  271.4 5.9 %collective-permute-start.46 = (bf16[24,3328]{1,0:T(8,128)(2,1)}, bf16[24,3328]{1,0:T(8,128)(2,1)}, u32[]{:S(2)}, u32[]{:S(2)}) collective-permute-start(bf16[24,3328]{1,0:T(8,128)(2,1)} %add_convert_fusion.1.refs_0_), channel_id=1, source_target_pairs={{0,24},{1,25},{2,26},{3,27},{4,28},{5,29},{6,30},{7,31},{8,16},{9,... | collective-permute-start | bytes 479240 | tf_op jit(solution)/shard_map/ppermute | solution.py:88
  278.8 4.2 %place_sums.2 = (f32[192,3072]{1,0:T(8,128)}, f32[768,768]{1,0:T(8,128)}) custom-call(s32[26]{0:T(128)} %concatenate.24.meta, bf16[1152,128]{1,0:T(8,128)(2,1)} %add_convert_fusion.refs_0_, bf16[1152,128]{1,0:T(8,128)(2,1)} %collective-permute-done.41.refs_1_, bf16[1152,128]{1,0:T(8,128)(2,1)} %collective-permute-done.42.refs_2_, ...), custom_call_target="tpu_custom_call" | custom-call | tf_op jit(solution)/shard_map/place_sums/pallas_call | solution.py:878
  283.0 2.4 collective-permute-done.45.refs_2_
  287.8 2.9 place_sums.3
  (128 shorter events, 61.2 us)
Async XLA Ops:
  4.5 17.6 %collective-permute-start.2 = (bf16[48,3328]{1,0:T(8,128)(2,1)}, bf16[48,3328]{1,0:T(8,128)(2,1)S(1)}, u32[]{:S(2)}, u32[]{:S(2)}) collective-permute-start(bf16[48,3328]{1,0:T(8,128)(2,1)} %get-tuple-element.137), channel_id=1, source_target_pairs={{0,1},{1,2},{2,3},{3,0},{4,7},{5,4},{6,5},{7,6},{8,9},{9,10},{10,1... | collective-permute-start | bytes 958472 | tf_op jit(solution)/shard_map/ppermute | solution.py:79
  7.6 14.5 %collective-permute-start.3 = (bf16[48,1664]{1,0:T(8,128)(2,1)}, bf16[48,1664]{1,0:T(8,128)(2,1)S(1)}, u32[]{:S(2)}, u32[]{:S(2)}) collective-permute-start(bf16[48,1664]{1,0:T(8,128)(2,1)} %get-tuple-element.138), channel_id=1, source_target_pairs={{0,2},{1,3},{2,0},{3,1},{4,6},{5,7},{6,4},{7,5},{8,10},{9,11},{10,... | collective-permute-start | bytes 479240 | tf_op jit(solution)/shard_map/ppermute | solution.py:82
  10.2 12.0 %collective-permute-start = (bf16[384,128]{1,0:T(8,128)(2,1)}, bf16[384,128]{1,0:T(8,128)(2,1)S(1)}, u32[]{:S(2)}, u32[]{:S(2)}) collective-permute-start(bf16[384,128]{1,0:T(8,128)(2,1)} %get-tuple-element.135), channel_id=1, source_target_pairs={{0,1},{1,0},{2,3},{3,2},{4,5},{5,4},{6,7},{7,6},{8,9},{9,8},{10,11... | collective-permute-start | bytes 294920 | tf_op jit(solution)/shard_map/ppermute | solution.py:85
  22.2 15.4 %collective-permute-start.4 = (bf16[48,4992]{1,0:T(8,128)(2,1)S(1)}, bf16[48,4992]{1,0:T(8,128)(2,1)S(1)}, u32[]{:S(2)}, u32[]{:S(2)}) collective-permute-start(bf16[48,4992]{1,0:T(8,128)(2,1)S(1)} %pad_maximum_fusion.1.refs_9_), channel_id=1, source_target_pairs={{0,8},{1,9},{2,10},{3,11},{4,20},{5,21},{6,22},{7,23},{8,0},{9,1},... | collective-permute-start | bytes 1437704 | tf_op jit(solution)/shard_map/ppermute | solution.py:73
  23.8 11.0 %collective-permute-start.6 = (bf16[768,128]{1,0:T(8,128)(2,1)}, bf16[768,128]{1,0:T(8,128)(2,1)S(1)}, u32[]{:S(2)}, u32[]{:S(2)}) collective-permute-start(bf16[768,128]{1,0:T(8,128)(2,1)} %get-tuple-element.140), channel_id=1, source_target_pairs={{0,1},{1,0},{2,3},{3,2},{4,5},{5,4},{6,7},{7,6},{8,9},{9,8},{10,11... | collective-permute-start | bytes 589832 | tf_op jit(solution)/shard_map/ppermute | solution.py:85
  26.8 10.7 %collective-permute-start.1 = (bf16[2,384,128]{2,1,0:T(8,128)(2,1)S(1)}, bf16[2,384,128]{2,1,0:T(8,128)(2,1)S(1)}, u32[]{:S(2)}, u32[]{:S(2)}) collective-permute-start(bf16[2,384,128]{2,1,0:T(8,128)(2,1)S(1)} %pad_maximum_fusion.4), channel_id=1, source_target_pairs={{0,2},{1,3},{2,0},{3,1},{4,6},{5,7},{6,4},{7,5},{8,10},{9,11},{10,... | collective-permute-start | bytes 589832 | tf_op jit(solution)/shard_map/ppermute | solution.py:85
  39.7 10.9 %collective-permute-start.8 = (bf16[48,4992]{1,0:T(8,128)(2,1)S(1)}, bf16[48,4992]{1,0:T(8,128)(2,1)S(1)}, u32[]{:S(2)}, u32[]{:S(2)}) collective-permute-start(bf16[48,4992]{1,0:T(8,128)(2,1)S(1)} %pad_maximum_fusion.1.refs_9_), channel_id=1, source_target_pairs={{0,4},{1,5},{2,6},{3,7},{4,0},{5,1},{6,2},{7,3},{8,12},{9,13},{10,... | collective-permute-start | bytes 1437704 | tf_op jit(solution)/shard_map/ppermute | solution.py:70
  39.8 13.0 %collective-permute-start.9 = (bf16[48,4992]{1,0:T(8,128)(2,1)S(1)}, bf16[48,4992]{1,0:T(8,128)(2,1)}, u32[]{:S(2)}, u32[]{:S(2)}) collective-permute-start(bf16[48,4992]{1,0:T(8,128)(2,1)S(1)} %collective-permute-done.4.refs_10_), channel_id=1, source_target_pairs={{0,4},{1,5},{2,6},{3,7},{4,0},{5,1},{6,2},{7,3},{8,12},{9,13},{10,... | collective-permute-start | bytes 1437704 | tf_op jit(solution)/shard_map/ppermute | solution.py:70
  40.3 11.9 %collective-permute-start.10 = (bf16[48,4992]{1,0:T(8,128)(2,1)S(1)}, bf16[48,4992]{1,0:T(8,128)(2,1)}, u32[]{:S(2)}, u32[]{:S(2)}) collective-permute-start(bf16[48,4992]{1,0:T(8,128)(2,1)S(1)} %collective-permute-done.5.refs_11_), channel_id=1, source_target_pairs={{0,4},{1,5},{2,6},{3,7},{4,0},{5,1},{6,2},{7,3},{8,12},{9,13},{10,... | collective-permute-start | bytes 1437704 | tf_op jit(solution)/shard_map/ppermute | solution.py:70
  48.4 29.9 %collective-permute-start.15 = (bf16[3,384,128]{2,1,0:T(8,128)(2,1)}, bf16[3,384,128]{2,1,0:T(8,128)(2,1)}, u32[]{:S(2)}, u32[]{:S(2)}) collective-permute-start(bf16[3,384,128]{2,1,0:T(8,128)(2,1)} %pad_maximum_fusion.3.refs_7_), channel_id=1, source_target_pairs={{0,24},{1,25},{2,26},{3,27},{4,28},{5,29},{6,30},{7,31},{8,16},{9,... | collective-permute-start | bytes 884744 | tf_op jit(solution)/shard_map/ppermute | solution.py:88
  50.6 27.7 %collective-permute-start.14 = (bf16[3,384,128]{2,1,0:T(8,128)(2,1)}, bf16[3,384,128]{2,1,0:T(8,128)(2,1)}, u32[]{:S(2)}, u32[]{:S(2)}) collective-permute-start(bf16[3,384,128]{2,1,0:T(8,128)(2,1)} %pad_maximum_fusion.3.refs_7_), channel_id=1, source_target_pairs={{0,16},{1,17},{2,18},{3,19},{4,12},{5,13},{6,14},{7,15},{8,24},{9,... | collective-permute-start | bytes 884744 | tf_op jit(solution)/shard_map/ppermute | solution.py:76
  52.2 26.1 %collective-permute-start.13 = (bf16[3,384,128]{2,1,0:T(8,128)(2,1)}, bf16[3,384,128]{2,1,0:T(8,128)(2,1)}, u32[]{:S(2)}, u32[]{:S(2)}) collective-permute-start(bf16[3,384,128]{2,1,0:T(8,128)(2,1)} %pad_maximum_fusion.3.refs_7_), channel_id=1, source_target_pairs={{0,8},{1,9},{2,10},{3,11},{4,20},{5,21},{6,22},{7,23},{8,0},{9,1},... | collective-permute-start | bytes 884744 | tf_op jit(solution)/shard_map/ppermute | solution.py:73
  52.7 23.6 %collective-permute-start.12 = (bf16[2,768,128]{2,1,0:T(8,128)(2,1)}, bf16[2,768,128]{2,1,0:T(8,128)(2,1)}, u32[]{:S(2)}, u32[]{:S(2)}) collective-permute-start(bf16[2,768,128]{2,1,0:T(8,128)(2,1)} %pad_maximum_fusion.2), channel_id=1, source_target_pairs={{0,2},{1,3},{2,0},{3,1},{4,6},{5,7},{6,4},{7,5},{8,10},{9,11},{10,... | collective-permute-start | bytes 1179656 | tf_op jit(solution)/shard_map/ppermute | solution.py:85
  78.8 28.2 %collective-permute-start.20 = (bf16[3,768,128]{2,1,0:T(8,128)(2,1)}, bf16[3,768,128]{2,1,0:T(8,128)(2,1)}, u32[]{:S(2)}, u32[]{:S(2)}) collective-permute-start(bf16[3,768,128]{2,1,0:T(8,128)(2,1)} %pad_maximum_fusion.refs_7_), channel_id=1, source_target_pairs={{0,24},{1,25},{2,26},{3,27},{4,28},{5,29},{6,30},{7,31},{8,16},{9,... | collective-permute-start | bytes 1769480 | tf_op jit(solution)/shard_map/ppermute | solution.py:88
  80.3 27.7 %collective-permute-start.19 = (bf16[3,768,128]{2,1,0:T(8,128)(2,1)}, bf16[3,768,128]{2,1,0:T(8,128)(2,1)}, u32[]{:S(2)}, u32[]{:S(2)}) collective-permute-start(bf16[3,768,128]{2,1,0:T(8,128)(2,1)} %pad_maximum_fusion.refs_7_), channel_id=1, source_target_pairs={{0,16},{1,17},{2,18},{3,19},{4,12},{5,13},{6,14},{7,15},{8,24},{9,... | collective-permute-start | bytes 1769480 | tf_op jit(solution)/shard_map/ppermute | solution.py:76
  81.8 26.2 %collective-permute-start.18 = (bf16[3,768,128]{2,1,0:T(8,128)(2,1)}, bf16[3,768,128]{2,1,0:T(8,128)(2,1)}, u32[]{:S(2)}, u32[]{:S(2)}) collective-permute-start(bf16[3,768,128]{2,1,0:T(8,128)(2,1)} %pad_maximum_fusion.refs_7_), channel_id=1, source_target_pairs={{0,8},{1,9},{2,10},{3,11},{4,20},{5,21},{6,22},{7,23},{8,0},{9,1},... | collective-permute-start | bytes 1769480 | tf_op jit(solution)/shard_map/ppermute | solution.py:73
  105.5 39.4 %collective-permute-start.21 = (bf16[2,4,384,128]{3,2,1,0:T(8,128)(2,1)}, bf16[2,4,384,128]{3,2,1,0:T(8,128)(2,1)}, u32[]{:S(2)}, u32[]{:S(2)}) collective-permute-start(bf16[2,4,384,128]{3,2,1,0:T(8,128)(2,1)} %get-tuple-element.157), channel_id=1, source_target_pairs={{0,8},{1,9},{2,10},{3,11},{4,20},{5,21},{6,22},{7,23},{8,0},{9,1},... | collective-permute-start | bytes 2359304 | tf_op jit(solution)/shard_map/ppermute | solution.py:73
  145.4 31.3 %collective-permute-start.25 = (bf16[2,4,768,128]{3,2,1,0:T(8,128)(2,1)}, bf16[2,4,768,128]{3,2,1,0:T(8,128)(2,1)}, u32[]{:S(2)}, u32[]{:S(2)}) collective-permute-start(bf16[2,4,768,128]{3,2,1,0:T(8,128)(2,1)} %get-tuple-element.180), channel_id=1, source_target_pairs={{0,8},{1,9},{2,10},{3,11},{4,20},{5,21},{6,22},{7,23},{8,0},{9,1},... | collective-permute-start | bytes 4718600 | tf_op jit(solution)/shard_map/ppermute | solution.py:73
  149.5 27.2 %collective-permute-start.23 = (bf16[1,16,96,128]{3,2,1,0:T(8,128)(2,1)}, bf16[1,16,96,128]{3,2,1,0:T(8,128)(2,1)}, u32[]{:S(2)}, u32[]{:S(2)}) collective-permute-start(bf16[1,16,96,128]{3,2,1,0:T(8,128)(2,1)} %get-tuple-element.164), channel_id=1, source_target_pairs={{0,16},{1,17},{2,18},{3,19},{4,12},{5,13},{6,14},{7,15},{8,24},{9,... | collective-permute-start | bytes 1179656 | tf_op jit(solution)/shard_map/ppermute | solution.py:76
  185.0 25.2 %collective-permute-start.29 = (bf16[1,8,24,2304]{3,2,1,0:T(8,128)(2,1)}, bf16[1,8,24,2304]{3,2,1,0:T(8,128)(2,1)}, u32[]{:S(2)}, u32[]{:S(2)}) collective-permute-start(bf16[1,8,24,2304]{3,2,1,0:T(8,128)(2,1)} %get-tuple-element.189), channel_id=1, source_target_pairs={{0,8},{1,9},{2,10},{3,11},{4,20},{5,21},{6,22},{7,23},{8,0},{9,1},... | collective-permute-start | bytes 2654216 | tf_op jit(solution)/shard_map/ppermute | solution.py:73
  186.5 23.7 %collective-permute-start.28 = (bf16[1,32,96,128]{3,2,1,0:T(8,128)(2,1)}, bf16[1,32,96,128]{3,2,1,0:T(8,128)(2,1)}, u32[]{:S(2)}, u32[]{:S(2)}) collective-permute-start(bf16[1,32,96,128]{3,2,1,0:T(8,128)(2,1)} %get-tuple-element.187), channel_id=1, source_target_pairs={{0,16},{1,17},{2,18},{3,19},{4,12},{5,13},{6,14},{7,15},{8,24},{9,... | collective-permute-start | bytes 2359304 | tf_op jit(solution)/shard_map/ppermute | solution.py:76
  187.1 23.1 %collective-permute-start.26 = (bf16[2,4,96,128]{3,2,1,0:T(8,128)(2,1)}, bf16[2,4,96,128]{3,2,1,0:T(8,128)(2,1)}, u32[]{:S(2)}, u32[]{:S(2)}) collective-permute-start(bf16[2,4,96,128]{3,2,1,0:T(8,128)(2,1)} %get-tuple-element.183), channel_id=1, source_target_pairs={{0,1},{1,0},{2,3},{3,2},{4,5},{5,4},{6,7},{7,6},{8,9},{9,8},{10,11... | collective-permute-start | bytes 589832 | tf_op jit(solution)/shard_map/ppermute | solution.py:85
  214.3 13.3 %collective-permute-start.30 = (bf16[1,4,24,2304]{3,2,1,0:T(8,128)(2,1)}, bf16[1,4,24,2304]{3,2,1,0:T(8,128)(2,1)}, u32[]{:S(2)}, u32[]{:S(2)}) collective-permute-start(bf16[1,4,24,2304]{3,2,1,0:T(8,128)(2,1)} %get-tuple-element.198), channel_id=1, source_target_pairs={{0,16},{1,17},{2,18},{3,19},{4,12},{5,13},{6,14},{7,15},{8,24},{9,... | collective-permute-start | bytes 1327112 | tf_op jit(solution)/shard_map/ppermute | solution.py:76
  214.9 12.6 %collective-permute-start.32 = (bf16[2,8,96,128]{3,2,1,0:T(8,128)(2,1)}, bf16[2,8,96,128]{3,2,1,0:T(8,128)(2,1)}, u32[]{:S(2)}, u32[]{:S(2)}) collective-permute-start(bf16[2,8,96,128]{3,2,1,0:T(8,128)(2,1)} %get-tuple-element.206), channel_id=1, source_target_pairs={{0,1},{1,0},{2,3},{3,2},{4,5},{5,4},{6,7},{7,6},{8,9},{9,8},{10,11... | collective-permute-start | bytes 1179656 | tf_op jit(solution)/shard_map/ppermute | solution.py:85
  215.0 10.6 %collective-permute-start.31 = (bf16[1,4,96,128]{3,2,1,0:T(8,128)(2,1)}, bf16[1,4,96,128]{3,2,1,0:T(8,128)(2,1)}, u32[]{:S(2)}, u32[]{:S(2)}) collective-permute-start(bf16[1,4,96,128]{3,2,1,0:T(8,128)(2,1)} %get-tuple-element.205), channel_id=1, source_target_pairs={{0,2},{1,3},{2,0},{3,1},{4,6},{5,7},{6,4},{7,5},{8,10},{9,11},{10,... | collective-permute-start | bytes 294920 | tf_op jit(solution)/shard_map/ppermute | solution.py:85
  232.7 12.7 %collective-permute-start.34 = (bf16[1,8,24,1024]{3,2,1,0:T(8,128)(2,1)}, bf16[1,8,24,1024]{3,2,1,0:T(8,128)(2,1)}, u32[]{:S(2)}, u32[]{:S(2)}) collective-permute-start(bf16[1,8,24,1024]{3,2,1,0:T(8,128)(2,1)} %get-tuple-element.214), channel_id=1, source_target_pairs={{0,8},{1,9},{2,10},{3,11},{4,20},{5,21},{6,22},{7,23},{8,0},{9,1},... | collective-permute-start | bytes 1179656 | tf_op jit(solution)/shard_map/ppermute | solution.py:73
  234.1 11.2 %collective-permute-start.35 = (bf16[2,1,24,2304]{3,2,0,1:T(8,128)(2,1)}, bf16[2,1,24,2304]{3,2,0,1:T(8,128)(2,1)}, u32[]{:S(2)}, u32[]{:S(2)}) collective-permute-start(bf16[2,1,24,2304]{3,2,0,1:T(8,128)(2,1)} %bitcast.78), channel_id=1, source_target_pairs={{0,1},{1,0},{2,3},{3,2},{4,5},{5,4},{6,7},{7,6},{8,9},{9,8},{10,11... | collective-permute-start | bytes 663560 | tf_op jit(solution)/shard_map/ppermute | solution.py:85
  234.2 14.8 %collective-permute-start.37 = (bf16[1,8,96,128]{3,2,1,0:T(8,128)(2,1)}, bf16[1,8,96,128]{3,2,1,0:T(8,128)(2,1)}, u32[]{:S(2)}, u32[]{:S(2)}) collective-permute-start(bf16[1,8,96,128]{3,2,1,0:T(8,128)(2,1)} %get-tuple-element.212), channel_id=1, source_target_pairs={{0,2},{1,3},{2,0},{3,1},{4,6},{5,7},{6,4},{7,5},{8,10},{9,11},{10,... | collective-permute-start | bytes 589832 | tf_op jit(solution)/shard_map/ppermute | solution.py:85
  250.9 14.7 %collective-permute-start.43 = (bf16[1152,128]{1,0:T(8,128)(2,1)}, bf16[1152,128]{1,0:T(8,128)(2,1)}, u32[]{:S(2)}, u32[]{:S(2)}) collective-permute-start(bf16[1152,128]{1,0:T(8,128)(2,1)} %add_convert_fusion.refs_0_), channel_id=1, source_target_pairs={{0,24},{1,25},{2,26},{3,27},{4,28},{5,29},{6,30},{7,31},{8,16},{9,... | collective-permute-start | bytes 884744 | tf_op jit(solution)/shard_map/ppermute | solution.py:88
  252.4 14.1 %collective-permute-start.42 = (bf16[1152,128]{1,0:T(8,128)(2,1)}, bf16[1152,128]{1,0:T(8,128)(2,1)}, u32[]{:S(2)}, u32[]{:S(2)}) collective-permute-start(bf16[1152,128]{1,0:T(8,128)(2,1)} %add_convert_fusion.refs_0_), channel_id=1, source_target_pairs={{0,16},{1,17},{2,18},{3,19},{4,12},{5,13},{6,14},{7,15},{8,24},{9,... | collective-permute-start | bytes 884744 | tf_op jit(solution)/shard_map/ppermute | solution.py:76
  253.7 13.4 %collective-permute-start.41 = (bf16[1152,128]{1,0:T(8,128)(2,1)}, bf16[1152,128]{1,0:T(8,128)(2,1)}, u32[]{:S(2)}, u32[]{:S(2)}) collective-permute-start(bf16[1152,128]{1,0:T(8,128)(2,1)} %add_convert_fusion.refs_0_), channel_id=1, source_target_pairs={{0,8},{1,9},{2,10},{3,11},{4,20},{5,21},{6,22},{7,23},{8,0},{9,1},... | collective-permute-start | bytes 884744 | tf_op jit(solution)/shard_map/ppermute | solution.py:73
  271.4 11.6 %collective-permute-start.46 = (bf16[24,3328]{1,0:T(8,128)(2,1)}, bf16[24,3328]{1,0:T(8,128)(2,1)}, u32[]{:S(2)}, u32[]{:S(2)}) collective-permute-start(bf16[24,3328]{1,0:T(8,128)(2,1)} %add_convert_fusion.1.refs_0_), channel_id=1, source_target_pairs={{0,24},{1,25},{2,26},{3,27},{4,28},{5,29},{6,30},{7,31},{8,16},{9,... | collective-permute-start | bytes 479240 | tf_op jit(solution)/shard_map/ppermute | solution.py:88
  (30 other events, 253.2 us)
where the time goes:
time: 292 us; the launch traced here: 291 us
  Pallas kernels  174 us (60%)
  starting transfers between devices  56.3 us (19%)
  waiting for transfers between devices  48 us (16%)
  other arithmetic  9.67 us (3%)
    pallas_call x2, Pallas kernels, mlp(): pl.pallas_call(functools.partial(mlp_body, ng, go, first), grid_spec=pltp...  58 us
    pallas_call x9, Pallas kernels, halve(): pl.pallas_call(functools.partial(halve_body, tuple(((p, len(ks), ks[0].sh...  25.4 us
    pallas_call x1, Pallas kernels, k1(): pl.pallas_call(k1_body, grid_spec=pltpu.PrefetchScalarGridSpec(num_scalar...  23.5 us
    ppermute x12, waiting for transfers between devices, z_flip(): return lax.ppermute(a, ALL, self.table(lambda d, z: (d, z ^ bit)))  21.1 us
    pallas_call x1, Pallas kernels, back_late(): pl.pallas_call(back_late_body, grid_spec=pltpu.PrefetchScalarGridSpec(num...  19.3 us
    pallas_call x1, Pallas kernels, back_early(): pl.pallas_call(back_early_body, grid=(t // BLOCK,), in_specs=[blk(d), blk...  15.9 us
    ppermute x12, starting transfers between devices, z_flip(): return lax.ppermute(a, ALL, self.table(lambda d, z: (d, z ^ bit)))  15.6 us
    pallas_call x2, Pallas kernels, grads(): pl.pallas_call(body, grid_spec=pltpu.PrefetchScalarGridSpec(num_scalar_pr...  15.3 us
  transfers between devices with their start and end apart: 55, of which 20 were waited for; matrix products, arithmetic and copies ran while one was open for 3% of the time, Pallas kernels for 54%

commit v1 on v0

--- a/solution.py
+++ b/solution.py
@@ -113,11 +113,10 @@
 
 def gather_mixed(routes, near, far, early, late):
     block = jnp.concatenate([routes.z_near(near), routes.z_far(far)], axis=1)
-    block = tie(block, early)
     one = routes.first(block)
     two = routes.second(block)
-    own = [block, one, two, routes.second(tie(one, *late))]
-    return own + [routes.core(b) for b in own]
+    own = [block, one, two, routes.second(tie(one, two, *early))]
+    return own + [routes.core(b) for b in own[:3]] + [routes.core(tie(own[3], late))]
 
 
 def mixed_copies(meta, shard, blocks, w, sems):
@@ -138,7 +137,7 @@
     return [pltpu.make_async_copy(s, d, sems.at[i]) for i, (s, d) in enumerate(out)]
 
 
-PARTS = ((1, 0), (2, 1))
+PARTS = ((3, 0),)
 
 
 def piece_rows(ng, rows, d):
@@ -149,7 +148,7 @@
     w_qkv, w_out = refs[0:2]
     vecs, b1, f1, f2 = refs[2:8], refs[8], refs[9], refs[10]
     mixed, near, far = refs[11:14]
-    outs, sems = refs[14:16], refs[16]
+    outs, sems = refs[14 : 14 + len(PARTS)], refs[14 + len(PARTS)]
     c, x, y = pos[0] & 1, (pos[0] >> 1) & 1, (pos[0] >> 2) & 1
     p = 2 * y + x
     d = w_out.shape[1]
@@ -195,7 +194,7 @@
     return pl.pallas_call(
         pack_body,
         in_specs=[pl.BlockSpec(memory_space=pltpu.SMEM)] + [WHOLE] * 9 + [ANY] * 2,
-        out_specs=[WHOLE] * 5,
+        out_specs=[WHOLE] * (3 + len(PARTS)),
         scratch_shapes=[pltpu.SemaphoreType.DMA((count,))],
         out_shape=[sd((rows, wide), BF16), sd((rows // 4, wide), BF16), sd((rows // 4, wide // 2), BF16)]
         + [sd((piece_rows(ng, rows, d), 128), BF16) for ng, _ in PARTS],
@@ -415,12 +414,11 @@
     rr = pl.ds(pl.multiple_of(b * BLOCK, BLOCK), BLOCK)
     a = a2[rr, :]
     gr = g[rr, :]
-    per = 2 // ng
+    lane = pl.ds(pl.multiple_of(c * (b1.shape[1] // 2) + go * 128, 128), n)
+    bias = jnp.concatenate([b1[zz : zz + 1, lane] for zz in range(4)], axis=1)
     for k in range(2 * ng):
         cols = slice(k * 256, (k + 1) * 256)
-        lane = pl.ds(pl.multiple_of(c * (b1.shape[1] // 2) + go * 128, 128), n)
-        bias = jnp.concatenate([b1[zz : zz + 1, lane] for zz in range(k * per, (k + 1) * per)], axis=1)
-        u, s = gelu_and_slope(nn(a, w1[:, cols]) + bias)
+        u, s = gelu_and_slope(nn(a, w1[:, cols]) + bias[:, cols])
         u_s[rr, cols] = u.astype(BF16)
         dz = (nt(gr, w2[cols, :]) * s).astype(BF16)
         dz_s[rr, cols] = dz
@@ -675,10 +673,11 @@
     split(meta, stage, send_o, keep_o, pl.multiple_of(s * d, 128), d)
 
 
-def grads_late_body(meta, a1, dq, acc, dba, dbb, send_o, keep_o, stage):
+def grads_late_body(meta, a1, dq, acc, *refs):
     d = a1.shape[1]
     c = meta[I_C]
     rows = d // 4
+    dbs, (send_o, keep_o, stage) = refs[: len(PARTS)], refs[len(PARTS) :]
     stage[...] = tn(a1[...], dq[...]).astype(BF16)
     split(meta, stage, send_o, keep_o, 0, d)
     stage[:, 0:128] = acc[...].T.astype(BF16)
@@ -686,7 +685,7 @@
     for zz in range(4):
         parts = []
         for hh in range(2):
-            for src, (ng, go) in ((dba, PARTS[0]), (dbb, PARTS[1])):
+            for src, (ng, go) in zip(dbs, PARTS):
                 for k in range(ng):
                     at = (zz * ng + k) * 128
                     parts.append(jnp.where(hh == c, src[0:1, at : at + 128], 0.0))
@@ -915,75 +914,53 @@
     meta = scalars(chip_ids)
 
     vecs = (ln1_gain, ln1_bias, b_out, ln2_gain, ln2_bias, b_fc2)
-    mixed, near, far, ha, hb = pack(pos, w_qkv, w_out, vecs, b_fc1, w_fc1, w_fc2)
-
-    def planes(own, other):
-        return routes.z_flip(jnp.stack([own, other]), 2)
-
-    join = lambda other, two: jnp.concatenate([other[None], two], axis=0)
-    mate_a, mate_b = routes.z_flip(ha, 1), routes.z_flip(hb, 1)
-    two_a = planes(ha, mate_a)
-    p_mixed = gather_mixed(routes, near, far, mate_a, (two_a, mate_b))
-    block_a = join(mate_a, two_a)
-    p_a = around(routes, block_a)
-    two_b = planes(hb, tie(mate_b, block_a))
-    qkv, prob, inv, o, x1, a2, a1, gp, w, vec, b1, dbf = k1(meta, tokens, cotangent, tie(mixed, block_a), p_mixed, ff)
-    block_b = join(mate_b, tie(two_b, a2))
-    p_b = around(routes, block_b)
-
-    swap = lax.optimization_barrier((a2, gp, block_b, *p_a))
+    mixed, near, far, hid = pack(pos, w_qkv, w_out, vecs, b_fc1, w_fc1, w_fc2)
+
+    mate, far_h = routes.z_flip(hid, 1), routes.z_flip(hid, 2)
+    last_h = routes.z_flip(far_h, 1)
+    p_mixed = gather_mixed(routes, near, far, (mate, far_h), last_h)
+    block = jnp.stack([mate, far_h, last_h])
+    p_hid = [block, routes.first(block), routes.second(block)]
+    qkv, prob, inv, o, x1, a2, a1, gp, w, vec, b1, dbf = k1(
+        meta, tokens, cotangent, tie(mixed, block), p_mixed, ff)
+    swap = lax.optimization_barrier((a2, gp, *p_hid[1:]))
+    p_hid.append(routes.second(swap[2]))
     a2p, gpp = routes.core(swap[0]), routes.core(swap[1])
-    *part, sa, ka, dba = mlp(0, meta, a2, a2p, gp, gpp, b1, w_fc1, w_fc2, p_a)
-    got_a = routes.first(sa)
-    yo, do, yp, dp, sb, kb, dbb = mlp(1, meta, a2, a2p, gp, gpp, b1, w_fc1, w_fc2, p_b, part)
-
-    def view(a, pre, rest):
-        return a.reshape((pre, 2) + rest)
-
-    tall = lambda a: (4 * a.shape[2] // 96, 96, 128)
-    flat = lambda a: (a.shape[2] // 96, 96, 128)
-    size_a, size_b = tall(sa), tall(sb)
-    s_a, k_a = halve(meta, (I_B2, view(ka, 1, size_a), view(got_a, 1, size_a)))
-    dp, yp, sb = lax.optimization_barrier((dp, yp, sb, got_a))[:3]
-    dq = routes.core(dp)
-    yq = routes.core(yp)
-    got_a, got_b = routes.second(s_a), routes.first(sb)
-    dx1, dl, dqe, acc = back_early(tie(gp, s_a), do, dq, x1, prob, inv, o, qkv, w, vec, dbf)
+    yo, do, yp, dp, sh, kh, db = mlp(0, meta, a2, a2p, gp, gpp, b1, w_fc1, w_fc2, p_hid)
+
+    cut = lambda a, pre, loops: a.reshape(pre, 2, loops, 96, 128)
+    nh = sh.shape[2] // 96
+    yq, dq = routes.core(yp), routes.core(dp)
+    got_h = routes.first(sh)
+    dx1, dl, dqe, acc = back_early(gp, do, dq, x1, prob, inv, o, qkv, w, vec, dbf)
     early = 3 * 64 * EARLY + d
     late = 4 * d - early + EXT
-    sm, km = grads(grads_early_body, early // d, early, meta, tie(a1, yq), dqe, o, dl, cost=SHORT)
-    got_m = routes.core(tie(sm, got_a, got_b))
-
-    lo_a, lo_b = (2, 2) + flat(sa), (2, 2) + flat(sb)
-    hi_a, hi_b = (1,) + lo_a[1:], (1,) + lo_b[1:]
-    s_a, k_a, s_b, k_b = halve(meta, (I_Z + 4, k_a.reshape(lo_a), tie(got_a, sm).reshape(lo_a)),
-                               (I_B2, view(kb, 1, size_b), view(tie(got_b, sm), 1, size_b)))
-    got_a, got_b = routes.z_flip(s_a, 1), routes.second(s_b)
+    sm, km = grads(grads_early_body, early // d, early, meta, a1, dqe, o, dl, cost=SHORT)
+    got_m = routes.core(tie(sm, got_h))
+    s_h, k_h = halve(meta, (I_B2, cut(kh, 1, 4 * nh), cut(tie(got_h, sm), 1, 4 * nh)))
+    got_h = routes.second(s_h)
     chunk = lambda a, pre, loops: a.reshape(pre, 2, loops, d // 32, a.shape[-1])
-    s_m, k_m = halve(meta, (I_B1, chunk(km, 1, 8), chunk(tie(got_m, s_b), 1, 8)))
+    s_m, k_m = halve(meta, (I_B1, chunk(km, 1, 8), chunk(tie(got_m, s_h), 1, 8)))
     got_m = routes.first(s_m)
-    gt, dql, acc = back_late(meta, tokens, tie(dx1, s_m), dl, dqe, prob, inv, o, qkv, w, vec, acc)
-
-    s_a, k_a, s_b, k_b, s_m, k_m = halve(
-        meta, (I_Z + 5, k_a.reshape(hi_a), tie(got_a, acc).reshape(hi_a)),
-        (I_Z + 4, k_b.reshape(lo_b), tie(got_b, acc).reshape(lo_b)),
+    gt, dql, acc = back_late(meta, tokens, tie(dx1, s_m, yq), dl, dqe, prob, inv, o, qkv, w, vec, acc)
+
+    s_h, k_h, s_m, k_m = halve(
+        meta, (I_Z + 4, cut(k_h, 2, nh), cut(tie(got_h, acc), 2, nh)),
         (I_B2, chunk(k_m, 1, 4), chunk(tie(got_m, acc), 1, 4)))
-    got_m = routes.second(s_m)
-    got_a, got_b = routes.z_flip(s_a, 2), routes.z_flip(s_b, 1)
-    sl, kl = grads(grads_late_body, 1, late, meta, tie(a1, s_m), dql, acc, dba, dbb)
-    joint = lambda a, b: jnp.concatenate([a.reshape(-1, 128), b.reshape(-1, 128)], axis=0)
-    got_l = routes.core(tie(sl, got_m, got_a, got_b))
-    s_m, k_m, s_b, k_b = halve(
+    got_m, got_h = routes.second(s_m), routes.z_flip(s_h, 1)
+    sl, kl = grads(grads_late_body, 1, late, meta, tie(a1, s_m), dql, acc, db)
+    got_l = routes.core(tie(sl, got_m, got_h))
+    s_m, k_m, s_h, k_h = halve(
         meta, (I_Z + 4, chunk(k_m, 2, 1), chunk(tie(got_m, sl), 2, 1)),
-        (I_Z + 5, k_b.reshape(hi_b), tie(got_b, sl).reshape(hi_b)))
-    got_m, got_b = routes.z_flip(s_m, 1), routes.z_flip(s_b, 2)
-    s_l, k_l = halve(meta, (I_B1, chunk(kl, 1, 8), chunk(tie(got_l, s_b), 1, 8)))
+        (I_Z + 5, cut(k_h, 1, nh), cut(tie(got_h, sl), 1, nh)))
+    got_m, got_h = routes.z_flip(s_m, 1), routes.z_flip(s_h, 2)
+    s_l, k_l = halve(meta, (I_B1, chunk(kl, 1, 8), chunk(tie(got_l, s_h), 1, 8)))
     got_l = routes.first(s_l)
     layer_out = layer_output(meta, yo, yq, x1, tie(vec, s_l))
     s_l, k_l, s_m, k_m = halve(meta, (I_B2, chunk(k_l, 1, 4), chunk(tie(got_l, layer_out), 1, 4)),
                                (I_Z + 5, chunk(k_m, 1, 1), chunk(tie(got_m, layer_out), 1, 1)))
     got_l, got_m = routes.second(s_l), routes.z_flip(s_m, 2)
-    piece = total(routes, joint(k_a, k_b), joint(got_a, tie(got_b, s_l)))
+    piece = total(routes, k_h.reshape(-1, 128), tie(got_h, s_l).reshape(-1, 128))
     near_by = around(routes, piece)
     s_l, k_l = halve(meta, (I_Z + 4, chunk(k_l, 2, 1), chunk(tie(got_l, piece), 2, 1)))
     s_l, k_l = halve(meta, (I_Z + 5, chunk(k_l, 1, 1), chunk(tie(routes.z_flip(s_l, 1), got_m), 1, 1)))

time: 292 us -> 285 us (0.976)
  waiting for transfers between devices: 48 us -> 72.9 us
  starting transfers between devices: 56.3 us -> 41.2 us
  Pallas kernels: 174 us -> 160 us
  other arithmetic: 9.67 us -> 6.3 us
    ppermute x12 -> x9, waiting for transfers between devices: 21.1 us -> 37.7 us  [z_flip(): return lax.ppermute(a, ALL, self.table(lambda d, z: (d, z ^ bit)))]
    pallas_call x2 -> x1, Pallas kernels: 58 us -> 46.2 us  [mlp(): pl.pallas_call(functools.partial(mlp_body, ng, go, first), grid_spec=pltp...]
    ppermute x1, waiting for transfers between devices: 0.01 us -> 8.13 us  [z_near(): lax.ppermute(a, ALL, self.table(lambda d, z: (d, z + (1 if d % 2 == 0 els...]
    ppermute x1, waiting for transfers between devices: 11.8 us -> 3.74 us  [z_far(): return lax.ppermute(a, ALL, self.table(lambda d, z: (d, z + 2)))]
    ppermute x10 -> x9, waiting for transfers between devices: 10.2 us -> 17.4 us  [second(): lax.ppermute(a, ALL, self.table(lambda d, z: (d ^ (4 if d % 2 == 0 else 2...]
    ppermute x4 -> x2, starting transfers between devices: 10.3 us -> 3.46 us  [diagonal(): return lax.ppermute(a, ALL, self.table(lambda d, z: (d ^ 6, z)))]
    ppermute x12 -> x9, starting transfers between devices: 15.6 us -> 9.75 us  [z_flip(): return lax.ppermute(a, ALL, self.table(lambda d, z: (d, z ^ bit)))]
    ppermute x9 -> x7, starting transfers between devices: 10.7 us -> 6.9 us  [first(): lax.ppermute(a, ALL, self.table(lambda d, z: (d ^ (2 if d % 2 == 0 else 4...]
  transfers between devices with their start and end apart: 55 -> 47, of which waited for: 20 -> 22; matrix products, arithmetic and copies ran while one was open for 3% -> 2% of each run, Pallas kernels for 54% -> 35%
where the time goes in v1:
time: 285 us; the launch traced here: 284 us
  Pallas kernels  160 us (56%)
  waiting for transfers between devices  72.9 us (26%)
  starting transfers between devices  41.2 us (14%)
  other arithmetic  6.3 us (2%)
    pallas_call x1, Pallas kernels, mlp(): pl.pallas_call(functools.partial(mlp_body, ng, go, first), grid_spec=pltp...  46.2 us
    ppermute x9, waiting for transfers between devices, z_flip(): return lax.ppermute(a, ALL, self.table(lambda d, z: (d, z ^ bit)))  37.7 us
    pallas_call x8, Pallas kernels, halve(): pl.pallas_call(functools.partial(halve_body, tuple(((p, len(ks), ks[0].sh...  24 us
    pallas_call x1, Pallas kernels, k1(): pl.pallas_call(k1_body, grid_spec=pltpu.PrefetchScalarGridSpec(num_scalar...  23.6 us
    pallas_call x1, Pallas kernels, back_late(): pl.pallas_call(back_late_body, grid_spec=pltpu.PrefetchScalarGridSpec(num...  19 us
    ppermute x9, waiting for transfers between devices, second(): lax.ppermute(a, ALL, self.table(lambda d, z: (d ^ (4 if d % 2 == 0 else 2...  17.4 us
    pallas_call x1, Pallas kernels, back_early(): pl.pallas_call(back_early_body, grid=(t // BLOCK,), in_specs=[blk(d), blk...  16.1 us
    pallas_call x2, Pallas kernels, grads(): pl.pallas_call(body, grid_spec=pltpu.PrefetchScalarGridSpec(num_scalar_pr...  15.3 us
  transfers between devices with their start and end apart: 47, of which 22 were waited for; matrix products, arithmetic and copies ran while one was open for 2% of the time, Pallas kernels for 35%

profile of v1, /device:TPU:0, one launch (start us, length us, event | category | flops | bytes accessed | tf_op | source)
XLA Modules:
  0.0 284.1 jit_solution(8091401060242522656)
XLA Ops:
  0.7 3.9 %pack.1 = (bf16[192,3328]{1,0:T(8,128)(2,1)}, bf16[48,3328]{1,0:T(8,128)(2,1)}, bf16[48,1664]{1,0:T(8,128)(2,1)}, bf16[1152,128]{1,0:T(8,128)(2,1)}) custom-call(s32[1]{0:T(128)} %bitcast.9.pos, bf16[192,2304]{1,0:T(8,128)(2,1)} %refs_0_.3, bf16[192,768]{1,0:T(8,128)(2,1)} %refs_1_.3, bf16[192]{0:T(256)(128)(2,1)} %refs_2_.3, bf16[192]{0:T(256)(128)(2,1)} %refs_3_.3, ...), custom_call_target="tpu_custom_call" | custom-call | tf_op jit(solution)/shard_map/pack/pallas_call | solution.py:194
  4.5 3.1 %collective-permute-start.3 = (bf16[48,3328]{1,0:T(8,128)(2,1)}, bf16[48,3328]{1,0:T(8,128)(2,1)S(1)}, u32[]{:S(2)}, u32[]{:S(2)}) collective-permute-start(bf16[48,3328]{1,0:T(8,128)(2,1)} %get-tuple-element.115), channel_id=1, source_target_pairs={{0,1},{1,2},{2,3},{3,0},{4,7},{5,4},{6,5},{7,6},{8,9},{9,10},{10,1... | collective-permute-start | bytes 958472 | tf_op jit(solution)/shard_map/ppermute | solution.py:79
  7.6 2.6 collective-permute-start.4
  10.2 8.1 %collective-permute-done.3 = bf16[48,3328]{1,0:T(8,128)(2,1)S(1)} collective-permute-done((bf16[48,3328]{1,0:T(8,128)(2,1)}, bf16[48,3328]{1,0:T(8,128)(2,1)S(1)}, u32[]{:S(2)}, u32[]{:S(2)}) %collective-permute-start.3) | collective-permute-done | bytes 319520 | tf_op jit(solution)/shard_map/ppermute | solution.py:79
  18.4 3.7 %collective-permute-done.4 = bf16[48,1664]{1,0:T(8,128)(2,1)S(1)} collective-permute-done((bf16[48,1664]{1,0:T(8,128)(2,1)}, bf16[48,1664]{1,0:T(8,128)(2,1)S(1)}, u32[]{:S(2)}, u32[]{:S(2)}) %collective-permute-start.4) | collective-permute-done | bytes 159776 | tf_op jit(solution)/shard_map/ppermute | solution.py:82
  25.3 2.2 collective-permute-start.1
  27.5 3.1 %collective-permute-start = (bf16[1152,128]{1,0:T(8,128)(2,1)}, bf16[1152,128]{1,0:T(8,128)(2,1)S(1)}, u32[]{:S(2)}, u32[]{:S(2)}) collective-permute-start(bf16[1152,128]{1,0:T(8,128)(2,1)} %get-tuple-element.113), channel_id=1, source_target_pairs={{0,1},{1,0},{2,3},{3,2},{4,5},{5,4},{6,7},{7,6},{8,9},{9,8},{10,11... | collective-permute-start | bytes 884744 | tf_op jit(solution)/shard_map/ppermute | solution.py:85
  31.5 8.7 %collective-permute-done.1 = bf16[1152,128]{1,0:T(8,128)(2,1)S(1)} collective-permute-done((bf16[1152,128]{1,0:T(8,128)(2,1)}, bf16[1152,128]{1,0:T(8,128)(2,1)S(1)}, u32[]{:S(2)}, u32[]{:S(2)}) %collective-permute-start.1) | collective-permute-done | bytes 294944 | tf_op jit(solution)/shard_map/ppermute | solution.py:85
  44.4 5.3 %collective-permute-done.2 = bf16[1152,128]{1,0:T(8,128)(2,1)S(1)} collective-permute-done((bf16[1152,128]{1,0:T(8,128)(2,1)S(1)}, bf16[1152,128]{1,0:T(8,128)(2,1)S(1)}, u32[]{:S(2)}, u32[]{:S(2)}) %collective-permute-start.2) | collective-permute-done | bytes 294944 | tf_op jit(solution)/shard_map/ppermute | solution.py:85
  54.3 23.6 %norm_qkv_attend.1 = (bf16[1024,2304]{1,0:T(8,128)(2,1)}, bf16[4,12,256,256]{3,2,1,0:T(8,128)(2,1)}, f32[1024,768]{1,0:T(8,128)}, bf16[1024,768]{1,0:T(8,128)(2,...) custom-call(s32[26]{0:T(128)} %concatenate.12.meta, ...), custom_call_target="tpu_custom_call" | custom-call | flops 6039797760 | bytes 41943040 | tf_op jit(solution)/shard_map/norm_qkv_attend/pallas_call | solution.py:306
  79.9 11.8 %collective-permute-done.16.refs_10_ = bf16[3,1152,128]{2,1,0:T(8,128)(2,1)} collective-permute-done((bf16[3,1152,128]{2,1,0:T(8,128)(2,1)}, bf16[3,1152,128]{2,1,0:T(8,128)(2,1)}, u32[]{:S(2)}, u32[]{:S(2)}) %collective-permute-start.16) | collective-permute-done | bytes 884768 | tf_op jit(solution)/shard_map/ppermute | solution.py:76
  91.8 46.2 %hidden_first.1 = (bf16[1024,768]{1,0:T(8,128)(2,1)}, bf16[1024,768]{1,0:T(8,128)(2,1)}, bf16[1024,768]{1,0:T(8,128)(2,1)}, bf16[1024,768]{1,0:T(8,128)(2,1)}, b...) custom-call(s32[26]{0:T(128)} %concatenate.12.meta, ...), custom_call_target="tpu_custom_call" | custom-call | flops 28991029248 | bytes 31457280 | tf_op jit(solution)/shard_map/hidden_first/pallas_call | solution.py:481
  138.8 3.7 %collective-permute-done.19.da_p = bf16[1024,768]{1,0:T(8,128)(2,1)} collective-permute-done((bf16[1024,768]{1,0:T(8,128)(2,1)}, bf16[1024,768]{1,0:T(8,128)(2,1)}, u32[]{:S(2)}, u32[]{:S(2)}) %collective-permute-start.19) | collective-permute-done | bytes 1572896 | tf_op jit(solution)/shard_map/ppermute | solution.py:70
  142.6 16.1 %attend_back_early.1 = (f32[1024,768]{1,0:T(8,128)}, bf16[1024,768]{1,0:T(8,128)(2,1)}, bf16[1024,1536]{1,0:T(8,128)(2,1)}, f32[128,768]{1,0:T(8,128)}) custom-call(bf16[1024,768]{1,0:T(8,128)(2,1)} %get-tuple-element.122.refs_2_.gp, bf16[1024,768]{1,0:T(8,128)(2,1)} %get-tuple-element.132.da_o, bf16[1024,768]{1,0:T(8,128)(2,1)} %collective-permute-done.19.da_p, ...), custom_call_target="tpu_custom_call" | custom-call | flops 4831838208 | bytes 25165824 | tf_op jit(solution)/shard_map/attend_back_early/pallas_call | solution.py:556
  158.6 9.9 %weight_grads.2 = (bf16[2,2,4,24,2304]{4,3,2,1,0:T(8,128)(2,1)}, bf16[2,2,4,24,2304]{4,3,2,1,0:T(8,128)(2,1)}) custom-call(s32[26]{0:T(128)} %concatenate.12.meta, bf16[1024,768]{1,0:T(8,128)(2,1)} %get-tuple-element.158.a1, bf16[1024,1536]{1,0:T(8,128)(2,1)} %get-tuple-element.140.dq.refs_6_, bf16[1024,768]{1,0:T(8,128)(2,1)} %get-tuple-element.136.o.refs_9_, ...), custom_call_target="tpu_custom_call" | custom-call | flops 1 | bytes 1 | tf_op jit(solution)/shard_map/weight_grads/pallas_call | solution.py:705
  169.1 4.9 %add_halve.8 = (bf16[1,48,96,128]{3,2,1,0:T(8,128)(2,1)}, bf16[1,48,96,128]{3,2,1,0:T(8,128)(2,1)}) custom-call(s32[26]{0:T(128)} %concatenate.12.meta, bf16[1,2,48,96,128]{4,3,2,1,0:T(8,128)(2,1)} %bitcast.42, bf16[1,2,48,96,128]{4,3,2,1,0:T(8,128)(2,1)} %bitcast.14.refs_1_), custom_call_target="tpu_custom_call" | custom-call | flops 1179648 | bytes 7077888 | tf_op jit(solution)/shard_map/add_halve/pallas_call | solution.py:802
  175.5 3.7 %add_halve.9 = (bf16[1,8,24,2304]{3,2,1,0:T(8,128)(2,1)}, bf16[1,8,24,2304]{3,2,1,0:T(8,128)(2,1)}) custom-call(s32[26]{0:T(128)} %concatenate.12.meta, bf16[1,2,8,24,2304]{4,3,2,1,0:T(8,128)(2,1)} %bitcast.43, bf16[1,2,8,24,2304]{4,3,2,1,0:T(8,128)(2,1)} %bitcast.17.refs_1_), custom_call_target="tpu_custom_call" | custom-call | flops 884736 | bytes 5308416 | tf_op jit(solution)/shard_map/add_halve/pallas_call | solution.py:802
  180.5 19.0 %attend_back_late.1 = (f32[1024,768]{1,0:T(8,128)}, bf16[1024,768]{1,0:T(8,128)(2,1)}, f32[128,768]{1,0:T(8,128)}) custom-call(s32[26]{0:T(128)} %concatenate.12.meta, bf16[1024,768]{1,0:T(8,128)(2,1)} %refs_3_.5, bf16[1024,768]{1,0:T(8,128)(2,1)} %refs_3_.5, bf16[1024,768]{1,0:T(8,128)(2,1)} %refs_3_.5, bf16[1024,768]{1,0:T(8,128)(2,1)} %refs_3_.5, ...), custom_call_target="tpu_custom_call" | custom-call | flops 6039797760 | bytes 20971520 | tf_op jit(solution)/shard_map/attend_back_late/pallas_call | solution.py:629
  199.5 4.2 %add_halve.10 = (bf16[2,12,96,128]{3,2,1,0:T(8,128)(2,1)}, bf16[2,12,96,128]{3,2,1,0:T(8,128)(2,1)}, bf16[1,4,24,2304]{3,2,1,0:T(8,128)(2,1)}, bf16[1,4,24,2304]{3,2,1,0:T(8,128)(2,1)}) custom-call(s32[26]{0:T(128)} %concatenate.12.meta, bf16[2,2,12,96,128]{4,3,2,1,0:T(8,128)(2,1)} %bitcast.44, bf16[2,2,12,96,128]{4,3,2,1,0:T(8,128)(2,1)} %bitcast.18.refs_1_, ...), custom_call_target="tpu_custom_call" | custom-call | flops 1032192 | bytes 6193152 | tf_op jit(solution)/shard_map/add_halve/pallas_call | solution.py:802
  205.4 5.3 %weight_grads.3 = (bf16[2,2,4,24,1024]{4,3,2,1,0:T(8,128)(2,1)}, bf16[2,2,4,24,1024]{4,3,2,1,0:T(8,128)(2,1)}) custom-call(s32[26]{0:T(128)} %concatenate.12.meta, bf16[1024,768]{1,0:T(8,128)(2,1)} %get-tuple-element.158.a1, bf16[1024,768]{1,0:T(8,128)(2,1)} %get-tuple-element.159.dq, f32[128,768]{1,0:T(8,128)} %get-tuple-element.153.acc, ...), custom_call_target="tpu_custom_call" | custom-call | flops 1207959552 | bytes 12582912 | tf_op jit(solution)/shard_map/weight_grads/pallas_call | solution.py:705
  212.6 6.9 %collective-permute-done.24 = bf16[2,12,96,128]{3,2,1,0:T(8,128)(2,1)} collective-permute-done((bf16[2,12,96,128]{3,2,1,0:T(8,128)(2,1)}, bf16[2,12,96,128]{3,2,1,0:T(8,128)(2,1)}, u32[]{:S(2)}, u32[]{:S(2)}) %collective-permute-start.24) | collective-permute-done | bytes 589856 | tf_op jit(solution)/shard_map/ppermute | solution.py:85
  219.6 2.9 %add_halve.11 = (bf16[2,1,24,2304]{3,2,1,0:T(8,128)(2,1)}, bf16[2,1,24,2304]{3,2,1,0:T(8,128)(2,1)}, bf16[1,12,96,128]{3,2,1,0:T(8,128)(2,1)}, bf16[1,12,96,128]{3,2,1,0:T(8,128)(2,1)}) custom-call(s32[26]{0:T(128)} %concatenate.12.meta, bf16[2,2,1,24,2304]{4,3,2,1,0:T(8,128)(2,1)} %bitcast.48, bf16[2,2,1,24,2304]{4,3,2,1,0:T(8,128)(2,1)} %bitcast.23.refs_1_, ...), custom_call_target="tpu_custom_call" | custom-call | flops 516096 | bytes 3096576 | tf_op jit(solution)/shard_map/add_halve/pallas_call | solution.py:802
  222.5 2.5 add_halve.12
  228.0 5.4 %layer_out.1 = bf16[1024,768]{1,0:T(8,128)(2,1)} custom-call(s32[26]{0:T(128)} %concatenate.12.meta, bf16[1024,768]{1,0:T(8,128)(2,1)} %get-tuple-element.125.ya, bf16[1024,768]{1,0:T(8,128)(2,1)} %collective-permute-done.17.yb, f32[1024,768]{1,0:T(8,128)} %get-tuple-element.127.x1_r.x1, f32[16,768]{1,0:T(8,128)} %get-tuple-element.172.vec.refs_12_), custom_call_target="tpu_custom_call" | custom-call | flops 3145728 | bytes 8388608 | tf_op jit(solution)/shard_map/layer_out/pallas_call | solution.py:756
  233.3 5.2 %collective-permute-done.27 = bf16[2,1,24,2304]{3,2,0,1:T(8,128)(2,1)} collective-permute-done((bf16[2,1,24,2304]{3,2,0,1:T(8,128)(2,1)}, bf16[2,1,24,2304]{3,2,0,1:T(8,128)(2,1)}, u32[]{:S(2)}, u32[]{:S(2)}) %collective-permute-start.27) | collective-permute-done | bytes 221216 | tf_op jit(solution)/shard_map/ppermute | solution.py:85
  238.6 2.4 add_halve.13
  252.0 4.2 %collective-permute-done.31 = bf16[1,1,24,2304]{3,2,1,0:T(8,128)(2,1)} collective-permute-done((bf16[1,1,24,2304]{3,2,1,0:T(8,128)(2,1)}, bf16[1,1,24,2304]{3,2,1,0:T(8,128)(2,1)}, u32[]{:S(2)}, u32[]{:S(2)}) %collective-permute-start.31) | collective-permute-done | bytes 110624 | tf_op jit(solution)/shard_map/ppermute | solution.py:85
  261.3 3.3 %collective-permute-done.32 = bf16[1,1,24,1024]{3,2,1,0:T(8,128)(2,1)S(1)} collective-permute-done((bf16[1,1,24,1024]{3,2,1,0:T(8,128)(2,1)}, bf16[1,1,24,1024]{3,2,1,0:T(8,128)(2,1)S(1)}, u32[]{:S(2)}, u32[]{:S(2)}) %collective-permute-start.32) | collective-permute-done | bytes 49184 | tf_op jit(solution)/shard_map/ppermute | solution.py:85
  267.3 2.3 collective-permute-start.38
  269.6 2.4 collective-permute-start.37
  272.0 4.2 %place_sums.2 = (f32[192,3072]{1,0:T(8,128)}, f32[768,768]{1,0:T(8,128)}) custom-call(s32[26]{0:T(128)} %concatenate.12.meta, bf16[1152,128]{1,0:T(8,128)(2,1)} %bitcast.34.refs_0_, bf16[1152,128]{1,0:T(8,128)(2,1)} %collective-permute-done.33.refs_1_, bf16[1152,128]{1,0:T(8,128)(2,1)} %collective-permute-done.34.refs_2_, ...), custom_call_target="tpu_custom_call" | custom-call | tf_op jit(solution)/shard_map/place_sums/pallas_call | solution.py:877
  281.0 2.9 %place_sums.3 = (f32[192,2304]{1,0:T(8,128)}, f32[192,768]{1,0:T(8,128)}, f32[192]{0:T(256)}, f32[192]{0:T(256)}, f32[192]{0:T(256)}, /*index=5*/f32[192]{0:T(256)}, f32[192]{0:T(256)}, f32[192]{0:T(256)}, f32[768]{0:T(1024)}) custom-call(s32[26]{0:T(128)} %concatenate.12.meta, bf16[24,3328]{1,0:T(8,128)(2,1)} %add_convert_fusion.1.refs_0_, ...), custom_call_target="tpu_custom_call" | custom-call | tf_op jit(solution)/shard_map/place_sums/pallas_call | solution.py:877
  (104 shorter events, 48.6 us)
Async XLA Ops:
  4.5 13.8 %collective-permute-start.3 = (bf16[48,3328]{1,0:T(8,128)(2,1)}, bf16[48,3328]{1,0:T(8,128)(2,1)S(1)}, u32[]{:S(2)}, u32[]{:S(2)}) collective-permute-start(bf16[48,3328]{1,0:T(8,128)(2,1)} %get-tuple-element.115), channel_id=1, source_target_pairs={{0,1},{1,2},{2,3},{3,0},{4,7},{5,4},{6,5},{7,6},{8,9},{9,10},{10,1... | collective-permute-start | bytes 958472 | tf_op jit(solution)/shard_map/ppermute | solution.py:79
  7.6 14.5 %collective-permute-start.4 = (bf16[48,1664]{1,0:T(8,128)(2,1)}, bf16[48,1664]{1,0:T(8,128)(2,1)S(1)}, u32[]{:S(2)}, u32[]{:S(2)}) collective-permute-start(bf16[48,1664]{1,0:T(8,128)(2,1)} %get-tuple-element.116), channel_id=1, source_target_pairs={{0,2},{1,3},{2,0},{3,1},{4,6},{5,7},{6,4},{7,5},{8,10},{9,11},{10,... | collective-permute-start | bytes 479240 | tf_op jit(solution)/shard_map/ppermute | solution.py:82
  22.2 19.0 %collective-permute-start.6 = (bf16[48,4992]{1,0:T(8,128)(2,1)S(1)}, bf16[48,4992]{1,0:T(8,128)(2,1)S(1)}, u32[]{:S(2)}, u32[]{:S(2)}) collective-permute-start(bf16[48,4992]{1,0:T(8,128)(2,1)S(1)} %constant_dynamic-update-slice_fusion.refs_9_), channel_id=1, source_target_pairs={{0,16},{1,17},{2,18},{3,19},{4,12},{5,13},{6,14},{7,15},{8,24},{9,... | collective-permute-start | bytes 1437704 | tf_op jit(solution)/shard_map/ppermute | solution.py:76
  23.8 17.4 %collective-permute-start.5 = (bf16[48,4992]{1,0:T(8,128)(2,1)S(1)}, bf16[48,4992]{1,0:T(8,128)(2,1)S(1)}, u32[]{:S(2)}, u32[]{:S(2)}) collective-permute-start(bf16[48,4992]{1,0:T(8,128)(2,1)S(1)} %constant_dynamic-update-slice_fusion.refs_9_), channel_id=1, source_target_pairs={{0,8},{1,9},{2,10},{3,11},{4,20},{5,21},{6,22},{7,23},{8,0},{9,1},... | collective-permute-start | bytes 1437704 | tf_op jit(solution)/shard_map/ppermute | solution.py:73
  25.3 14.9 %collective-permute-start.1 = (bf16[1152,128]{1,0:T(8,128)(2,1)}, bf16[1152,128]{1,0:T(8,128)(2,1)S(1)}, u32[]{:S(2)}, u32[]{:S(2)}) collective-permute-start(bf16[1152,128]{1,0:T(8,128)(2,1)} %get-tuple-element.113), channel_id=1, source_target_pairs={{0,2},{1,3},{2,0},{3,1},{4,6},{5,7},{6,4},{7,5},{8,10},{9,11},{10,... | collective-permute-start | bytes 884744 | tf_op jit(solution)/shard_map/ppermute | solution.py:85
  27.5 13.7 %collective-permute-start = (bf16[1152,128]{1,0:T(8,128)(2,1)}, bf16[1152,128]{1,0:T(8,128)(2,1)S(1)}, u32[]{:S(2)}, u32[]{:S(2)}) collective-permute-start(bf16[1152,128]{1,0:T(8,128)(2,1)} %get-tuple-element.113), channel_id=1, source_target_pairs={{0,1},{1,0},{2,3},{3,2},{4,5},{5,4},{6,7},{7,6},{8,9},{9,8},{10,11... | collective-permute-start | bytes 884744 | tf_op jit(solution)/shard_map/ppermute | solution.py:85
  41.2 8.8 %collective-permute-start.7 = (bf16[48,4992]{1,0:T(8,128)(2,1)S(1)}, bf16[48,4992]{1,0:T(8,128)(2,1)S(1)}, u32[]{:S(2)}, u32[]{:S(2)}) collective-permute-start(bf16[48,4992]{1,0:T(8,128)(2,1)S(1)} %collective-permute-done.5.refs_10_), channel_id=1, source_target_pairs={{0,16},{1,17},{2,18},{3,19},{4,12},{5,13},{6,14},{7,15},{8,24},{9,... | collective-permute-start | bytes 1437704 | tf_op jit(solution)/shard_map/ppermute | solution.py:76
  42.0 7.8 %collective-permute-start.2 = (bf16[1152,128]{1,0:T(8,128)(2,1)S(1)}, bf16[1152,128]{1,0:T(8,128)(2,1)S(1)}, u32[]{:S(2)}, u32[]{:S(2)}) collective-permute-start(bf16[1152,128]{1,0:T(8,128)(2,1)S(1)} %collective-permute-done.1), channel_id=1, source_target_pairs={{0,1},{1,0},{2,3},{3,2},{4,5},{5,4},{6,7},{7,6},{8,9},{9,8},{10,11... | collective-permute-start | bytes 884744 | tf_op jit(solution)/shard_map/ppermute | solution.py:85
  42.3 9.2 %collective-permute-start.8 = (bf16[48,4992]{1,0:T(8,128)(2,1)S(1)}, bf16[48,4992]{1,0:T(8,128)(2,1)S(1)}, u32[]{:S(2)}, u32[]{:S(2)}) collective-permute-start(bf16[48,4992]{1,0:T(8,128)(2,1)S(1)} %constant_dynamic-update-slice_fusion.refs_9_), channel_id=1, source_target_pairs={{0,4},{1,5},{2,6},{3,7},{4,0},{5,1},{6,2},{7,3},{8,12},{9,13},{10,... | collective-permute-start | bytes 1437704 | tf_op jit(solution)/shard_map/ppermute | solution.py:70
  43.8 10.5 %collective-permute-start.10 = (bf16[48,4992]{1,0:T(8,128)(2,1)S(1)}, bf16[48,4992]{1,0:T(8,128)(2,1)}, u32[]{:S(2)}, u32[]{:S(2)}) collective-permute-start(bf16[48,4992]{1,0:T(8,128)(2,1)S(1)} %collective-permute-done.6.refs_11_), channel_id=1, source_target_pairs={{0,4},{1,5},{2,6},{3,7},{4,0},{5,1},{6,2},{7,3},{8,12},{9,13},{10,... | collective-permute-start | bytes 1437704 | tf_op jit(solution)/shard_map/ppermute | solution.py:70
  44.3 9.9 %collective-permute-start.9 = (bf16[48,4992]{1,0:T(8,128)(2,1)S(1)}, bf16[48,4992]{1,0:T(8,128)(2,1)}, u32[]{:S(2)}, u32[]{:S(2)}) collective-permute-start(bf16[48,4992]{1,0:T(8,128)(2,1)S(1)} %collective-permute-done.5.refs_10_), channel_id=1, source_target_pairs={{0,4},{1,5},{2,6},{3,7},{4,0},{5,1},{6,2},{7,3},{8,12},{9,13},{10,... | collective-permute-start | bytes 1437704 | tf_op jit(solution)/shard_map/ppermute | solution.py:70
  51.1 26.8 %collective-permute-start.13 = (bf16[3,1152,128]{2,1,0:T(8,128)(2,1)}, bf16[3,1152,128]{2,1,0:T(8,128)(2,1)}, u32[]{:S(2)}, u32[]{:S(2)}) collective-permute-start(bf16[3,1152,128]{2,1,0:T(8,128)(2,1)} %pad_maximum_fusion.refs_7_), channel_id=1, source_target_pairs={{0,16},{1,17},{2,18},{3,19},{4,12},{5,13},{6,14},{7,15},{8,24},{9,... | collective-permute-start | bytes 2654216 | tf_op jit(solution)/shard_map/ppermute | solution.py:76
  51.6 26.3 %collective-permute-start.12 = (bf16[3,1152,128]{2,1,0:T(8,128)(2,1)}, bf16[3,1152,128]{2,1,0:T(8,128)(2,1)}, u32[]{:S(2)}, u32[]{:S(2)}) collective-permute-start(bf16[3,1152,128]{2,1,0:T(8,128)(2,1)} %pad_maximum_fusion.refs_7_), channel_id=1, source_target_pairs={{0,8},{1,9},{2,10},{3,11},{4,20},{5,21},{6,22},{7,23},{8,0},{9,1},... | collective-permute-start | bytes 2654216 | tf_op jit(solution)/shard_map/ppermute | solution.py:73
  77.9 13.9 %collective-permute-start.14 = (bf16[1024,768]{1,0:T(8,128)(2,1)}, bf16[1024,768]{1,0:T(8,128)(2,1)}, u32[]{:S(2)}, u32[]{:S(2)}) collective-permute-start(bf16[1024,768]{1,0:T(8,128)(2,1)} %get-tuple-element.121.refs_0_), channel_id=1, source_target_pairs={{0,4},{1,5},{2,6},{3,7},{4,0},{5,1},{6,2},{7,3},{8,12},{9,13},{10,... | collective-permute-start | bytes 4718600 | tf_op jit(solution)/shard_map/ppermute | solution.py:70
  77.9 13.9 %collective-permute-start.15 = (bf16[1024,768]{1,0:T(8,128)(2,1)}, bf16[1024,768]{1,0:T(8,128)(2,1)}, u32[]{:S(2)}, u32[]{:S(2)}) collective-permute-start(bf16[1024,768]{1,0:T(8,128)(2,1)} %get-tuple-element.122.refs_2_.gp), channel_id=1, source_target_pairs={{0,4},{1,5},{2,6},{3,7},{4,0},{5,1},{6,2},{7,3},{8,12},{9,13},{10,... | collective-permute-start | bytes 4718600 | tf_op jit(solution)/shard_map/ppermute | solution.py:70
  78.4 13.4 %collective-permute-start.16 = (bf16[3,1152,128]{2,1,0:T(8,128)(2,1)}, bf16[3,1152,128]{2,1,0:T(8,128)(2,1)}, u32[]{:S(2)}, u32[]{:S(2)}) collective-permute-start(bf16[3,1152,128]{2,1,0:T(8,128)(2,1)} %collective-permute-done.12.refs_8_), channel_id=1, source_target_pairs={{0,16},{1,17},{2,18},{3,19},{4,12},{5,13},{6,14},{7,15},{8,24},{9,... | collective-permute-start | bytes 2654216 | tf_op jit(solution)/shard_map/ppermute | solution.py:76
  138.0 30.6 %collective-permute-start.18 = (bf16[2,4,1152,128]{3,2,1,0:T(8,128)(2,1)}, bf16[2,4,1152,128]{3,2,1,0:T(8,128)(2,1)}, u32[]{:S(2)}, u32[]{:S(2)}) collective-permute-start(bf16[2,4,1152,128]{3,2,1,0:T(8,128)(2,1)} %get-tuple-element.131), channel_id=1, source_target_pairs={{0,8},{1,9},{2,10},{3,11},{4,20},{5,21},{6,22},{7,23},{8,0},{9,1},... | collective-permute-start | bytes 7077896 | tf_op jit(solution)/shard_map/ppermute | solution.py:73
  168.7 11.8 %collective-permute-start.17 = (bf16[1024,768]{1,0:T(8,128)(2,1)}, bf16[1024,768]{1,0:T(8,128)(2,1)}, u32[]{:S(2)}, u32[]{:S(2)}) collective-permute-start(bf16[1024,768]{1,0:T(8,128)(2,1)} %get-tuple-element.126), channel_id=1, source_target_pairs={{0,4},{1,5},{2,6},{3,7},{4,0},{5,1},{6,2},{7,3},{8,12},{9,13},{10,... | collective-permute-start | bytes 4718600 | tf_op jit(solution)/shard_map/ppermute | solution.py:70
  174.0 25.5 %collective-permute-start.20 = (bf16[1,48,96,128]{3,2,1,0:T(8,128)(2,1)}, bf16[1,48,96,128]{3,2,1,0:T(8,128)(2,1)}, u32[]{:S(2)}, u32[]{:S(2)}) collective-permute-start(bf16[1,48,96,128]{3,2,1,0:T(8,128)(2,1)} %get-tuple-element.145), channel_id=1, source_target_pairs={{0,16},{1,17},{2,18},{3,19},{4,12},{5,13},{6,14},{7,15},{8,24},{9,... | collective-permute-start | bytes 3538952 | tf_op jit(solution)/shard_map/ppermute | solution.py:76
  179.2 20.3 %collective-permute-start.22 = (bf16[1,8,24,2304]{3,2,1,0:T(8,128)(2,1)}, bf16[1,8,24,2304]{3,2,1,0:T(8,128)(2,1)}, u32[]{:S(2)}, u32[]{:S(2)}) collective-permute-start(bf16[1,8,24,2304]{3,2,1,0:T(8,128)(2,1)} %get-tuple-element.150), channel_id=1, source_target_pairs={{0,8},{1,9},{2,10},{3,11},{4,20},{5,21},{6,22},{7,23},{8,0},{9,1},... | collective-permute-start | bytes 2654216 | tf_op jit(solution)/shard_map/ppermute | solution.py:73
  203.8 15.8 %collective-permute-start.24 = (bf16[2,12,96,128]{3,2,1,0:T(8,128)(2,1)}, bf16[2,12,96,128]{3,2,1,0:T(8,128)(2,1)}, u32[]{:S(2)}, u32[]{:S(2)}) collective-permute-start(bf16[2,12,96,128]{3,2,1,0:T(8,128)(2,1)} %get-tuple-element.163), channel_id=1, source_target_pairs={{0,1},{1,0},{2,3},{3,2},{4,5},{5,4},{6,7},{7,6},{8,9},{9,8},{10,11... | collective-permute-start | bytes 1769480 | tf_op jit(solution)/shard_map/ppermute | solution.py:85
  204.0 8.6 %collective-permute-start.23 = (bf16[1,4,24,2304]{3,2,1,0:T(8,128)(2,1)}, bf16[1,4,24,2304]{3,2,1,0:T(8,128)(2,1)}, u32[]{:S(2)}, u32[]{:S(2)}) collective-permute-start(bf16[1,4,24,2304]{3,2,1,0:T(8,128)(2,1)} %get-tuple-element.157), channel_id=1, source_target_pairs={{0,16},{1,17},{2,18},{3,19},{4,12},{5,13},{6,14},{7,15},{8,24},{9,... | collective-permute-start | bytes 1327112 | tf_op jit(solution)/shard_map/ppermute | solution.py:76
  225.0 13.6 %collective-permute-start.26 = (bf16[1,8,24,1024]{3,2,1,0:T(8,128)(2,1)}, bf16[1,8,24,1024]{3,2,1,0:T(8,128)(2,1)}, u32[]{:S(2)}, u32[]{:S(2)}) collective-permute-start(bf16[1,8,24,1024]{3,2,1,0:T(8,128)(2,1)} %get-tuple-element.171), channel_id=1, source_target_pairs={{0,8},{1,9},{2,10},{3,11},{4,20},{5,21},{6,22},{7,23},{8,0},{9,1},... | collective-permute-start | bytes 1179656 | tf_op jit(solution)/shard_map/ppermute | solution.py:73
  226.3 16.7 %collective-permute-start.29 = (bf16[1,12,96,128]{3,2,1,0:T(8,128)(2,1)}, bf16[1,12,96,128]{3,2,1,0:T(8,128)(2,1)}, u32[]{:S(2)}, u32[]{:S(2)}) collective-permute-start(bf16[1,12,96,128]{3,2,1,0:T(8,128)(2,1)} %get-tuple-element.169), channel_id=1, source_target_pairs={{0,2},{1,3},{2,0},{3,1},{4,6},{5,7},{6,4},{7,5},{8,10},{9,11},{10,... | collective-permute-start | bytes 884744 | tf_op jit(solution)/shard_map/ppermute | solution.py:85
  226.5 12.1 %collective-permute-start.27 = (bf16[2,1,24,2304]{3,2,0,1:T(8,128)(2,1)}, bf16[2,1,24,2304]{3,2,0,1:T(8,128)(2,1)}, u32[]{:S(2)}, u32[]{:S(2)}) collective-permute-start(bf16[2,1,24,2304]{3,2,0,1:T(8,128)(2,1)} %bitcast.59), channel_id=1, source_target_pairs={{0,1},{1,0},{2,3},{3,2},{4,5},{5,4},{6,7},{7,6},{8,9},{9,8},{10,11... | collective-permute-start | bytes 663560 | tf_op jit(solution)/shard_map/ppermute | solution.py:85
  240.9 9.3 %collective-permute-start.28 = (bf16[1,4,24,1024]{3,2,1,0:T(8,128)(2,1)}, bf16[1,4,24,1024]{3,2,1,0:T(8,128)(2,1)}, u32[]{:S(2)}, u32[]{:S(2)}) collective-permute-start(bf16[1,4,24,1024]{3,2,1,0:T(8,128)(2,1)} %get-tuple-element.181), channel_id=1, source_target_pairs={{0,16},{1,17},{2,18},{3,19},{4,12},{5,13},{6,14},{7,15},{8,24},{9,... | collective-permute-start | bytes 589832 | tf_op jit(solution)/shard_map/ppermute | solution.py:76
  244.8 14.7 %collective-permute-start.35 = (bf16[1152,128]{1,0:T(8,128)(2,1)}, bf16[1152,128]{1,0:T(8,128)(2,1)}, u32[]{:S(2)}, u32[]{:S(2)}) collective-permute-start(bf16[1152,128]{1,0:T(8,128)(2,1)} %bitcast.34.refs_0_), channel_id=1, source_target_pairs={{0,24},{1,25},{2,26},{3,27},{4,28},{5,29},{6,30},{7,31},{8,16},{9,... | collective-permute-start | bytes 884744 | tf_op jit(solution)/shard_map/ppermute | solution.py:88
  246.0 15.3 %collective-permute-start.34 = (bf16[1152,128]{1,0:T(8,128)(2,1)}, bf16[1152,128]{1,0:T(8,128)(2,1)}, u32[]{:S(2)}, u32[]{:S(2)}) collective-permute-start(bf16[1152,128]{1,0:T(8,128)(2,1)} %bitcast.34.refs_0_), channel_id=1, source_target_pairs={{0,16},{1,17},{2,18},{3,19},{4,12},{5,13},{6,14},{7,15},{8,24},{9,... | collective-permute-start | bytes 884744 | tf_op jit(solution)/shard_map/ppermute | solution.py:76
  247.5 13.8 %collective-permute-start.33 = (bf16[1152,128]{1,0:T(8,128)(2,1)}, bf16[1152,128]{1,0:T(8,128)(2,1)}, u32[]{:S(2)}, u32[]{:S(2)}) collective-permute-start(bf16[1152,128]{1,0:T(8,128)(2,1)} %bitcast.34.refs_0_), channel_id=1, source_target_pairs={{0,8},{1,9},{2,10},{3,11},{4,20},{5,21},{6,22},{7,23},{8,0},{9,1},... | collective-permute-start | bytes 884744 | tf_op jit(solution)/shard_map/ppermute | solution.py:73
  248.3 7.9 %collective-permute-start.31 = (bf16[1,1,24,2304]{3,2,1,0:T(8,128)(2,1)}, bf16[1,1,24,2304]{3,2,1,0:T(8,128)(2,1)}, u32[]{:S(2)}, u32[]{:S(2)}) collective-permute-start(bf16[1,1,24,2304]{3,2,1,0:T(8,128)(2,1)} %get-tuple-element.187), channel_id=1, source_target_pairs={{0,2},{1,3},{2,0},{3,1},{4,6},{5,7},{6,4},{7,5},{8,10},{9,11},{10,... | collective-permute-start | bytes 331784 | tf_op jit(solution)/shard_map/ppermute | solution.py:85
  267.3 8.9 %collective-permute-start.38 = (bf16[24,3328]{1,0:T(8,128)(2,1)}, bf16[24,3328]{1,0:T(8,128)(2,1)}, u32[]{:S(2)}, u32[]{:S(2)}) collective-permute-start(bf16[24,3328]{1,0:T(8,128)(2,1)} %add_convert_fusion.1.refs_0_), channel_id=1, source_target_pairs={{0,24},{1,25},{2,26},{3,27},{4,28},{5,29},{6,30},{7,31},{8,16},{9,... | collective-permute-start | bytes 479240 | tf_op jit(solution)/shard_map/ppermute | solution.py:88
  269.6 8.3 %collective-permute-start.37 = (bf16[24,3328]{1,0:T(8,128)(2,1)}, bf16[24,3328]{1,0:T(8,128)(2,1)}, u32[]{:S(2)}, u32[]{:S(2)}) collective-permute-start(bf16[24,3328]{1,0:T(8,128)(2,1)} %add_convert_fusion.1.refs_0_), channel_id=1, source_target_pairs={{0,16},{1,17},{2,18},{3,19},{4,12},{5,13},{6,14},{7,15},{8,24},{9,... | collective-permute-start | bytes 479240 | tf_op jit(solution)/shard_map/ppermute | solution.py:76
  (20 other events, 124.3 us)

commit v2 on v1

--- a/solution.py
+++ b/solution.py
@@ -918,7 +918,7 @@
 
     mate, far_h = routes.z_flip(hid, 1), routes.z_flip(hid, 2)
     last_h = routes.z_flip(far_h, 1)
-    p_mixed = gather_mixed(routes, near, far, (mate, far_h), last_h)
+    p_mixed = gather_mixed(routes, near, far, (mate,), last_h)
     block = jnp.stack([mate, far_h, last_h])
     p_hid = [block, routes.first(block), routes.second(block)]
     qkv, prob, inv, o, x1, a2, a1, gp, w, vec, b1, dbf = k1(
@@ -957,13 +957,14 @@
     s_l, k_l = halve(meta, (I_B1, chunk(kl, 1, 8), chunk(tie(got_l, s_h), 1, 8)))
     got_l = routes.first(s_l)
     layer_out = layer_output(meta, yo, yq, x1, tie(vec, s_l))
-    s_l, k_l, s_m, k_m = halve(meta, (I_B2, chunk(k_l, 1, 4), chunk(tie(got_l, layer_out), 1, 4)),
-                               (I_Z + 5, chunk(k_m, 1, 1), chunk(tie(got_m, layer_out), 1, 1)))
-    got_l, got_m = routes.second(s_l), routes.z_flip(s_m, 2)
+    s_l, k_l = halve(meta, (I_B2, chunk(k_l, 1, 4), chunk(tie(got_l, layer_out), 1, 4)))
+    got_l = routes.second(s_l)
+    s_l, k_l, s_m, k_m = halve(meta, (I_Z + 4, chunk(k_l, 2, 1), chunk(got_l, 2, 1)),
+                               (I_Z + 5, chunk(k_m, 1, 1), chunk(tie(got_m, s_l), 1, 1)))
     piece = total(routes, k_h.reshape(-1, 128), tie(got_h, s_l).reshape(-1, 128))
     near_by = around(routes, piece)
-    s_l, k_l = halve(meta, (I_Z + 4, chunk(k_l, 2, 1), chunk(tie(got_l, piece), 2, 1)))
-    s_l, k_l = halve(meta, (I_Z + 5, chunk(k_l, 1, 1), chunk(tie(routes.z_flip(s_l, 1), got_m), 1, 1)))
+    got_l, got_m = routes.z_flip(s_l, 1), routes.z_flip(s_m, 2)
+    s_l, k_l = halve(meta, (I_Z + 5, chunk(k_l, 1, 1), chunk(tie(got_l, piece), 1, 1)))
     got_l = tie(routes.z_flip(s_l, 2), *near_by)
     side = lambda a, b: jnp.concatenate([a.reshape(d // 32, -1), b.reshape(d // 32, -1)], axis=1)
     piece = total(routes, side(k_m, k_l), side(got_m, got_l))

time: 285 us -> 281 us (0.986)
  waiting for transfers between devices: 72.9 us -> 66.9 us
    ppermute x9, waiting for transfers between devices: 37.7 us -> 29.2 us  [z_flip(): return lax.ppermute(a, ALL, self.table(lambda d, z: (d, z ^ bit)))]
  transfers between devices with their start and end apart: 47 -> 47, of which waited for: 22 -> 20; matrix products, arithmetic and copies ran while one was open for 2% -> 2% of each run, Pallas kernels for 35% -> 36%
where the time goes in v2:
time: 281 us; the launch traced here: 280 us
  Pallas kernels  160 us (57%)
  waiting for transfers between devices  66.9 us (24%)
  starting transfers between devices  43.1 us (15%)
  other arithmetic  6.3 us (2%)
    pallas_call x1, Pallas kernels, mlp(): pl.pallas_call(functools.partial(mlp_body, ng, go, first), grid_spec=pltp...  46.1 us
    ppermute x9, waiting for transfers between devices, z_flip(): return lax.ppermute(a, ALL, self.table(lambda d, z: (d, z ^ bit)))  29.2 us
    pallas_call x8, Pallas kernels, halve(): pl.pallas_call(functools.partial(halve_body, tuple(((p, len(ks), ks[0].sh...  24.1 us
    pallas_call x1, Pallas kernels, k1(): pl.pallas_call(k1_body, grid_spec=pltpu.PrefetchScalarGridSpec(num_scalar...  23.5 us
    ppermute x9, waiting for transfers between devices, second(): lax.ppermute(a, ALL, self.table(lambda d, z: (d ^ (4 if d % 2 == 0 else 2...  20 us
    pallas_call x1, Pallas kernels, back_late(): pl.pallas_call(back_late_body, grid_spec=pltpu.PrefetchScalarGridSpec(num...  19 us
    pallas_call x1, Pallas kernels, back_early(): pl.pallas_call(back_early_body, grid=(t // BLOCK,), in_specs=[blk(d), blk...  16.1 us
    pallas_call x2, Pallas kernels, grads(): pl.pallas_call(body, grid_spec=pltpu.PrefetchScalarGridSpec(num_scalar_pr...  15.3 us
  transfers between devices with their start and end apart: 47, of which 20 were waited for; matrix products, arithmetic and copies ran while one was open for 2% of the time, Pallas kernels for 36%

profile of v2, /device:TPU:0, one launch (start us, length us, event | category | flops | bytes accessed | tf_op | source)
XLA Modules:
  0.0 280.0 jit_solution(9484533067402145197)
XLA Ops:
  0.7 3.9 %pack.1 = (bf16[192,3328]{1,0:T(8,128)(2,1)}, bf16[48,3328]{1,0:T(8,128)(2,1)}, bf16[48,1664]{1,0:T(8,128)(2,1)}, bf16[1152,128]{1,0:T(8,128)(2,1)}) custom-call(s32[1]{0:T(128)} %bitcast.9.pos, bf16[192,2304]{1,0:T(8,128)(2,1)} %refs_0_.3, bf16[192,768]{1,0:T(8,128)(2,1)} %refs_1_.3, bf16[192]{0:T(256)(128)(2,1)} %refs_2_.3, bf16[192]{0:T(256)(128)(2,1)} %refs_3_.3, ...), custom_call_target="tpu_custom_call" | custom-call | tf_op jit(solution)/shard_map/pack/pallas_call | solution.py:194
  4.5 3.1 %collective-permute-start.3 = (bf16[48,3328]{1,0:T(8,128)(2,1)}, bf16[48,3328]{1,0:T(8,128)(2,1)S(1)}, u32[]{:S(2)}, u32[]{:S(2)}) collective-permute-start(bf16[48,3328]{1,0:T(8,128)(2,1)} %get-tuple-element.114), channel_id=1, source_target_pairs={{0,1},{1,2},{2,3},{3,0},{4,7},{5,4},{6,5},{7,6},{8,9},{9,10},{10,1... | collective-permute-start | bytes 958472 | tf_op jit(solution)/shard_map/ppermute | solution.py:79
  7.6 2.6 collective-permute-start.4
  10.2 8.1 %collective-permute-done.3 = bf16[48,3328]{1,0:T(8,128)(2,1)S(1)} collective-permute-done((bf16[48,3328]{1,0:T(8,128)(2,1)}, bf16[48,3328]{1,0:T(8,128)(2,1)S(1)}, u32[]{:S(2)}, u32[]{:S(2)}) %collective-permute-start.3) | collective-permute-done | bytes 319520 | tf_op jit(solution)/shard_map/ppermute | solution.py:79
  18.4 3.7 %collective-permute-done.4 = bf16[48,1664]{1,0:T(8,128)(2,1)S(1)} collective-permute-done((bf16[48,1664]{1,0:T(8,128)(2,1)}, bf16[48,1664]{1,0:T(8,128)(2,1)S(1)}, u32[]{:S(2)}, u32[]{:S(2)}) %collective-permute-start.4) | collective-permute-done | bytes 159776 | tf_op jit(solution)/shard_map/ppermute | solution.py:82
  27.4 3.3 %collective-permute-start.1 = (bf16[1152,128]{1,0:T(8,128)(2,1)}, bf16[1152,128]{1,0:T(8,128)(2,1)S(1)}, u32[]{:S(2)}, u32[]{:S(2)}) collective-permute-start(bf16[1152,128]{1,0:T(8,128)(2,1)} %get-tuple-element.112), channel_id=1, source_target_pairs={{0,2},{1,3},{2,0},{3,1},{4,6},{5,7},{6,4},{7,5},{8,10},{9,11},{10,... | collective-permute-start | bytes 884744 | tf_op jit(solution)/shard_map/ppermute | solution.py:85
  31.5 8.2 %collective-permute-done = bf16[1152,128]{1,0:T(8,128)(2,1)S(1)} collective-permute-done((bf16[1152,128]{1,0:T(8,128)(2,1)}, bf16[1152,128]{1,0:T(8,128)(2,1)S(1)}, u32[]{:S(2)}, u32[]{:S(2)}) %collective-permute-start) | collective-permute-done | bytes 294944 | tf_op jit(solution)/shard_map/ppermute | solution.py:85
  44.2 4.7 %collective-permute-done.2 = bf16[1152,128]{1,0:T(8,128)(2,1)S(1)} collective-permute-done((bf16[1152,128]{1,0:T(8,128)(2,1)S(1)}, bf16[1152,128]{1,0:T(8,128)(2,1)S(1)}, u32[]{:S(2)}, u32[]{:S(2)}) %collective-permute-start.2) | collective-permute-done | bytes 294944 | tf_op jit(solution)/shard_map/ppermute | solution.py:85
  53.3 23.5 %norm_qkv_attend.1 = (bf16[1024,2304]{1,0:T(8,128)(2,1)}, bf16[4,12,256,256]{3,2,1,0:T(8,128)(2,1)}, f32[1024,768]{1,0:T(8,128)}, bf16[1024,768]{1,0:T(8,128)(2,...) custom-call(s32[26]{0:T(128)} %concatenate.12.meta, ...), custom_call_target="tpu_custom_call" | custom-call | flops 6039797760 | bytes 41943040 | tf_op jit(solution)/shard_map/norm_qkv_attend/pallas_call | solution.py:306
  79.0 11.8 %collective-permute-done.16.refs_10_ = bf16[3,1152,128]{2,1,0:T(8,128)(2,1)} collective-permute-done((bf16[3,1152,128]{2,1,0:T(8,128)(2,1)}, bf16[3,1152,128]{2,1,0:T(8,128)(2,1)}, u32[]{:S(2)}, u32[]{:S(2)}) %collective-permute-start.16) | collective-permute-done | bytes 884768 | tf_op jit(solution)/shard_map/ppermute | solution.py:76
  90.8 46.1 %hidden_first.1 = (bf16[1024,768]{1,0:T(8,128)(2,1)}, bf16[1024,768]{1,0:T(8,128)(2,1)}, bf16[1024,768]{1,0:T(8,128)(2,1)}, bf16[1024,768]{1,0:T(8,128)(2,1)}, b...) custom-call(s32[26]{0:T(128)} %concatenate.12.meta, ...), custom_call_target="tpu_custom_call" | custom-call | flops 28991029248 | bytes 31457280 | tf_op jit(solution)/shard_map/hidden_first/pallas_call | solution.py:481
  137.7 3.7 %collective-permute-done.19.da_p = bf16[1024,768]{1,0:T(8,128)(2,1)} collective-permute-done((bf16[1024,768]{1,0:T(8,128)(2,1)}, bf16[1024,768]{1,0:T(8,128)(2,1)}, u32[]{:S(2)}, u32[]{:S(2)}) %collective-permute-start.19) | collective-permute-done | bytes 1572896 | tf_op jit(solution)/shard_map/ppermute | solution.py:70
  141.4 16.1 %attend_back_early.1 = (f32[1024,768]{1,0:T(8,128)}, bf16[1024,768]{1,0:T(8,128)(2,1)}, bf16[1024,1536]{1,0:T(8,128)(2,1)}, f32[128,768]{1,0:T(8,128)}) custom-call(bf16[1024,768]{1,0:T(8,128)(2,1)} %get-tuple-element.121.refs_2_.gp, bf16[1024,768]{1,0:T(8,128)(2,1)} %get-tuple-element.131.da_o, bf16[1024,768]{1,0:T(8,128)(2,1)} %collective-permute-done.19.da_p, ...), custom_call_target="tpu_custom_call" | custom-call | flops 4831838208 | bytes 25165824 | tf_op jit(solution)/shard_map/attend_back_early/pallas_call | solution.py:556
  157.5 9.9 %weight_grads.2 = (bf16[2,2,4,24,2304]{4,3,2,1,0:T(8,128)(2,1)}, bf16[2,2,4,24,2304]{4,3,2,1,0:T(8,128)(2,1)}) custom-call(s32[26]{0:T(128)} %concatenate.12.meta, bf16[1024,768]{1,0:T(8,128)(2,1)} %get-tuple-element.157.a1, bf16[1024,1536]{1,0:T(8,128)(2,1)} %get-tuple-element.139.dq.refs_6_, bf16[1024,768]{1,0:T(8,128)(2,1)} %get-tuple-element.135.o.refs_9_, ...), custom_call_target="tpu_custom_call" | custom-call | flops 1 | bytes 1 | tf_op jit(solution)/shard_map/weight_grads/pallas_call | solution.py:705
  167.9 4.9 %add_halve.8 = (bf16[1,48,96,128]{3,2,1,0:T(8,128)(2,1)}, bf16[1,48,96,128]{3,2,1,0:T(8,128)(2,1)}) custom-call(s32[26]{0:T(128)} %concatenate.12.meta, bf16[1,2,48,96,128]{4,3,2,1,0:T(8,128)(2,1)} %bitcast.42, bf16[1,2,48,96,128]{4,3,2,1,0:T(8,128)(2,1)} %bitcast.14.refs_1_), custom_call_target="tpu_custom_call" | custom-call | flops 1179648 | bytes 7077888 | tf_op jit(solution)/shard_map/add_halve/pallas_call | solution.py:802
  174.4 3.7 %add_halve.9 = (bf16[1,8,24,2304]{3,2,1,0:T(8,128)(2,1)}, bf16[1,8,24,2304]{3,2,1,0:T(8,128)(2,1)}) custom-call(s32[26]{0:T(128)} %concatenate.12.meta, bf16[1,2,8,24,2304]{4,3,2,1,0:T(8,128)(2,1)} %bitcast.43, bf16[1,2,8,24,2304]{4,3,2,1,0:T(8,128)(2,1)} %bitcast.17.refs_1_), custom_call_target="tpu_custom_call" | custom-call | flops 884736 | bytes 5308416 | tf_op jit(solution)/shard_map/add_halve/pallas_call | solution.py:802
  179.5 19.0 %attend_back_late.1 = (f32[1024,768]{1,0:T(8,128)}, bf16[1024,768]{1,0:T(8,128)(2,1)}, f32[128,768]{1,0:T(8,128)}) custom-call(s32[26]{0:T(128)} %concatenate.12.meta, bf16[1024,768]{1,0:T(8,128)(2,1)} %refs_3_.5, bf16[1024,768]{1,0:T(8,128)(2,1)} %refs_3_.5, bf16[1024,768]{1,0:T(8,128)(2,1)} %refs_3_.5, bf16[1024,768]{1,0:T(8,128)(2,1)} %refs_3_.5, ...), custom_call_target="tpu_custom_call" | custom-call | flops 6039797760 | bytes 20971520 | tf_op jit(solution)/shard_map/attend_back_late/pallas_call | solution.py:629
  198.6 4.2 %add_halve.10 = (bf16[2,12,96,128]{3,2,1,0:T(8,128)(2,1)}, bf16[2,12,96,128]{3,2,1,0:T(8,128)(2,1)}, bf16[1,4,24,2304]{3,2,1,0:T(8,128)(2,1)}, bf16[1,4,24,2304]{3,2,1,0:T(8,128)(2,1)}) custom-call(s32[26]{0:T(128)} %concatenate.12.meta, bf16[2,2,12,96,128]{4,3,2,1,0:T(8,128)(2,1)} %bitcast.44, bf16[2,2,12,96,128]{4,3,2,1,0:T(8,128)(2,1)} %bitcast.18.refs_1_, ...), custom_call_target="tpu_custom_call" | custom-call | flops 1032192 | bytes 6193152 | tf_op jit(solution)/shard_map/add_halve/pallas_call | solution.py:802
  204.0 5.3 %weight_grads.3 = (bf16[2,2,4,24,1024]{4,3,2,1,0:T(8,128)(2,1)}, bf16[2,2,4,24,1024]{4,3,2,1,0:T(8,128)(2,1)}) custom-call(s32[26]{0:T(128)} %concatenate.12.meta, bf16[1024,768]{1,0:T(8,128)(2,1)} %get-tuple-element.157.a1, bf16[1024,768]{1,0:T(8,128)(2,1)} %get-tuple-element.158.dq, f32[128,768]{1,0:T(8,128)} %get-tuple-element.152.acc, ...), custom_call_target="tpu_custom_call" | custom-call | flops 1207959552 | bytes 12582912 | tf_op jit(solution)/shard_map/weight_grads/pallas_call | solution.py:705
  209.3 2.4 collective-permute-done.23
  211.7 6.8 %collective-permute-done.24 = bf16[2,12,96,128]{3,2,1,0:T(8,128)(2,1)} collective-permute-done((bf16[2,12,96,128]{3,2,1,0:T(8,128)(2,1)}, bf16[2,12,96,128]{3,2,1,0:T(8,128)(2,1)}, u32[]{:S(2)}, u32[]{:S(2)}) %collective-permute-start.24) | collective-permute-done | bytes 589856 | tf_op jit(solution)/shard_map/ppermute | solution.py:85
  218.5 2.9 %add_halve.11 = (bf16[2,1,24,2304]{3,2,1,0:T(8,128)(2,1)}, bf16[2,1,24,2304]{3,2,1,0:T(8,128)(2,1)}, bf16[1,12,96,128]{3,2,1,0:T(8,128)(2,1)}, bf16[1,12,96,128]{3,2,1,0:T(8,128)(2,1)}) custom-call(s32[26]{0:T(128)} %concatenate.12.meta, bf16[2,2,1,24,2304]{4,3,2,1,0:T(8,128)(2,1)} %bitcast.48, bf16[2,2,1,24,2304]{4,3,2,1,0:T(8,128)(2,1)} %bitcast.23.refs_1_, ...), custom_call_target="tpu_custom_call" | custom-call | flops 516096 | bytes 3096576 | tf_op jit(solution)/shard_map/add_halve/pallas_call | solution.py:802
  221.4 2.5 add_halve.12
  227.1 5.4 %layer_out.1 = bf16[1024,768]{1,0:T(8,128)(2,1)} custom-call(s32[26]{0:T(128)} %concatenate.12.meta, bf16[1024,768]{1,0:T(8,128)(2,1)} %get-tuple-element.124.ya, bf16[1024,768]{1,0:T(8,128)(2,1)} %collective-permute-done.17.yb, f32[1024,768]{1,0:T(8,128)} %get-tuple-element.126.x1_r.x1, f32[16,768]{1,0:T(8,128)} %get-tuple-element.171.vec.refs_12_), custom_call_target="tpu_custom_call" | custom-call | flops 3145728 | bytes 8388608 | tf_op jit(solution)/shard_map/layer_out/pallas_call | solution.py:756
  237.5 3.1 %collective-permute-done.27 = bf16[1,4,24,1024]{3,2,1,0:T(8,128)(2,1)} collective-permute-done((bf16[1,4,24,1024]{3,2,1,0:T(8,128)(2,1)}, bf16[1,4,24,1024]{3,2,1,0:T(8,128)(2,1)}, u32[]{:S(2)}, u32[]{:S(2)}) %collective-permute-start.27) | collective-permute-done | bytes 196640 | tf_op jit(solution)/shard_map/ppermute | solution.py:76
  244.5 2.7 collective-permute-start.35
  248.4 2.9 %collective-permute-start.31 = (bf16[1,1,24,2304]{3,2,1,0:T(8,128)(2,1)}, bf16[1,1,24,2304]{3,2,1,0:T(8,128)(2,1)}, u32[]{:S(2)}, u32[]{:S(2)}) collective-permute-start(bf16[1,1,24,2304]{3,2,1,0:T(8,128)(2,1)} %get-tuple-element.187), channel_id=1, source_target_pairs={{0,2},{1,3},{2,0},{3,1},{4,6},{5,7},{6,4},{7,5},{8,10},{9,11},{10,... | collective-permute-start | bytes 331784 | tf_op jit(solution)/shard_map/ppermute | solution.py:85
  251.3 2.4 collective-permute-done.29
  256.7 4.2 %collective-permute-done.32 = bf16[1,1,24,1024]{3,2,1,0:T(8,128)(2,1)S(1)} collective-permute-done((bf16[1,1,24,1024]{3,2,1,0:T(8,128)(2,1)}, bf16[1,1,24,1024]{3,2,1,0:T(8,128)(2,1)S(1)}, u32[]{:S(2)}, u32[]{:S(2)}) %collective-permute-start.32) | collective-permute-done | bytes 49184 | tf_op jit(solution)/shard_map/ppermute | solution.py:85
  267.3 4.2 %place_sums.2 = (f32[192,3072]{1,0:T(8,128)}, f32[768,768]{1,0:T(8,128)}) custom-call(s32[26]{0:T(128)} %concatenate.12.meta, bf16[1152,128]{1,0:T(8,128)(2,1)} %bitcast.37.refs_0_, bf16[1152,128]{1,0:T(8,128)(2,1)} %collective-permute-done.33.refs_1_, bf16[1152,128]{1,0:T(8,128)(2,1)} %collective-permute-done.34.refs_2_, ...), custom_call_target="tpu_custom_call" | custom-call | tf_op jit(solution)/shard_map/place_sums/pallas_call | solution.py:877
  272.0 2.5 collective-permute-done.37.refs_2_
  276.9 2.9 %place_sums.3 = (f32[192,2304]{1,0:T(8,128)}, f32[192,768]{1,0:T(8,128)}, f32[192]{0:T(256)}, f32[192]{0:T(256)}, f32[192]{0:T(256)}, /*index=5*/f32[192]{0:T(256)}, f32[192]{0:T(256)}, f32[192]{0:T(256)}, f32[768]{0:T(1024)}) custom-call(s32[26]{0:T(128)} %concatenate.12.meta, bf16[24,3328]{1,0:T(8,128)(2,1)} %add_convert_fusion.1.refs_0_, ...), custom_call_target="tpu_custom_call" | custom-call | tf_op jit(solution)/shard_map/place_sums/pallas_call | solution.py:877
  (104 shorter events, 47.3 us)
Async XLA Ops:
  4.5 13.8 %collective-permute-start.3 = (bf16[48,3328]{1,0:T(8,128)(2,1)}, bf16[48,3328]{1,0:T(8,128)(2,1)S(1)}, u32[]{:S(2)}, u32[]{:S(2)}) collective-permute-start(bf16[48,3328]{1,0:T(8,128)(2,1)} %get-tuple-element.114), channel_id=1, source_target_pairs={{0,1},{1,2},{2,3},{3,0},{4,7},{5,4},{6,5},{7,6},{8,9},{9,10},{10,1... | collective-permute-start | bytes 958472 | tf_op jit(solution)/shard_map/ppermute | solution.py:79
  7.6 14.5 %collective-permute-start.4 = (bf16[48,1664]{1,0:T(8,128)(2,1)}, bf16[48,1664]{1,0:T(8,128)(2,1)S(1)}, u32[]{:S(2)}, u32[]{:S(2)}) collective-permute-start(bf16[48,1664]{1,0:T(8,128)(2,1)} %get-tuple-element.115), channel_id=1, source_target_pairs={{0,2},{1,3},{2,0},{3,1},{4,6},{5,7},{6,4},{7,5},{8,10},{9,11},{10,... | collective-permute-start | bytes 479240 | tf_op jit(solution)/shard_map/ppermute | solution.py:82
  22.2 17.6 %collective-permute-start.6 = (bf16[48,4992]{1,0:T(8,128)(2,1)S(1)}, bf16[48,4992]{1,0:T(8,128)(2,1)S(1)}, u32[]{:S(2)}, u32[]{:S(2)}) collective-permute-start(bf16[48,4992]{1,0:T(8,128)(2,1)S(1)} %constant_dynamic-update-slice_fusion.refs_9_), channel_id=1, source_target_pairs={{0,16},{1,17},{2,18},{3,19},{4,12},{5,13},{6,14},{7,15},{8,24},{9,... | collective-permute-start | bytes 1437704 | tf_op jit(solution)/shard_map/ppermute | solution.py:76
  23.8 15.9 %collective-permute-start.5 = (bf16[48,4992]{1,0:T(8,128)(2,1)S(1)}, bf16[48,4992]{1,0:T(8,128)(2,1)S(1)}, u32[]{:S(2)}, u32[]{:S(2)}) collective-permute-start(bf16[48,4992]{1,0:T(8,128)(2,1)S(1)} %constant_dynamic-update-slice_fusion.refs_9_), channel_id=1, source_target_pairs={{0,8},{1,9},{2,10},{3,11},{4,20},{5,21},{6,22},{7,23},{8,0},{9,1},... | collective-permute-start | bytes 1437704 | tf_op jit(solution)/shard_map/ppermute | solution.py:73
  25.3 14.4 %collective-permute-start = (bf16[1152,128]{1,0:T(8,128)(2,1)}, bf16[1152,128]{1,0:T(8,128)(2,1)S(1)}, u32[]{:S(2)}, u32[]{:S(2)}) collective-permute-start(bf16[1152,128]{1,0:T(8,128)(2,1)} %get-tuple-element.112), channel_id=1, source_target_pairs={{0,1},{1,0},{2,3},{3,2},{4,5},{5,4},{6,7},{7,6},{8,9},{9,8},{10,11... | collective-permute-start | bytes 884744 | tf_op jit(solution)/shard_map/ppermute | solution.py:85
  27.4 14.8 %collective-permute-start.1 = (bf16[1152,128]{1,0:T(8,128)(2,1)}, bf16[1152,128]{1,0:T(8,128)(2,1)S(1)}, u32[]{:S(2)}, u32[]{:S(2)}) collective-permute-start(bf16[1152,128]{1,0:T(8,128)(2,1)} %get-tuple-element.112), channel_id=1, source_target_pairs={{0,2},{1,3},{2,0},{3,1},{4,6},{5,7},{6,4},{7,5},{8,10},{9,11},{10,... | collective-permute-start | bytes 884744 | tf_op jit(solution)/shard_map/ppermute | solution.py:85
  39.7 9.1 %collective-permute-start.7 = (bf16[48,4992]{1,0:T(8,128)(2,1)S(1)}, bf16[48,4992]{1,0:T(8,128)(2,1)S(1)}, u32[]{:S(2)}, u32[]{:S(2)}) collective-permute-start(bf16[48,4992]{1,0:T(8,128)(2,1)S(1)} %collective-permute-done.5.refs_10_), channel_id=1, source_target_pairs={{0,16},{1,17},{2,18},{3,19},{4,12},{5,13},{6,14},{7,15},{8,24},{9,... | collective-permute-start | bytes 1437704 | tf_op jit(solution)/shard_map/ppermute | solution.py:76
  42.1 8.3 %collective-permute-start.8 = (bf16[48,4992]{1,0:T(8,128)(2,1)S(1)}, bf16[48,4992]{1,0:T(8,128)(2,1)S(1)}, u32[]{:S(2)}, u32[]{:S(2)}) collective-permute-start(bf16[48,4992]{1,0:T(8,128)(2,1)S(1)} %constant_dynamic-update-slice_fusion.refs_9_), channel_id=1, source_target_pairs={{0,4},{1,5},{2,6},{3,7},{4,0},{5,1},{6,2},{7,3},{8,12},{9,13},{10,... | collective-permute-start | bytes 1437704 | tf_op jit(solution)/shard_map/ppermute | solution.py:70
  43.5 9.7 %collective-permute-start.10 = (bf16[48,4992]{1,0:T(8,128)(2,1)S(1)}, bf16[48,4992]{1,0:T(8,128)(2,1)}, u32[]{:S(2)}, u32[]{:S(2)}) collective-permute-start(bf16[48,4992]{1,0:T(8,128)(2,1)S(1)} %collective-permute-done.6.refs_11_), channel_id=1, source_target_pairs={{0,4},{1,5},{2,6},{3,7},{4,0},{5,1},{6,2},{7,3},{8,12},{9,13},{10,... | collective-permute-start | bytes 1437704 | tf_op jit(solution)/shard_map/ppermute | solution.py:70
  44.1 9.2 %collective-permute-start.9 = (bf16[48,4992]{1,0:T(8,128)(2,1)S(1)}, bf16[48,4992]{1,0:T(8,128)(2,1)}, u32[]{:S(2)}, u32[]{:S(2)}) collective-permute-start(bf16[48,4992]{1,0:T(8,128)(2,1)S(1)} %collective-permute-done.5.refs_10_), channel_id=1, source_target_pairs={{0,4},{1,5},{2,6},{3,7},{4,0},{5,1},{6,2},{7,3},{8,12},{9,13},{10,... | collective-permute-start | bytes 1437704 | tf_op jit(solution)/shard_map/ppermute | solution.py:70
  49.9 26.9 %collective-permute-start.13 = (bf16[3,1152,128]{2,1,0:T(8,128)(2,1)}, bf16[3,1152,128]{2,1,0:T(8,128)(2,1)}, u32[]{:S(2)}, u32[]{:S(2)}) collective-permute-start(bf16[3,1152,128]{2,1,0:T(8,128)(2,1)} %pad_maximum_fusion.refs_7_), channel_id=1, source_target_pairs={{0,16},{1,17},{2,18},{3,19},{4,12},{5,13},{6,14},{7,15},{8,24},{9,... | collective-permute-start | bytes 2654216 | tf_op jit(solution)/shard_map/ppermute | solution.py:76
  50.5 26.4 %collective-permute-start.12 = (bf16[3,1152,128]{2,1,0:T(8,128)(2,1)}, bf16[3,1152,128]{2,1,0:T(8,128)(2,1)}, u32[]{:S(2)}, u32[]{:S(2)}) collective-permute-start(bf16[3,1152,128]{2,1,0:T(8,128)(2,1)} %pad_maximum_fusion.refs_7_), channel_id=1, source_target_pairs={{0,8},{1,9},{2,10},{3,11},{4,20},{5,21},{6,22},{7,23},{8,0},{9,1},... | collective-permute-start | bytes 2654216 | tf_op jit(solution)/shard_map/ppermute | solution.py:73
  76.9 13.9 %collective-permute-start.14 = (bf16[1024,768]{1,0:T(8,128)(2,1)}, bf16[1024,768]{1,0:T(8,128)(2,1)}, u32[]{:S(2)}, u32[]{:S(2)}) collective-permute-start(bf16[1024,768]{1,0:T(8,128)(2,1)} %get-tuple-element.120.refs_0_), channel_id=1, source_target_pairs={{0,4},{1,5},{2,6},{3,7},{4,0},{5,1},{6,2},{7,3},{8,12},{9,13},{10,... | collective-permute-start | bytes 4718600 | tf_op jit(solution)/shard_map/ppermute | solution.py:70
  77.0 13.9 %collective-permute-start.15 = (bf16[1024,768]{1,0:T(8,128)(2,1)}, bf16[1024,768]{1,0:T(8,128)(2,1)}, u32[]{:S(2)}, u32[]{:S(2)}) collective-permute-start(bf16[1024,768]{1,0:T(8,128)(2,1)} %get-tuple-element.121.refs_2_.gp), channel_id=1, source_target_pairs={{0,4},{1,5},{2,6},{3,7},{4,0},{5,1},{6,2},{7,3},{8,12},{9,13},{10,... | collective-permute-start | bytes 4718600 | tf_op jit(solution)/shard_map/ppermute | solution.py:70
  77.5 13.4 %collective-permute-start.16 = (bf16[3,1152,128]{2,1,0:T(8,128)(2,1)}, bf16[3,1152,128]{2,1,0:T(8,128)(2,1)}, u32[]{:S(2)}, u32[]{:S(2)}) collective-permute-start(bf16[3,1152,128]{2,1,0:T(8,128)(2,1)} %collective-permute-done.12.refs_8_), channel_id=1, source_target_pairs={{0,16},{1,17},{2,18},{3,19},{4,12},{5,13},{6,14},{7,15},{8,24},{9,... | collective-permute-start | bytes 2654216 | tf_op jit(solution)/shard_map/ppermute | solution.py:76
  137.0 30.5 %collective-permute-start.18 = (bf16[2,4,1152,128]{3,2,1,0:T(8,128)(2,1)}, bf16[2,4,1152,128]{3,2,1,0:T(8,128)(2,1)}, u32[]{:S(2)}, u32[]{:S(2)}) collective-permute-start(bf16[2,4,1152,128]{3,2,1,0:T(8,128)(2,1)} %get-tuple-element.130), channel_id=1, source_target_pairs={{0,8},{1,9},{2,10},{3,11},{4,20},{5,21},{6,22},{7,23},{8,0},{9,1},... | collective-permute-start | bytes 7077896 | tf_op jit(solution)/shard_map/ppermute | solution.py:73
  167.4 7.0 %collective-permute-start.21 = (bf16[2,2,4,24,2304]{4,3,2,1,0:T(8,128)(2,1)}, bf16[2,2,4,24,2304]{4,3,2,1,0:T(8,128)(2,1)}, u32[]{:S(2)}, u32[]{:S(2)}) collective-permute-start(bf16[2,2,4,24,2304]{4,3,2,1,0:T(8,128)(2,1)} %get-tuple-element.147), channel_id=1, source_target_pairs={{0,4},{1,5},{2,6},{3,7},{4,0},{5,1},{6,2},{7,3},{8,12},{9,13},{10,... | collective-permute-start | bytes 5308424 | tf_op jit(solution)/shard_map/ppermute | solution.py:70
  167.6 11.9 %collective-permute-start.17 = (bf16[1024,768]{1,0:T(8,128)(2,1)}, bf16[1024,768]{1,0:T(8,128)(2,1)}, u32[]{:S(2)}, u32[]{:S(2)}) collective-permute-start(bf16[1024,768]{1,0:T(8,128)(2,1)} %get-tuple-element.125), channel_id=1, source_target_pairs={{0,4},{1,5},{2,6},{3,7},{4,0},{5,1},{6,2},{7,3},{8,12},{9,13},{10,... | collective-permute-start | bytes 4718600 | tf_op jit(solution)/shard_map/ppermute | solution.py:70
  172.9 25.7 %collective-permute-start.20 = (bf16[1,48,96,128]{3,2,1,0:T(8,128)(2,1)}, bf16[1,48,96,128]{3,2,1,0:T(8,128)(2,1)}, u32[]{:S(2)}, u32[]{:S(2)}) collective-permute-start(bf16[1,48,96,128]{3,2,1,0:T(8,128)(2,1)} %get-tuple-element.144), channel_id=1, source_target_pairs={{0,16},{1,17},{2,18},{3,19},{4,12},{5,13},{6,14},{7,15},{8,24},{9,... | collective-permute-start | bytes 3538952 | tf_op jit(solution)/shard_map/ppermute | solution.py:76
  178.1 20.5 %collective-permute-start.22 = (bf16[1,8,24,2304]{3,2,1,0:T(8,128)(2,1)}, bf16[1,8,24,2304]{3,2,1,0:T(8,128)(2,1)}, u32[]{:S(2)}, u32[]{:S(2)}) collective-permute-start(bf16[1,8,24,2304]{3,2,1,0:T(8,128)(2,1)} %get-tuple-element.149), channel_id=1, source_target_pairs={{0,8},{1,9},{2,10},{3,11},{4,20},{5,21},{6,22},{7,23},{8,0},{9,1},... | collective-permute-start | bytes 2654216 | tf_op jit(solution)/shard_map/ppermute | solution.py:73
  202.8 15.7 %collective-permute-start.24 = (bf16[2,12,96,128]{3,2,1,0:T(8,128)(2,1)}, bf16[2,12,96,128]{3,2,1,0:T(8,128)(2,1)}, u32[]{:S(2)}, u32[]{:S(2)}) collective-permute-start(bf16[2,12,96,128]{3,2,1,0:T(8,128)(2,1)} %get-tuple-element.162), channel_id=1, source_target_pairs={{0,1},{1,0},{2,3},{3,2},{4,5},{5,4},{6,7},{7,6},{8,9},{9,8},{10,11... | collective-permute-start | bytes 1769480 | tf_op jit(solution)/shard_map/ppermute | solution.py:85
  203.1 8.6 %collective-permute-start.23 = (bf16[1,4,24,2304]{3,2,1,0:T(8,128)(2,1)}, bf16[1,4,24,2304]{3,2,1,0:T(8,128)(2,1)}, u32[]{:S(2)}, u32[]{:S(2)}) collective-permute-start(bf16[1,4,24,2304]{3,2,1,0:T(8,128)(2,1)} %get-tuple-element.156), channel_id=1, source_target_pairs={{0,16},{1,17},{2,18},{3,19},{4,12},{5,13},{6,14},{7,15},{8,24},{9,... | collective-permute-start | bytes 1327112 | tf_op jit(solution)/shard_map/ppermute | solution.py:76
  223.9 8.6 %collective-permute-start.26 = (bf16[1,8,24,1024]{3,2,1,0:T(8,128)(2,1)}, bf16[1,8,24,1024]{3,2,1,0:T(8,128)(2,1)}, u32[]{:S(2)}, u32[]{:S(2)}) collective-permute-start(bf16[1,8,24,1024]{3,2,1,0:T(8,128)(2,1)} %get-tuple-element.170), channel_id=1, source_target_pairs={{0,8},{1,9},{2,10},{3,11},{4,20},{5,21},{6,22},{7,23},{8,0},{9,1},... | collective-permute-start | bytes 1179656 | tf_op jit(solution)/shard_map/ppermute | solution.py:73
  225.5 17.2 %collective-permute-start.30 = (bf16[1,12,96,128]{3,2,1,0:T(8,128)(2,1)}, bf16[1,12,96,128]{3,2,1,0:T(8,128)(2,1)}, u32[]{:S(2)}, u32[]{:S(2)}) collective-permute-start(bf16[1,12,96,128]{3,2,1,0:T(8,128)(2,1)} %get-tuple-element.168), channel_id=1, source_target_pairs={{0,2},{1,3},{2,0},{3,1},{4,6},{5,7},{6,4},{7,5},{8,10},{9,11},{10,... | collective-permute-start | bytes 884744 | tf_op jit(solution)/shard_map/ppermute | solution.py:85
  225.5 12.1 %collective-permute-start.28 = (bf16[2,1,24,2304]{3,2,0,1:T(8,128)(2,1)}, bf16[2,1,24,2304]{3,2,0,1:T(8,128)(2,1)}, u32[]{:S(2)}, u32[]{:S(2)}) collective-permute-start(bf16[2,1,24,2304]{3,2,0,1:T(8,128)(2,1)} %bitcast.59), channel_id=1, source_target_pairs={{0,1},{1,0},{2,3},{3,2},{4,5},{5,4},{6,7},{7,6},{8,9},{9,8},{10,11... | collective-permute-start | bytes 663560 | tf_op jit(solution)/shard_map/ppermute | solution.py:85
  244.5 16.3 %collective-permute-start.35 = (bf16[1152,128]{1,0:T(8,128)(2,1)}, bf16[1152,128]{1,0:T(8,128)(2,1)}, u32[]{:S(2)}, u32[]{:S(2)}) collective-permute-start(bf16[1152,128]{1,0:T(8,128)(2,1)} %bitcast.37.refs_0_), channel_id=1, source_target_pairs={{0,24},{1,25},{2,26},{3,27},{4,28},{5,29},{6,30},{7,31},{8,16},{9,... | collective-permute-start | bytes 884744 | tf_op jit(solution)/shard_map/ppermute | solution.py:88
  247.3 13.8 %collective-permute-start.34 = (bf16[1152,128]{1,0:T(8,128)(2,1)}, bf16[1152,128]{1,0:T(8,128)(2,1)}, u32[]{:S(2)}, u32[]{:S(2)}) collective-permute-start(bf16[1152,128]{1,0:T(8,128)(2,1)} %bitcast.37.refs_0_), channel_id=1, source_target_pairs={{0,16},{1,17},{2,18},{3,19},{4,12},{5,13},{6,14},{7,15},{8,24},{9,... | collective-permute-start | bytes 884744 | tf_op jit(solution)/shard_map/ppermute | solution.py:76
  247.8 13.3 %collective-permute-start.33 = (bf16[1152,128]{1,0:T(8,128)(2,1)}, bf16[1152,128]{1,0:T(8,128)(2,1)}, u32[]{:S(2)}, u32[]{:S(2)}) collective-permute-start(bf16[1152,128]{1,0:T(8,128)(2,1)} %bitcast.37.refs_0_), channel_id=1, source_target_pairs={{0,8},{1,9},{2,10},{3,11},{4,20},{5,21},{6,22},{7,23},{8,0},{9,1},... | collective-permute-start | bytes 884744 | tf_op jit(solution)/shard_map/ppermute | solution.py:73
  248.4 12.7 %collective-permute-start.31 = (bf16[1,1,24,2304]{3,2,1,0:T(8,128)(2,1)}, bf16[1,1,24,2304]{3,2,1,0:T(8,128)(2,1)}, u32[]{:S(2)}, u32[]{:S(2)}) collective-permute-start(bf16[1,1,24,2304]{3,2,1,0:T(8,128)(2,1)} %get-tuple-element.187), channel_id=1, source_target_pairs={{0,2},{1,3},{2,0},{3,1},{4,6},{5,7},{6,4},{7,5},{8,10},{9,11},{10,... | collective-permute-start | bytes 331784 | tf_op jit(solution)/shard_map/ppermute | solution.py:85
  263.8 8.2 %collective-permute-start.38 = (bf16[24,3328]{1,0:T(8,128)(2,1)}, bf16[24,3328]{1,0:T(8,128)(2,1)}, u32[]{:S(2)}, u32[]{:S(2)}) collective-permute-start(bf16[24,3328]{1,0:T(8,128)(2,1)} %add_convert_fusion.1.refs_0_), channel_id=1, source_target_pairs={{0,24},{1,25},{2,26},{3,27},{4,28},{5,29},{6,30},{7,31},{8,16},{9,... | collective-permute-start | bytes 479240 | tf_op jit(solution)/shard_map/ppermute | solution.py:88
  265.5 9.0 %collective-permute-start.37 = (bf16[24,3328]{1,0:T(8,128)(2,1)}, bf16[24,3328]{1,0:T(8,128)(2,1)}, u32[]{:S(2)}, u32[]{:S(2)}) collective-permute-start(bf16[24,3328]{1,0:T(8,128)(2,1)} %add_convert_fusion.1.refs_0_), channel_id=1, source_target_pairs={{0,16},{1,17},{2,18},{3,19},{4,12},{5,13},{6,14},{7,15},{8,24},{9,... | collective-permute-start | bytes 479240 | tf_op jit(solution)/shard_map/ppermute | solution.py:76
  266.4 8.0 %collective-permute-start.36 = (bf16[24,3328]{1,0:T(8,128)(2,1)}, bf16[24,3328]{1,0:T(8,128)(2,1)}, u32[]{:S(2)}, u32[]{:S(2)}) collective-permute-start(bf16[24,3328]{1,0:T(8,128)(2,1)} %add_convert_fusion.1.refs_0_), channel_id=1, source_target_pairs={{0,8},{1,9},{2,10},{3,11},{4,20},{5,21},{6,22},{7,23},{8,0},{9,1},... | collective-permute-start | bytes 479240 | tf_op jit(solution)/shard_map/ppermute | solution.py:73
  (20 other events, 118.8 us)

commit v3 on v2

--- a/solution.py
+++ b/solution.py
@@ -235,13 +235,22 @@
         copies = mixed_copies(meta, shard, blocks, w, sems)
         for cp in copies:
             cp.start()
-        for cp in copies:
+        dbf_o[...] = jnp.zeros_like(dbf_o)
+
+    x = jnp.concatenate([r[...] for r in tok], axis=0).astype(F32)
+    g = jnp.concatenate([r[...] for r in cot], axis=0)
+    gp_o[...] = g
+    dbf_o[0:1] += jnp.sum(g.astype(F32), axis=0, keepdims=True)
+    n1, _ = norm_stats(x)
+
+    @pl.when(b == 0)
+    def _():
+        for cp in mixed_copies(meta, shard, blocks, w, sems):
             cp.wait()
         pltpu.make_async_copy(w, w_o, out_sem).start()
         ext = w[:, 4 * d : 4 * d + 128].astype(F32).T
         vec[...] = ext[0:16]
         vec_o[...] = ext[0:16]
-        dbf_o[...] = jnp.zeros_like(dbf_o)
         rows = d // 4
         for zz in range(4):
             for r in range(b1_o.shape[1] // 128):
@@ -251,11 +260,6 @@
 
     g1, s1, b_out = vec[0:1], vec[1:2], vec[2:3]
     g2, s2 = vec[3:4], vec[4:5]
-    x = jnp.concatenate([r[...] for r in tok], axis=0).astype(F32)
-    g = jnp.concatenate([r[...] for r in cot], axis=0)
-    gp_o[...] = g
-    dbf_o[0:1] += jnp.sum(g.astype(F32), axis=0, keepdims=True)
-    n1, _ = norm_stats(x)
     a1 = (n1 * g1 + s1).astype(BF16)
     a1_o[...] = a1
     for k in range(3):

time: 281 us -> 281 us (level)
  no operation moved by 1% of the time
where the time goes in v3:
time: 281 us; the launch traced here: 280 us
  Pallas kernels  161 us (57%)
  waiting for transfers between devices  66.8 us (24%)
  starting transfers between devices  43.2 us (15%)
  other arithmetic  6.3 us (2%)
    pallas_call x1, Pallas kernels, mlp(): pl.pallas_call(functools.partial(mlp_body, ng, go, first), grid_spec=pltp...  46.2 us
    ppermute x9, waiting for transfers between devices, z_flip(): return lax.ppermute(a, ALL, self.table(lambda d, z: (d, z ^ bit)))  29.2 us
    pallas_call x8, Pallas kernels, halve(): pl.pallas_call(functools.partial(halve_body, tuple(((p, len(ks), ks[0].sh...  24.1 us
    pallas_call x1, Pallas kernels, k1(): pl.pallas_call(k1_body, grid_spec=pltpu.PrefetchScalarGridSpec(num_scalar...  23.7 us
    ppermute x9, waiting for transfers between devices, second(): lax.ppermute(a, ALL, self.table(lambda d, z: (d ^ (4 if d % 2 == 0 else 2...  19.9 us
    pallas_call x1, Pallas kernels, back_late(): pl.pallas_call(back_late_body, grid_spec=pltpu.PrefetchScalarGridSpec(num...  19 us
    pallas_call x1, Pallas kernels, back_early(): pl.pallas_call(back_early_body, grid=(t // BLOCK,), in_specs=[blk(d), blk...  16.1 us
    pallas_call x2, Pallas kernels, grads(): pl.pallas_call(body, grid_spec=pltpu.PrefetchScalarGridSpec(num_scalar_pr...  15.3 us
  transfers between devices with their start and end apart: 47, of which 20 were waited for; matrix products, arithmetic and copies ran while one was open for 2% of the time, Pallas kernels for 36%

profile of v3, /device:TPU:0, one launch (start us, length us, event | category | flops | bytes accessed | tf_op | source)
XLA Modules:
  0.0 280.1 jit_solution(3258014659857272507)
XLA Ops:
  0.7 3.9 %pack.1 = (bf16[192,3328]{1,0:T(8,128)(2,1)}, bf16[48,3328]{1,0:T(8,128)(2,1)}, bf16[48,1664]{1,0:T(8,128)(2,1)}, bf16[1152,128]{1,0:T(8,128)(2,1)}) custom-call(s32[1]{0:T(128)} %bitcast.9.pos, bf16[192,2304]{1,0:T(8,128)(2,1)} %refs_0_.3, bf16[192,768]{1,0:T(8,128)(2,1)} %refs_1_.3, bf16[192]{0:T(256)(128)(2,1)} %refs_2_.3, bf16[192]{0:T(256)(128)(2,1)} %refs_3_.3, ...), custom_call_target="tpu_custom_call" | custom-call | tf_op jit(solution)/shard_map/pack/pallas_call | solution.py:194
  4.5 3.1 %collective-permute-start.3 = (bf16[48,3328]{1,0:T(8,128)(2,1)}, bf16[48,3328]{1,0:T(8,128)(2,1)S(1)}, u32[]{:S(2)}, u32[]{:S(2)}) collective-permute-start(bf16[48,3328]{1,0:T(8,128)(2,1)} %get-tuple-element.114), channel_id=1, source_target_pairs={{0,1},{1,2},{2,3},{3,0},{4,7},{5,4},{6,5},{7,6},{8,9},{9,10},{10,1... | collective-permute-start | bytes 958472 | tf_op jit(solution)/shard_map/ppermute | solution.py:79
  7.6 2.6 collective-permute-start.4
  10.2 8.1 %collective-permute-done.3 = bf16[48,3328]{1,0:T(8,128)(2,1)S(1)} collective-permute-done((bf16[48,3328]{1,0:T(8,128)(2,1)}, bf16[48,3328]{1,0:T(8,128)(2,1)S(1)}, u32[]{:S(2)}, u32[]{:S(2)}) %collective-permute-start.3) | collective-permute-done | bytes 319520 | tf_op jit(solution)/shard_map/ppermute | solution.py:79
  18.4 3.7 %collective-permute-done.4 = bf16[48,1664]{1,0:T(8,128)(2,1)S(1)} collective-permute-done((bf16[48,1664]{1,0:T(8,128)(2,1)}, bf16[48,1664]{1,0:T(8,128)(2,1)S(1)}, u32[]{:S(2)}, u32[]{:S(2)}) %collective-permute-start.4) | collective-permute-done | bytes 159776 | tf_op jit(solution)/shard_map/ppermute | solution.py:82
  27.4 3.3 %collective-permute-start.1 = (bf16[1152,128]{1,0:T(8,128)(2,1)}, bf16[1152,128]{1,0:T(8,128)(2,1)S(1)}, u32[]{:S(2)}, u32[]{:S(2)}) collective-permute-start(bf16[1152,128]{1,0:T(8,128)(2,1)} %get-tuple-element.112), channel_id=1, source_target_pairs={{0,2},{1,3},{2,0},{3,1},{4,6},{5,7},{6,4},{7,5},{8,10},{9,11},{10,... | collective-permute-start | bytes 884744 | tf_op jit(solution)/shard_map/ppermute | solution.py:85
  31.5 8.2 %collective-permute-done = bf16[1152,128]{1,0:T(8,128)(2,1)S(1)} collective-permute-done((bf16[1152,128]{1,0:T(8,128)(2,1)}, bf16[1152,128]{1,0:T(8,128)(2,1)S(1)}, u32[]{:S(2)}, u32[]{:S(2)}) %collective-permute-start) | collective-permute-done | bytes 294944 | tf_op jit(solution)/shard_map/ppermute | solution.py:85
  44.2 4.7 %collective-permute-done.2 = bf16[1152,128]{1,0:T(8,128)(2,1)S(1)} collective-permute-done((bf16[1152,128]{1,0:T(8,128)(2,1)S(1)}, bf16[1152,128]{1,0:T(8,128)(2,1)S(1)}, u32[]{:S(2)}, u32[]{:S(2)}) %collective-permute-start.2) | collective-permute-done | bytes 294944 | tf_op jit(solution)/shard_map/ppermute | solution.py:85
  53.3 23.7 %norm_qkv_attend.1 = (bf16[1024,2304]{1,0:T(8,128)(2,1)}, bf16[4,12,256,256]{3,2,1,0:T(8,128)(2,1)}, f32[1024,768]{1,0:T(8,128)}, bf16[1024,768]{1,0:T(8,128)(2,...) custom-call(s32[26]{0:T(128)} %concatenate.12.meta, ...), custom_call_target="tpu_custom_call" | custom-call | flops 6039797760 | bytes 41943040 | tf_op jit(solution)/shard_map/norm_qkv_attend/pallas_call | solution.py:310
  79.1 11.8 %collective-permute-done.16.refs_10_ = bf16[3,1152,128]{2,1,0:T(8,128)(2,1)} collective-permute-done((bf16[3,1152,128]{2,1,0:T(8,128)(2,1)}, bf16[3,1152,128]{2,1,0:T(8,128)(2,1)}, u32[]{:S(2)}, u32[]{:S(2)}) %collective-permute-start.16) | collective-permute-done | bytes 884768 | tf_op jit(solution)/shard_map/ppermute | solution.py:76
  90.9 46.2 %hidden_first.1 = (bf16[1024,768]{1,0:T(8,128)(2,1)}, bf16[1024,768]{1,0:T(8,128)(2,1)}, bf16[1024,768]{1,0:T(8,128)(2,1)}, bf16[1024,768]{1,0:T(8,128)(2,1)}, b...) custom-call(s32[26]{0:T(128)} %concatenate.12.meta, ...), custom_call_target="tpu_custom_call" | custom-call | flops 28991029248 | bytes 31457280 | tf_op jit(solution)/shard_map/hidden_first/pallas_call | solution.py:485
  137.8 3.7 %collective-permute-done.19.da_p = bf16[1024,768]{1,0:T(8,128)(2,1)} collective-permute-done((bf16[1024,768]{1,0:T(8,128)(2,1)}, bf16[1024,768]{1,0:T(8,128)(2,1)}, u32[]{:S(2)}, u32[]{:S(2)}) %collective-permute-start.19) | collective-permute-done | bytes 1572896 | tf_op jit(solution)/shard_map/ppermute | solution.py:70
  141.5 16.1 %attend_back_early.1 = (f32[1024,768]{1,0:T(8,128)}, bf16[1024,768]{1,0:T(8,128)(2,1)}, bf16[1024,1536]{1,0:T(8,128)(2,1)}, f32[128,768]{1,0:T(8,128)}) custom-call(bf16[1024,768]{1,0:T(8,128)(2,1)} %get-tuple-element.121.refs_2_.gp, bf16[1024,768]{1,0:T(8,128)(2,1)} %get-tuple-element.131.da_o, bf16[1024,768]{1,0:T(8,128)(2,1)} %collective-permute-done.19.da_p, ...), custom_call_target="tpu_custom_call" | custom-call | flops 4831838208 | bytes 25165824 | tf_op jit(solution)/shard_map/attend_back_early/pallas_call | solution.py:560
  157.6 9.9 %weight_grads.2 = (bf16[2,2,4,24,2304]{4,3,2,1,0:T(8,128)(2,1)}, bf16[2,2,4,24,2304]{4,3,2,1,0:T(8,128)(2,1)}) custom-call(s32[26]{0:T(128)} %concatenate.12.meta, bf16[1024,768]{1,0:T(8,128)(2,1)} %get-tuple-element.157.a1, bf16[1024,1536]{1,0:T(8,128)(2,1)} %get-tuple-element.139.dq.refs_6_, bf16[1024,768]{1,0:T(8,128)(2,1)} %get-tuple-element.135.o.refs_9_, ...), custom_call_target="tpu_custom_call" | custom-call | flops 1 | bytes 1 | tf_op jit(solution)/shard_map/weight_grads/pallas_call | solution.py:709
  168.0 4.9 %add_halve.8 = (bf16[1,48,96,128]{3,2,1,0:T(8,128)(2,1)}, bf16[1,48,96,128]{3,2,1,0:T(8,128)(2,1)}) custom-call(s32[26]{0:T(128)} %concatenate.12.meta, bf16[1,2,48,96,128]{4,3,2,1,0:T(8,128)(2,1)} %bitcast.42, bf16[1,2,48,96,128]{4,3,2,1,0:T(8,128)(2,1)} %bitcast.14.refs_1_), custom_call_target="tpu_custom_call" | custom-call | flops 1179648 | bytes 7077888 | tf_op jit(solution)/shard_map/add_halve/pallas_call | solution.py:806
  174.5 3.7 %add_halve.9 = (bf16[1,8,24,2304]{3,2,1,0:T(8,128)(2,1)}, bf16[1,8,24,2304]{3,2,1,0:T(8,128)(2,1)}) custom-call(s32[26]{0:T(128)} %concatenate.12.meta, bf16[1,2,8,24,2304]{4,3,2,1,0:T(8,128)(2,1)} %bitcast.43, bf16[1,2,8,24,2304]{4,3,2,1,0:T(8,128)(2,1)} %bitcast.17.refs_1_), custom_call_target="tpu_custom_call" | custom-call | flops 884736 | bytes 5308416 | tf_op jit(solution)/shard_map/add_halve/pallas_call | solution.py:806
  179.6 19.0 %attend_back_late.1 = (f32[1024,768]{1,0:T(8,128)}, bf16[1024,768]{1,0:T(8,128)(2,1)}, f32[128,768]{1,0:T(8,128)}) custom-call(s32[26]{0:T(128)} %concatenate.12.meta, bf16[1024,768]{1,0:T(8,128)(2,1)} %refs_3_.5, bf16[1024,768]{1,0:T(8,128)(2,1)} %refs_3_.5, bf16[1024,768]{1,0:T(8,128)(2,1)} %refs_3_.5, bf16[1024,768]{1,0:T(8,128)(2,1)} %refs_3_.5, ...), custom_call_target="tpu_custom_call" | custom-call | flops 6039797760 | bytes 20971520 | tf_op jit(solution)/shard_map/attend_back_late/pallas_call | solution.py:633
  198.7 4.2 %add_halve.10 = (bf16[2,12,96,128]{3,2,1,0:T(8,128)(2,1)}, bf16[2,12,96,128]{3,2,1,0:T(8,128)(2,1)}, bf16[1,4,24,2304]{3,2,1,0:T(8,128)(2,1)}, bf16[1,4,24,2304]{3,2,1,0:T(8,128)(2,1)}) custom-call(s32[26]{0:T(128)} %concatenate.12.meta, bf16[2,2,12,96,128]{4,3,2,1,0:T(8,128)(2,1)} %bitcast.44, bf16[2,2,12,96,128]{4,3,2,1,0:T(8,128)(2,1)} %bitcast.18.refs_1_, ...), custom_call_target="tpu_custom_call" | custom-call | flops 1032192 | bytes 6193152 | tf_op jit(solution)/shard_map/add_halve/pallas_call | solution.py:806
  204.1 5.3 %weight_grads.3 = (bf16[2,2,4,24,1024]{4,3,2,1,0:T(8,128)(2,1)}, bf16[2,2,4,24,1024]{4,3,2,1,0:T(8,128)(2,1)}) custom-call(s32[26]{0:T(128)} %concatenate.12.meta, bf16[1024,768]{1,0:T(8,128)(2,1)} %get-tuple-element.157.a1, bf16[1024,768]{1,0:T(8,128)(2,1)} %get-tuple-element.158.dq, f32[128,768]{1,0:T(8,128)} %get-tuple-element.152.acc, ...), custom_call_target="tpu_custom_call" | custom-call | flops 1207959552 | bytes 12582912 | tf_op jit(solution)/shard_map/weight_grads/pallas_call | solution.py:709
  209.4 2.4 collective-permute-done.23
  211.8 6.8 %collective-permute-done.24 = bf16[2,12,96,128]{3,2,1,0:T(8,128)(2,1)} collective-permute-done((bf16[2,12,96,128]{3,2,1,0:T(8,128)(2,1)}, bf16[2,12,96,128]{3,2,1,0:T(8,128)(2,1)}, u32[]{:S(2)}, u32[]{:S(2)}) %collective-permute-start.24) | collective-permute-done | bytes 589856 | tf_op jit(solution)/shard_map/ppermute | solution.py:85
  218.6 2.9 %add_halve.11 = (bf16[2,1,24,2304]{3,2,1,0:T(8,128)(2,1)}, bf16[2,1,24,2304]{3,2,1,0:T(8,128)(2,1)}, bf16[1,12,96,128]{3,2,1,0:T(8,128)(2,1)}, bf16[1,12,96,128]{3,2,1,0:T(8,128)(2,1)}) custom-call(s32[26]{0:T(128)} %concatenate.12.meta, bf16[2,2,1,24,2304]{4,3,2,1,0:T(8,128)(2,1)} %bitcast.48, bf16[2,2,1,24,2304]{4,3,2,1,0:T(8,128)(2,1)} %bitcast.23.refs_1_, ...), custom_call_target="tpu_custom_call" | custom-call | flops 516096 | bytes 3096576 | tf_op jit(solution)/shard_map/add_halve/pallas_call | solution.py:806
  221.5 2.5 add_halve.12
  227.2 5.4 %layer_out.1 = bf16[1024,768]{1,0:T(8,128)(2,1)} custom-call(s32[26]{0:T(128)} %concatenate.12.meta, bf16[1024,768]{1,0:T(8,128)(2,1)} %get-tuple-element.124.ya, bf16[1024,768]{1,0:T(8,128)(2,1)} %collective-permute-done.17.yb, f32[1024,768]{1,0:T(8,128)} %get-tuple-element.126.x1_r.x1, f32[16,768]{1,0:T(8,128)} %get-tuple-element.171.vec.refs_12_), custom_call_target="tpu_custom_call" | custom-call | flops 3145728 | bytes 8388608 | tf_op jit(solution)/shard_map/layer_out/pallas_call | solution.py:760
  237.7 3.1 %collective-permute-done.27 = bf16[1,4,24,1024]{3,2,1,0:T(8,128)(2,1)} collective-permute-done((bf16[1,4,24,1024]{3,2,1,0:T(8,128)(2,1)}, bf16[1,4,24,1024]{3,2,1,0:T(8,128)(2,1)}, u32[]{:S(2)}, u32[]{:S(2)}) %collective-permute-start.27) | collective-permute-done | bytes 196640 | tf_op jit(solution)/shard_map/ppermute | solution.py:76
  244.6 2.7 collective-permute-start.35
  248.5 2.9 %collective-permute-start.31 = (bf16[1,1,24,2304]{3,2,1,0:T(8,128)(2,1)}, bf16[1,1,24,2304]{3,2,1,0:T(8,128)(2,1)}, u32[]{:S(2)}, u32[]{:S(2)}) collective-permute-start(bf16[1,1,24,2304]{3,2,1,0:T(8,128)(2,1)} %get-tuple-element.187), channel_id=1, source_target_pairs={{0,2},{1,3},{2,0},{3,1},{4,6},{5,7},{6,4},{7,5},{8,10},{9,11},{10,... | collective-permute-start | bytes 331784 | tf_op jit(solution)/shard_map/ppermute | solution.py:85
  251.5 2.3 collective-permute-done.29
  256.8 4.2 %collective-permute-done.32 = bf16[1,1,24,1024]{3,2,1,0:T(8,128)(2,1)S(1)} collective-permute-done((bf16[1,1,24,1024]{3,2,1,0:T(8,128)(2,1)}, bf16[1,1,24,1024]{3,2,1,0:T(8,128)(2,1)S(1)}, u32[]{:S(2)}, u32[]{:S(2)}) %collective-permute-start.32) | collective-permute-done | bytes 49184 | tf_op jit(solution)/shard_map/ppermute | solution.py:85
  267.4 4.2 %place_sums.2 = (f32[192,3072]{1,0:T(8,128)}, f32[768,768]{1,0:T(8,128)}) custom-call(s32[26]{0:T(128)} %concatenate.12.meta, bf16[1152,128]{1,0:T(8,128)(2,1)} %bitcast.37.refs_0_, bf16[1152,128]{1,0:T(8,128)(2,1)} %collective-permute-done.33.refs_1_, bf16[1152,128]{1,0:T(8,128)(2,1)} %collective-permute-done.34.refs_2_, ...), custom_call_target="tpu_custom_call" | custom-call | tf_op jit(solution)/shard_map/place_sums/pallas_call | solution.py:881
  272.1 2.5 collective-permute-done.37.refs_2_
  277.0 2.9 %place_sums.3 = (f32[192,2304]{1,0:T(8,128)}, f32[192,768]{1,0:T(8,128)}, f32[192]{0:T(256)}, f32[192]{0:T(256)}, f32[192]{0:T(256)}, /*index=5*/f32[192]{0:T(256)}, f32[192]{0:T(256)}, f32[192]{0:T(256)}, f32[768]{0:T(1024)}) custom-call(s32[26]{0:T(128)} %concatenate.12.meta, bf16[24,3328]{1,0:T(8,128)(2,1)} %add_convert_fusion.1.refs_0_, ...), custom_call_target="tpu_custom_call" | custom-call | tf_op jit(solution)/shard_map/place_sums/pallas_call | solution.py:881
  (104 shorter events, 47.5 us)
Async XLA Ops:
  4.5 13.8 %collective-permute-start.3 = (bf16[48,3328]{1,0:T(8,128)(2,1)}, bf16[48,3328]{1,0:T(8,128)(2,1)S(1)}, u32[]{:S(2)}, u32[]{:S(2)}) collective-permute-start(bf16[48,3328]{1,0:T(8,128)(2,1)} %get-tuple-element.114), channel_id=1, source_target_pairs={{0,1},{1,2},{2,3},{3,0},{4,7},{5,4},{6,5},{7,6},{8,9},{9,10},{10,1... | collective-permute-start | bytes 958472 | tf_op jit(solution)/shard_map/ppermute | solution.py:79
  7.6 14.5 %collective-permute-start.4 = (bf16[48,1664]{1,0:T(8,128)(2,1)}, bf16[48,1664]{1,0:T(8,128)(2,1)S(1)}, u32[]{:S(2)}, u32[]{:S(2)}) collective-permute-start(bf16[48,1664]{1,0:T(8,128)(2,1)} %get-tuple-element.115), channel_id=1, source_target_pairs={{0,2},{1,3},{2,0},{3,1},{4,6},{5,7},{6,4},{7,5},{8,10},{9,11},{10,... | collective-permute-start | bytes 479240 | tf_op jit(solution)/shard_map/ppermute | solution.py:82
  22.2 17.6 %collective-permute-start.6 = (bf16[48,4992]{1,0:T(8,128)(2,1)S(1)}, bf16[48,4992]{1,0:T(8,128)(2,1)S(1)}, u32[]{:S(2)}, u32[]{:S(2)}) collective-permute-start(bf16[48,4992]{1,0:T(8,128)(2,1)S(1)} %constant_dynamic-update-slice_fusion.refs_9_), channel_id=1, source_target_pairs={{0,16},{1,17},{2,18},{3,19},{4,12},{5,13},{6,14},{7,15},{8,24},{9,... | collective-permute-start | bytes 1437704 | tf_op jit(solution)/shard_map/ppermute | solution.py:76
  23.8 15.9 %collective-permute-start.5 = (bf16[48,4992]{1,0:T(8,128)(2,1)S(1)}, bf16[48,4992]{1,0:T(8,128)(2,1)S(1)}, u32[]{:S(2)}, u32[]{:S(2)}) collective-permute-start(bf16[48,4992]{1,0:T(8,128)(2,1)S(1)} %constant_dynamic-update-slice_fusion.refs_9_), channel_id=1, source_target_pairs={{0,8},{1,9},{2,10},{3,11},{4,20},{5,21},{6,22},{7,23},{8,0},{9,1},... | collective-permute-start | bytes 1437704 | tf_op jit(solution)/shard_map/ppermute | solution.py:73
  25.3 14.4 %collective-permute-start = (bf16[1152,128]{1,0:T(8,128)(2,1)}, bf16[1152,128]{1,0:T(8,128)(2,1)S(1)}, u32[]{:S(2)}, u32[]{:S(2)}) collective-permute-start(bf16[1152,128]{1,0:T(8,128)(2,1)} %get-tuple-element.112), channel_id=1, source_target_pairs={{0,1},{1,0},{2,3},{3,2},{4,5},{5,4},{6,7},{7,6},{8,9},{9,8},{10,11... | collective-permute-start | bytes 884744 | tf_op jit(solution)/shard_map/ppermute | solution.py:85
  27.4 14.8 %collective-permute-start.1 = (bf16[1152,128]{1,0:T(8,128)(2,1)}, bf16[1152,128]{1,0:T(8,128)(2,1)S(1)}, u32[]{:S(2)}, u32[]{:S(2)}) collective-permute-start(bf16[1152,128]{1,0:T(8,128)(2,1)} %get-tuple-element.112), channel_id=1, source_target_pairs={{0,2},{1,3},{2,0},{3,1},{4,6},{5,7},{6,4},{7,5},{8,10},{9,11},{10,... | collective-permute-start | bytes 884744 | tf_op jit(solution)/shard_map/ppermute | solution.py:85
  39.7 9.1 %collective-permute-start.7 = (bf16[48,4992]{1,0:T(8,128)(2,1)S(1)}, bf16[48,4992]{1,0:T(8,128)(2,1)S(1)}, u32[]{:S(2)}, u32[]{:S(2)}) collective-permute-start(bf16[48,4992]{1,0:T(8,128)(2,1)S(1)} %collective-permute-done.5.refs_10_), channel_id=1, source_target_pairs={{0,16},{1,17},{2,18},{3,19},{4,12},{5,13},{6,14},{7,15},{8,24},{9,... | collective-permute-start | bytes 1437704 | tf_op jit(solution)/shard_map/ppermute | solution.py:76
  42.1 8.3 %collective-permute-start.8 = (bf16[48,4992]{1,0:T(8,128)(2,1)S(1)}, bf16[48,4992]{1,0:T(8,128)(2,1)S(1)}, u32[]{:S(2)}, u32[]{:S(2)}) collective-permute-start(bf16[48,4992]{1,0:T(8,128)(2,1)S(1)} %constant_dynamic-update-slice_fusion.refs_9_), channel_id=1, source_target_pairs={{0,4},{1,5},{2,6},{3,7},{4,0},{5,1},{6,2},{7,3},{8,12},{9,13},{10,... | collective-permute-start | bytes 1437704 | tf_op jit(solution)/shard_map/ppermute | solution.py:70
  43.5 9.7 %collective-permute-start.10 = (bf16[48,4992]{1,0:T(8,128)(2,1)S(1)}, bf16[48,4992]{1,0:T(8,128)(2,1)}, u32[]{:S(2)}, u32[]{:S(2)}) collective-permute-start(bf16[48,4992]{1,0:T(8,128)(2,1)S(1)} %collective-permute-done.6.refs_11_), channel_id=1, source_target_pairs={{0,4},{1,5},{2,6},{3,7},{4,0},{5,1},{6,2},{7,3},{8,12},{9,13},{10,... | collective-permute-start | bytes 1437704 | tf_op jit(solution)/shard_map/ppermute | solution.py:70
  44.1 9.2 %collective-permute-start.9 = (bf16[48,4992]{1,0:T(8,128)(2,1)S(1)}, bf16[48,4992]{1,0:T(8,128)(2,1)}, u32[]{:S(2)}, u32[]{:S(2)}) collective-permute-start(bf16[48,4992]{1,0:T(8,128)(2,1)S(1)} %collective-permute-done.5.refs_10_), channel_id=1, source_target_pairs={{0,4},{1,5},{2,6},{3,7},{4,0},{5,1},{6,2},{7,3},{8,12},{9,13},{10,... | collective-permute-start | bytes 1437704 | tf_op jit(solution)/shard_map/ppermute | solution.py:70
  49.9 27.0 %collective-permute-start.13 = (bf16[3,1152,128]{2,1,0:T(8,128)(2,1)}, bf16[3,1152,128]{2,1,0:T(8,128)(2,1)}, u32[]{:S(2)}, u32[]{:S(2)}) collective-permute-start(bf16[3,1152,128]{2,1,0:T(8,128)(2,1)} %pad_maximum_fusion.refs_7_), channel_id=1, source_target_pairs={{0,16},{1,17},{2,18},{3,19},{4,12},{5,13},{6,14},{7,15},{8,24},{9,... | collective-permute-start | bytes 2654216 | tf_op jit(solution)/shard_map/ppermute | solution.py:76
  50.5 26.5 %collective-permute-start.12 = (bf16[3,1152,128]{2,1,0:T(8,128)(2,1)}, bf16[3,1152,128]{2,1,0:T(8,128)(2,1)}, u32[]{:S(2)}, u32[]{:S(2)}) collective-permute-start(bf16[3,1152,128]{2,1,0:T(8,128)(2,1)} %pad_maximum_fusion.refs_7_), channel_id=1, source_target_pairs={{0,8},{1,9},{2,10},{3,11},{4,20},{5,21},{6,22},{7,23},{8,0},{9,1},... | collective-permute-start | bytes 2654216 | tf_op jit(solution)/shard_map/ppermute | solution.py:73
  77.0 13.9 %collective-permute-start.14 = (bf16[1024,768]{1,0:T(8,128)(2,1)}, bf16[1024,768]{1,0:T(8,128)(2,1)}, u32[]{:S(2)}, u32[]{:S(2)}) collective-permute-start(bf16[1024,768]{1,0:T(8,128)(2,1)} %get-tuple-element.120.refs_0_), channel_id=1, source_target_pairs={{0,4},{1,5},{2,6},{3,7},{4,0},{5,1},{6,2},{7,3},{8,12},{9,13},{10,... | collective-permute-start | bytes 4718600 | tf_op jit(solution)/shard_map/ppermute | solution.py:70
  77.1 13.9 %collective-permute-start.15 = (bf16[1024,768]{1,0:T(8,128)(2,1)}, bf16[1024,768]{1,0:T(8,128)(2,1)}, u32[]{:S(2)}, u32[]{:S(2)}) collective-permute-start(bf16[1024,768]{1,0:T(8,128)(2,1)} %get-tuple-element.121.refs_2_.gp), channel_id=1, source_target_pairs={{0,4},{1,5},{2,6},{3,7},{4,0},{5,1},{6,2},{7,3},{8,12},{9,13},{10,... | collective-permute-start | bytes 4718600 | tf_op jit(solution)/shard_map/ppermute | solution.py:70
  77.6 13.4 %collective-permute-start.16 = (bf16[3,1152,128]{2,1,0:T(8,128)(2,1)}, bf16[3,1152,128]{2,1,0:T(8,128)(2,1)}, u32[]{:S(2)}, u32[]{:S(2)}) collective-permute-start(bf16[3,1152,128]{2,1,0:T(8,128)(2,1)} %collective-permute-done.12.refs_8_), channel_id=1, source_target_pairs={{0,16},{1,17},{2,18},{3,19},{4,12},{5,13},{6,14},{7,15},{8,24},{9,... | collective-permute-start | bytes 2654216 | tf_op jit(solution)/shard_map/ppermute | solution.py:76
  137.1 30.4 %collective-permute-start.18 = (bf16[2,4,1152,128]{3,2,1,0:T(8,128)(2,1)}, bf16[2,4,1152,128]{3,2,1,0:T(8,128)(2,1)}, u32[]{:S(2)}, u32[]{:S(2)}) collective-permute-start(bf16[2,4,1152,128]{3,2,1,0:T(8,128)(2,1)} %get-tuple-element.130), channel_id=1, source_target_pairs={{0,8},{1,9},{2,10},{3,11},{4,20},{5,21},{6,22},{7,23},{8,0},{9,1},... | collective-permute-start | bytes 7077896 | tf_op jit(solution)/shard_map/ppermute | solution.py:73
  167.5 7.0 %collective-permute-start.21 = (bf16[2,2,4,24,2304]{4,3,2,1,0:T(8,128)(2,1)}, bf16[2,2,4,24,2304]{4,3,2,1,0:T(8,128)(2,1)}, u32[]{:S(2)}, u32[]{:S(2)}) collective-permute-start(bf16[2,2,4,24,2304]{4,3,2,1,0:T(8,128)(2,1)} %get-tuple-element.147), channel_id=1, source_target_pairs={{0,4},{1,5},{2,6},{3,7},{4,0},{5,1},{6,2},{7,3},{8,12},{9,13},{10,... | collective-permute-start | bytes 5308424 | tf_op jit(solution)/shard_map/ppermute | solution.py:70
  167.7 11.9 %collective-permute-start.17 = (bf16[1024,768]{1,0:T(8,128)(2,1)}, bf16[1024,768]{1,0:T(8,128)(2,1)}, u32[]{:S(2)}, u32[]{:S(2)}) collective-permute-start(bf16[1024,768]{1,0:T(8,128)(2,1)} %get-tuple-element.125), channel_id=1, source_target_pairs={{0,4},{1,5},{2,6},{3,7},{4,0},{5,1},{6,2},{7,3},{8,12},{9,13},{10,... | collective-permute-start | bytes 4718600 | tf_op jit(solution)/shard_map/ppermute | solution.py:70
  173.0 25.7 %collective-permute-start.20 = (bf16[1,48,96,128]{3,2,1,0:T(8,128)(2,1)}, bf16[1,48,96,128]{3,2,1,0:T(8,128)(2,1)}, u32[]{:S(2)}, u32[]{:S(2)}) collective-permute-start(bf16[1,48,96,128]{3,2,1,0:T(8,128)(2,1)} %get-tuple-element.144), channel_id=1, source_target_pairs={{0,16},{1,17},{2,18},{3,19},{4,12},{5,13},{6,14},{7,15},{8,24},{9,... | collective-permute-start | bytes 3538952 | tf_op jit(solution)/shard_map/ppermute | solution.py:76
  178.2 20.5 %collective-permute-start.22 = (bf16[1,8,24,2304]{3,2,1,0:T(8,128)(2,1)}, bf16[1,8,24,2304]{3,2,1,0:T(8,128)(2,1)}, u32[]{:S(2)}, u32[]{:S(2)}) collective-permute-start(bf16[1,8,24,2304]{3,2,1,0:T(8,128)(2,1)} %get-tuple-element.149), channel_id=1, source_target_pairs={{0,8},{1,9},{2,10},{3,11},{4,20},{5,21},{6,22},{7,23},{8,0},{9,1},... | collective-permute-start | bytes 2654216 | tf_op jit(solution)/shard_map/ppermute | solution.py:73
  202.9 15.7 %collective-permute-start.24 = (bf16[2,12,96,128]{3,2,1,0:T(8,128)(2,1)}, bf16[2,12,96,128]{3,2,1,0:T(8,128)(2,1)}, u32[]{:S(2)}, u32[]{:S(2)}) collective-permute-start(bf16[2,12,96,128]{3,2,1,0:T(8,128)(2,1)} %get-tuple-element.162), channel_id=1, source_target_pairs={{0,1},{1,0},{2,3},{3,2},{4,5},{5,4},{6,7},{7,6},{8,9},{9,8},{10,11... | collective-permute-start | bytes 1769480 | tf_op jit(solution)/shard_map/ppermute | solution.py:85
  203.2 8.6 %collective-permute-start.23 = (bf16[1,4,24,2304]{3,2,1,0:T(8,128)(2,1)}, bf16[1,4,24,2304]{3,2,1,0:T(8,128)(2,1)}, u32[]{:S(2)}, u32[]{:S(2)}) collective-permute-start(bf16[1,4,24,2304]{3,2,1,0:T(8,128)(2,1)} %get-tuple-element.156), channel_id=1, source_target_pairs={{0,16},{1,17},{2,18},{3,19},{4,12},{5,13},{6,14},{7,15},{8,24},{9,... | collective-permute-start | bytes 1327112 | tf_op jit(solution)/shard_map/ppermute | solution.py:76
  224.0 8.6 %collective-permute-start.26 = (bf16[1,8,24,1024]{3,2,1,0:T(8,128)(2,1)}, bf16[1,8,24,1024]{3,2,1,0:T(8,128)(2,1)}, u32[]{:S(2)}, u32[]{:S(2)}) collective-permute-start(bf16[1,8,24,1024]{3,2,1,0:T(8,128)(2,1)} %get-tuple-element.170), channel_id=1, source_target_pairs={{0,8},{1,9},{2,10},{3,11},{4,20},{5,21},{6,22},{7,23},{8,0},{9,1},... | collective-permute-start | bytes 1179656 | tf_op jit(solution)/shard_map/ppermute | solution.py:73
  225.6 17.2 %collective-permute-start.30 = (bf16[1,12,96,128]{3,2,1,0:T(8,128)(2,1)}, bf16[1,12,96,128]{3,2,1,0:T(8,128)(2,1)}, u32[]{:S(2)}, u32[]{:S(2)}) collective-permute-start(bf16[1,12,96,128]{3,2,1,0:T(8,128)(2,1)} %get-tuple-element.168), channel_id=1, source_target_pairs={{0,2},{1,3},{2,0},{3,1},{4,6},{5,7},{6,4},{7,5},{8,10},{9,11},{10,... | collective-permute-start | bytes 884744 | tf_op jit(solution)/shard_map/ppermute | solution.py:85
  225.6 12.1 %collective-permute-start.28 = (bf16[2,1,24,2304]{3,2,0,1:T(8,128)(2,1)}, bf16[2,1,24,2304]{3,2,0,1:T(8,128)(2,1)}, u32[]{:S(2)}, u32[]{:S(2)}) collective-permute-start(bf16[2,1,24,2304]{3,2,0,1:T(8,128)(2,1)} %bitcast.59), channel_id=1, source_target_pairs={{0,1},{1,0},{2,3},{3,2},{4,5},{5,4},{6,7},{7,6},{8,9},{9,8},{10,11... | collective-permute-start | bytes 663560 | tf_op jit(solution)/shard_map/ppermute | solution.py:85
  244.6 16.3 %collective-permute-start.35 = (bf16[1152,128]{1,0:T(8,128)(2,1)}, bf16[1152,128]{1,0:T(8,128)(2,1)}, u32[]{:S(2)}, u32[]{:S(2)}) collective-permute-start(bf16[1152,128]{1,0:T(8,128)(2,1)} %bitcast.37.refs_0_), channel_id=1, source_target_pairs={{0,24},{1,25},{2,26},{3,27},{4,28},{5,29},{6,30},{7,31},{8,16},{9,... | collective-permute-start | bytes 884744 | tf_op jit(solution)/shard_map/ppermute | solution.py:88
  247.4 13.8 %collective-permute-start.34 = (bf16[1152,128]{1,0:T(8,128)(2,1)}, bf16[1152,128]{1,0:T(8,128)(2,1)}, u32[]{:S(2)}, u32[]{:S(2)}) collective-permute-start(bf16[1152,128]{1,0:T(8,128)(2,1)} %bitcast.37.refs_0_), channel_id=1, source_target_pairs={{0,16},{1,17},{2,18},{3,19},{4,12},{5,13},{6,14},{7,15},{8,24},{9,... | collective-permute-start | bytes 884744 | tf_op jit(solution)/shard_map/ppermute | solution.py:76
  247.9 13.3 %collective-permute-start.33 = (bf16[1152,128]{1,0:T(8,128)(2,1)}, bf16[1152,128]{1,0:T(8,128)(2,1)}, u32[]{:S(2)}, u32[]{:S(2)}) collective-permute-start(bf16[1152,128]{1,0:T(8,128)(2,1)} %bitcast.37.refs_0_), channel_id=1, source_target_pairs={{0,8},{1,9},{2,10},{3,11},{4,20},{5,21},{6,22},{7,23},{8,0},{9,1},... | collective-permute-start | bytes 884744 | tf_op jit(solution)/shard_map/ppermute | solution.py:73
  248.5 12.6 %collective-permute-start.31 = (bf16[1,1,24,2304]{3,2,1,0:T(8,128)(2,1)}, bf16[1,1,24,2304]{3,2,1,0:T(8,128)(2,1)}, u32[]{:S(2)}, u32[]{:S(2)}) collective-permute-start(bf16[1,1,24,2304]{3,2,1,0:T(8,128)(2,1)} %get-tuple-element.187), channel_id=1, source_target_pairs={{0,2},{1,3},{2,0},{3,1},{4,6},{5,7},{6,4},{7,5},{8,10},{9,11},{10,... | collective-permute-start | bytes 331784 | tf_op jit(solution)/shard_map/ppermute | solution.py:85
  263.9 8.2 %collective-permute-start.38 = (bf16[24,3328]{1,0:T(8,128)(2,1)}, bf16[24,3328]{1,0:T(8,128)(2,1)}, u32[]{:S(2)}, u32[]{:S(2)}) collective-permute-start(bf16[24,3328]{1,0:T(8,128)(2,1)} %add_convert_fusion.1.refs_0_), channel_id=1, source_target_pairs={{0,24},{1,25},{2,26},{3,27},{4,28},{5,29},{6,30},{7,31},{8,16},{9,... | collective-permute-start | bytes 479240 | tf_op jit(solution)/shard_map/ppermute | solution.py:88
  265.6 9.0 %collective-permute-start.37 = (bf16[24,3328]{1,0:T(8,128)(2,1)}, bf16[24,3328]{1,0:T(8,128)(2,1)}, u32[]{:S(2)}, u32[]{:S(2)}) collective-permute-start(bf16[24,3328]{1,0:T(8,128)(2,1)} %add_convert_fusion.1.refs_0_), channel_id=1, source_target_pairs={{0,16},{1,17},{2,18},{3,19},{4,12},{5,13},{6,14},{7,15},{8,24},{9,... | collective-permute-start | bytes 479240 | tf_op jit(solution)/shard_map/ppermute | solution.py:76
  266.5 8.1 %collective-permute-start.36 = (bf16[24,3328]{1,0:T(8,128)(2,1)}, bf16[24,3328]{1,0:T(8,128)(2,1)}, u32[]{:S(2)}, u32[]{:S(2)}) collective-permute-start(bf16[24,3328]{1,0:T(8,128)(2,1)} %add_convert_fusion.1.refs_0_), channel_id=1, source_target_pairs={{0,8},{1,9},{2,10},{3,11},{4,20},{5,21},{6,22},{7,23},{8,0},{9,1},... | collective-permute-start | bytes 479240 | tf_op jit(solution)/shard_map/ppermute | solution.py:73
  (20 other events, 118.8 us)
